TPU v7x, 32 devices: a whole 2x2x4 slice. The times are simulated.
32 devices in a mesh: dp: 2 (over x), seq: 16 (over z, y, core).
Axes of the slice: x: 2, y: 2, z: 4, core: 2. Of those that a mesh axis runs over, the one named last changes fastest.
Arguments:
- hidden_in: bfloat16 [2, 3072, 3584], P('dp', 'seq'), may hold values from -6 to 6
- spike_level: int32 [2, 3072], P('dp', 'seq'), may hold values from 1 to 4
- value_weight: bfloat16 [3584, 256], P('dp'), may hold values from -0.09375 to 0.09375
- queries: bfloat16 [2, 3072, 1792], P('dp', 'seq'), may hold values from -32 to 32
- key_states: bfloat16 [2, 3072, 256], P('dp', 'seq'), may hold values from -32 to 32
- spike_mask: int32 [2, 3072, 14], P('dp', 'seq'), may hold values 0 or 1
- out_grad: bfloat16 [2, 3072, 1792], P('dp', 'seq'), may hold values from -6 to 6
Outputs:
- query_grad: bfloat16 [2, 3072, 1792], P('dp', 'seq')
- key_grad: bfloat16 [2, 3072, 256], P('dp', 'seq')
- value_weight_grad: bfloat16 [3584, 256], P('dp')
All inputs are finite; a program needn't handle non-finite values. No bound on the sum of `spike_mask` on one device may be relied on, other than what follows from the above.
Results may differ from a plain program's by a relative error of at most 0.012.
The roundings to bfloat16 on the way count: a program that leaves them out, or rounds other values in their place, can miss the bound.
Values may be sent and summed in bfloat16 or wider, within the bound.
No kernel may reach another device: no remote copies, remote signals or barrier semaphores. Data moves between devices by JAX's collectives and lax.ppermute only.
A program may use at most 64 MiB of HBM per device.

v0:
```python
import math

import jax
import jax.numpy as jnp
from jax import lax
from jax.sharding import PartitionSpec as P

QH = 14
KVH = 2
HD = 128
WINDOW = 512
LEVELS = 4
GROUP = 7


masked_score = -1e30


def shifted(value, axis, steps):
    count = lax.axis_size(axis)
    first, last = (max(0, -steps), min(count, count - steps))
    return lax.ppermute(value, axis, [(source, source + steps) for source in range(first, last)])


def body(hidden_in, spike_level, value_weight, queries, key_states, spike_mask, out_grad):
    tok_rows = hidden_in.shape[1]
    reach_blocks = (WINDOW + tok_rows - 2) // tok_rows
    key_span = (reach_blocks + 1) * tok_rows
    score_scale = 1.0 / math.sqrt(HD)
    position = lax.axis_index("seq")
    spiked = (
        hidden_in[0].astype(jnp.float32) * (spike_level[0].astype(jnp.float32) / LEVELS)[:, None]
    ).astype(jnp.bfloat16)
    values = jnp.dot(
        spiked,
        lax.all_gather(value_weight, "dp", axis=0, tiled=True),
        preferred_element_type=jnp.float32,
    ).astype(jnp.bfloat16)
    own_keys = key_states[0]
    key_pieces = []
    value_pieces = []
    for offset in range(reach_blocks, 0, -1):
        got_keys, got_values = shifted((own_keys, values), "seq", offset)
        key_pieces.append(got_keys)
        value_pieces.append(got_values)
    key_block = jnp.concatenate(key_pieces + [own_keys], axis=0)
    value_block = jnp.concatenate(value_pieces + [values], axis=0)
    query_pos = position * tok_rows + jnp.arange(tok_rows, dtype=jnp.int32)
    key_pos = position * tok_rows - reach_blocks * tok_rows + jnp.arange(key_span, dtype=jnp.int32)
    allowed = (
        (key_pos[None, :] <= query_pos[:, None])
        & (key_pos[None, :] > query_pos[:, None] - WINDOW)
        & (key_pos[None, :] >= 0)
    )
    gated = (
        out_grad[0].reshape(tok_rows, QH, HD) * spike_mask[0][:, :, None].astype(jnp.bfloat16)
    ).reshape(tok_rows, KVH, GROUP, HD)
    query_heads = queries[0].reshape(tok_rows, KVH, GROUP, HD)
    query_parts = []
    key_parts = []
    value_parts = []
    for group in range(KVH):
        query_grp = query_heads[:, group]
        gated_grp = gated[:, group]
        key_grp = key_block[:, group * HD : (group + 1) * HD]
        value_grp = value_block[:, group * HD : (group + 1) * HD]
        scores = (
            jnp.einsum("thd,jd->htj", query_grp, key_grp, preferred_element_type=jnp.float32)
            * score_scale
        )
        scores = jnp.where(allowed[None], scores, masked_score)
        highest = jnp.max(scores, axis=-1, keepdims=True)
        expo = jnp.exp(scores - highest)
        probs = expo / jnp.sum(expo, axis=-1, keepdims=True)
        rounded_probs = probs.astype(jnp.bfloat16)
        attended = jnp.einsum(
            "htj,jd->thd", rounded_probs, value_grp, preferred_element_type=jnp.float32
        )
        delta = jnp.sum(gated_grp.astype(jnp.float32) * attended, axis=-1)
        prob_grad = jnp.einsum(
            "thd,jd->htj", gated_grp, value_grp, preferred_element_type=jnp.float32
        )
        score_grad = (probs * (prob_grad - jnp.transpose(delta)[:, :, None])).astype(jnp.bfloat16)
        query_part = (
            jnp.einsum("htj,jd->thd", score_grad, key_grp, preferred_element_type=jnp.float32)
            * score_scale
        )
        query_parts.append(query_part.astype(jnp.bfloat16))
        key_parts.append(
            jnp.einsum("htj,thd->jd", score_grad, query_grp, preferred_element_type=jnp.float32)
            * score_scale
        )
        value_parts.append(
            jnp.einsum("htj,thd->jd", rounded_probs, gated_grp, preferred_element_type=jnp.float32)
        )
    query_grad = jnp.stack(query_parts, axis=1).reshape(tok_rows, QH * HD)
    key_terms = jnp.concatenate(key_parts, axis=1)
    value_terms = jnp.concatenate(value_parts, axis=1)
    key_total = key_terms[reach_blocks * tok_rows :]
    value_total = value_terms[reach_blocks * tok_rows :]
    for offset in range(1, reach_blocks + 1):
        first_row = (reach_blocks - offset) * tok_rows
        back_keys, back_values = shifted(
            (
                key_terms[first_row : first_row + tok_rows],
                value_terms[first_row : first_row + tok_rows],
            ),
            "seq",
            -offset,
        )
        key_total = key_total + back_keys
        value_total = value_total + back_values
    value_grad = value_total.astype(jnp.bfloat16)
    whole_term = lax.dot_general(
        spiked, value_grad, (((0,), (0,)), ((), ())), preferred_element_type=jnp.float32
    )
    summed = lax.psum(whole_term, "seq")
    owned = lax.psum_scatter(summed, "dp", scatter_dimension=0, tiled=True)
    return (query_grad[None], key_total.astype(jnp.bfloat16)[None], owned.astype(jnp.bfloat16))


def solution(mesh):
    placed = (
        P("dp", "seq", None),
        P("dp", "seq"),
        P("dp", None),
        P("dp", "seq", None),
        P("dp", "seq", None),
        P("dp", "seq", None),
        P("dp", "seq", None),
    )
    return jax.shard_map(
        body,
        mesh=mesh,
        in_specs=placed,
        out_specs=(P("dp", "seq", None), P("dp", "seq", None), P("dp", None)),
        check_vma=False,
    )
```

profile of v0, /device:TPU:0, one launch (start us, length us, event | category | flops | bytes accessed | tf_op | source)
XLA Modules:
  0.0 193.0 jit_solution(12145091537902446400)
XLA Ops:
  7.2 2.5 %collective-permute-start.2 = (bf16[192,256]{1,0:T(8,128)(2,1)}, bf16[192,256]{1,0:T(8,128)(2,1)S(1)}, u32[]{:S(2)}, u32[]{:S(2)}) collective-permute-start(bf16[192,256]{1,0:T(8,128)(2,1)} %bitcast.156), channel_id=1, source_target_pairs={{0,1},{1,2},{2,3},{3,4},{4,5},{5,6},{6,7},{7,8},{8,9},{9,10},{10,1... | collective-permute-start | bytes 294920 | tf_op jit(solution)/shard_map/ppermute | solution.py:22
  9.7 4.4 %collective-permute-start.1 = (bf16[192,256]{1,0:T(8,128)(2,1)}, bf16[192,256]{1,0:T(8,128)(2,1)S(1)}, u32[]{:S(2)}, u32[]{:S(2)}) collective-permute-start(bf16[192,256]{1,0:T(8,128)(2,1)} %bitcast.157), channel_id=1, source_target_pairs={{0,2},{1,3},{2,4},{3,5},{4,6},{5,7},{6,8},{7,9},{8,10},{9,11},{10,... | collective-permute-start | bytes 294920 | tf_op jit(solution)/shard_map/ppermute | solution.py:22
  14.2 5.0 %collective-permute-start = (bf16[192,256]{1,0:T(8,128)(2,1)}, bf16[192,256]{1,0:T(8,128)(2,1)}, u32[]{:S(2)}, u32[]{:S(2)}) collective-permute-start(bf16[192,256]{1,0:T(8,128)(2,1)} %bitcast.158), channel_id=1, source_target_pairs={{0,3},{1,4},{2,5},{3,6},{4,7},{5,8},{6,9},{7,10},{8,11},{9,12},{10... | collective-permute-start | bytes 294920 | tf_op jit(solution)/shard_map/ppermute | solution.py:22
  20.1 1.9 reshape_squeeze.6
  24.8 1.1 pad_maximum_fusion.1
  26.0 3.5 %fusion.59 = (f32[7,192]{1,0:T(8,128)S(1)}, f32[7,192,768]{2,1,0:T(8,128)}) fusion(pred[192,768]{1,0:T(8,128)(4,1)S(1)} %and_and_fusion, bf16[192,1,7,128]{3,2,1,0:T(8,128)(2,1)S(1)} %get-tuple-element.15, bf16[768,256]{1,0:T(8,128)(2,1)S(1)} %pad_maximum_fusion.1), kind=kOutput, calls=%fused_computation.105 | convolution fusion | flops 268370688 | bytes 4871424 | tf_op jit(solution)/shard_map/sub | solution.py:73
  29.5 2.5 %fusion.15 = bf16[7,192,768]{2,1,0:T(8,128)(2,1)S(1)} fusion(f32[7,192,768]{2,1,0:T(8,128)} %get-tuple-element.20, f32[7,192]{1,0:T(8,128)S(1)} %get-tuple-element.19), kind=kLoop, calls=%fused_computation.24 | loop fusion | flops 2064384 | bytes 6198528 | tf_op jit(solution)/shard_map/convert_element_type | solution.py:75
  32.0 4.4 %fusion.58 = (f32[7,192]{1,0:T(8,128)S(1)}, f32[7,192,768]{2,1,0:T(8,128)}) fusion(pred[192,768]{1,0:T(8,128)(4,1)} %copy-done.9, bf16[192,1,7,128]{3,2,1,0:T(8,128)(2,1)S(1)} %get-tuple-element.16, bf16[768,256]{1,0:T(8,128)(2,1)S(1)} %pad_maximum_fusion.1), kind=kOutput, calls=%fused_computation.104 | convolution fusion | flops 268370688 | bytes 4871424 | tf_op jit(solution)/shard_map/sub | solution.py:73
  37.0 1.6 copy-done
  40.3 1.3 collective-permute-start.9
  41.6 1.3 collective-permute-start.11
  42.9 1.3 collective-permute-start.10
  44.3 8.4 %collective-permute-done.11 = f32[192,256]{0,1:T(8,128)S(1)} collective-permute-done((f32[192,256]{0,1:T(8,128)S(1)}, f32[192,256]{0,1:T(8,128)S(1)}, u32[]{:S(2)}, u32[]{:S(2)}) %collective-permute-start.11) | collective-permute-done | bytes 196640 | tf_op jit(solution)/shard_map/ppermute | solution.py:22
  52.7 2.0 %collective-permute-done.10 = f32[192,256]{0,1:T(8,128)S(1)} collective-permute-done((f32[192,256]{0,1:T(8,128)S(1)}, f32[192,256]{0,1:T(8,128)S(1)}, u32[]{:S(2)}, u32[]{:S(2)}) %collective-permute-start.10) | collective-permute-done | bytes 196640 | tf_op jit(solution)/shard_map/ppermute | solution.py:22
  54.7 2.7 %fusion.27 = f32[3584,256]{1,0:T(8,128)} fusion(bf16[1,192,3584]{2,1,0:T(8,128)(2,1)S(1)} %copy-done.5, f32[192]{0:T(256)S(1)} %bitcast.160, f32[192,256]{0,1:T(8,128)S(1)} %collective-permute-done.11, f32[192,256]{0,1:T(8,128)S(1)} %collective-permute-done.10, f32[192,256]{0,1:T(8,128)S(1)} %collective-permute-done.9, ...), kind=kOutput, calls=%fused_computation.60 | convolution fusion | flops 354631680 | bytes 6423296 | tf_op jit(solution)/shard_map/dot_general | solution.py:114
  57.4 2.6 %convolution_convert_fusion = bf16[192,256]{1,0:T(8,128)(2,1)S(1)} fusion(bf16[3584,256]{1,0:T(8,128)(2,1)} %all-gather.2.cloned.1.call-done, bf16[1,192,3584]{2,1,0:T(8,128)(2,1)} %param.7, f32[192]{0:T(256)} %bitcast.161), kind=kOutput, calls=%fused_computation.44 | convolution fusion | flops 354435072 | bytes 3310336 | tf_op jit(solution)/shard_map/dot_general | solution.py:34
  60.1 3.5 %collective-permute-start.5 = (bf16[192,256]{1,0:T(8,128)(2,1)S(1)}, bf16[192,256]{1,0:T(8,128)(2,1)S(1)}, u32[]{:S(2)}, u32[]{:S(2)}) collective-permute-start(bf16[192,256]{1,0:T(8,128)(2,1)S(1)} %convolution_convert_fusion), channel_id=1, source_target_pairs={{0,1},{1,2},{2,3},{3,4},{4,5},{5,6},{6,7},{7,8},{8,9},{9,10},{10,1... | collective-permute-start | bytes 294920 | tf_op jit(solution)/shard_map/ppermute | solution.py:22
  63.6 5.9 %collective-permute-start.4 = (bf16[192,256]{1,0:T(8,128)(2,1)S(1)}, bf16[192,256]{1,0:T(8,128)(2,1)S(1)}, u32[]{:S(2)}, u32[]{:S(2)}) collective-permute-start(bf16[192,256]{1,0:T(8,128)(2,1)S(1)} %convolution_convert_fusion), channel_id=1, source_target_pairs={{0,2},{1,3},{2,4},{3,5},{4,6},{5,7},{6,8},{7,9},{8,10},{9,11},{10,... | collective-permute-start | bytes 294920 | tf_op jit(solution)/shard_map/ppermute | solution.py:22
  69.6 4.7 %collective-permute-start.3 = (bf16[192,256]{1,0:T(8,128)(2,1)S(1)}, bf16[192,256]{1,0:T(8,128)(2,1)S(1)}, u32[]{:S(2)}, u32[]{:S(2)}) collective-permute-start(bf16[192,256]{1,0:T(8,128)(2,1)S(1)} %convolution_convert_fusion), channel_id=1, source_target_pairs={{0,3},{1,4},{2,5},{3,6},{4,7},{5,8},{6,9},{7,10},{8,11},{9,12},{10... | collective-permute-start | bytes 294920 | tf_op jit(solution)/shard_map/ppermute | solution.py:22
  74.3 2.0 %collective-permute-done.3 = bf16[192,256]{1,0:T(8,128)(2,1)S(1)} collective-permute-done((bf16[192,256]{1,0:T(8,128)(2,1)S(1)}, bf16[192,256]{1,0:T(8,128)(2,1)S(1)}, u32[]{:S(2)}, u32[]{:S(2)}) %collective-permute-start.3) | collective-permute-done | bytes 98336 | tf_op jit(solution)/shard_map/ppermute | solution.py:22
  77.1 0.8 fusion.24
  78.4 1.0 fusion.5
  80.1 1.7 copy-done.1
  81.8 1.0 fusion.3
  83.5 1.3 collective-permute-start.6
  84.8 1.3 collective-permute-start.8
  86.1 1.3 collective-permute-start.7
  89.3 1.6 broadcast_in_dim_reshape.3
  90.9 4.6 %collective-permute-done.8 = f32[192,256]{0,1:T(8,128)S(1)} collective-permute-done((f32[192,256]{0,1:T(8,128)S(1)}, f32[192,256]{0,1:T(8,128)S(1)}, u32[]{:S(2)}, u32[]{:S(2)}) %collective-permute-start.8) | collective-permute-done | bytes 196640 | tf_op jit(solution)/shard_map/ppermute | solution.py:22
  95.6 1.6 collective-permute-done.7
  98.0 12.7 %reduce-scatter.2.cloned.1.call-done = f32[1792,256]{1,0:T(8,128)} async-done(((f32[3584,256]{1,0:T(8,128)}), f32[1792,256]{1,0:T(8,128)}) %reduce-scatter.2.cloned.1.call-update) | async-done | bytes 1835024 | tf_op jit(solution)/shard_map/reduce_scatter | solution.py:118
  110.8 75.4 %all-reduce.1 = bf16[1792,256]{1,0:T(8,128)(2,1)} all-reduce(f32[1792,256]{1,0:T(8,128)} %reduce-scatter.2.cloned.1.call-done), channel_id=1, replica_groups=mesh['dp'=2,'seq'=16] {'seq'}, use_global_device_ids=true, to_apply=%region_6.7 | all-reduce | flops 458752 | bytes 2752512 | tf_op jit(solution)/shard_map/psum | solution.py:117
  (63 shorter events, 11.3 us)
Async XLA Ops:
  7.2 14.9 %copy-start.6 = (bf16[1,192,1792]{2,1,0:T(8,128)(2,1)S(1)}, bf16[1,192,1792]{2,1,0:T(8,128)(2,1)}, u32[]{:S(2)}) copy-start(bf16[1,192,1792]{2,1,0:T(8,128)(2,1)} %param.13) | copy-start | bytes 2064388
  7.2 50.3 %all-gather.2.cloned.1.call-start = ((), (), s32[]{:S(2)}) async-start(), calls=%async_computation.1 | async-start | bytes 2752512 | tf_op jit(solution)/shard_map/all_gather | solution.py:36
  7.2 16.3 %collective-permute-start.2 = (bf16[192,256]{1,0:T(8,128)(2,1)}, bf16[192,256]{1,0:T(8,128)(2,1)S(1)}, u32[]{:S(2)}, u32[]{:S(2)}) collective-permute-start(bf16[192,256]{1,0:T(8,128)(2,1)} %bitcast.156), channel_id=1, source_target_pairs={{0,1},{1,2},{2,3},{3,4},{4,5},{5,6},{6,7},{7,8},{8,9},{9,10},{10,1... | collective-permute-start | bytes 294920 | tf_op jit(solution)/shard_map/ppermute | solution.py:22
  9.7 13.8 %collective-permute-start.1 = (bf16[192,256]{1,0:T(8,128)(2,1)}, bf16[192,256]{1,0:T(8,128)(2,1)S(1)}, u32[]{:S(2)}, u32[]{:S(2)}) collective-permute-start(bf16[192,256]{1,0:T(8,128)(2,1)} %bitcast.157), channel_id=1, source_target_pairs={{0,2},{1,3},{2,4},{3,5},{4,6},{5,7},{6,8},{7,9},{8,10},{9,11},{10,... | collective-permute-start | bytes 294920 | tf_op jit(solution)/shard_map/ppermute | solution.py:22
  14.2 10.7 %collective-permute-start = (bf16[192,256]{1,0:T(8,128)(2,1)}, bf16[192,256]{1,0:T(8,128)(2,1)}, u32[]{:S(2)}, u32[]{:S(2)}) collective-permute-start(bf16[192,256]{1,0:T(8,128)(2,1)} %bitcast.158), channel_id=1, source_target_pairs={{0,3},{1,4},{2,5},{3,6},{4,7},{5,8},{6,9},{7,10},{8,11},{9,12},{10... | collective-permute-start | bytes 294920 | tf_op jit(solution)/shard_map/ppermute | solution.py:22
  19.2 91.6 %reduce-scatter.2.cloned.1.call-start = ((), (), s32[]{:S(2)}) async-start(), calls=%async_computation.2 | async-start | bytes 5505024 | tf_op jit(solution)/shard_map/reduce_scatter | solution.py:118
  22.1 7.5 %copy-start.7 = (bf16[192,1,7,128]{3,2,1,0:T(8,128)(2,1)}, bf16[192,1,7,128]{3,2,1,0:T(8,128)(2,1)S(1)}, u32[]{:S(2)}) copy-start(bf16[192,1,7,128]{3,2,1,0:T(8,128)(2,1)S(1)} %get-tuple-element.15) | copy-start | bytes 1032196
  23.5 6.0 %copy-start.9 = (pred[192,768]{1,0:T(8,128)(4,1)}, pred[192,768]{1,0:T(8,128)(4,1)S(1)}, u32[]{:S(2)}) copy-start(pred[192,768]{1,0:T(8,128)(4,1)S(1)} %and_and_fusion) | copy-start | bytes 442372
  23.5 0.7 copy-start.10
  24.2 0.6 copy-start.11
  36.4 2.2 %copy-start = (f32[7,192,768]{2,1,0:T(8,128)S(1)}, f32[7,192,768]{2,1,0:T(8,128)}, u32[]{:S(2)}) copy-start(f32[7,192,768]{2,1,0:T(8,128)} %get-tuple-element.18) | copy-start | bytes 12386308
  38.9 1.4 copy-start.3
  39.0 5.3 %copy-start.13 = (s32[1,192]{1,0:T(1,128)S(1)}, s32[1,192]{1,0:T(1,128)}, u32[]{:S(2)}) copy-start(s32[1,192]{1,0:T(1,128)} %param.8) | copy-start | bytes 2308
  39.0 15.8 %copy-start.5 = (bf16[1,192,3584]{2,1,0:T(8,128)(2,1)S(1)}, bf16[1,192,3584]{2,1,0:T(8,128)(2,1)}, u32[]{:S(2)}) copy-start(bf16[1,192,3584]{2,1,0:T(8,128)(2,1)} %param.7) | copy-start | bytes 4128772
  40.3 3.9 %collective-permute-start.9 = (f32[192,256]{0,1:T(8,128)S(1)}, f32[192,256]{0,1:T(8,128)S(1)}, u32[]{:S(2)}, u32[]{:S(2)}) collective-permute-start(f32[192,256]{0,1:T(8,128)S(1)} %get-tuple-element.9), channel_id=1, source_target_pairs={{1,0},{2,1},{3,2},{4,3},{5,4},{6,5},{7,6},{8,7},{9,8},{10,9},{11,1... | collective-permute-start | bytes 589832 | tf_op jit(solution)/shard_map/ppermute | solution.py:22
  41.6 11.1 %collective-permute-start.11 = (f32[192,256]{0,1:T(8,128)S(1)}, f32[192,256]{0,1:T(8,128)S(1)}, u32[]{:S(2)}, u32[]{:S(2)}) collective-permute-start(f32[192,256]{0,1:T(8,128)S(1)} %get-tuple-element.10), channel_id=1, source_target_pairs={{3,0},{4,1},{5,2},{6,3},{7,4},{8,5},{9,6},{10,7},{11,8},{12,9},{13... | collective-permute-start | bytes 589832 | tf_op jit(solution)/shard_map/ppermute | solution.py:22
  42.9 11.8 %collective-permute-start.10 = (f32[192,256]{0,1:T(8,128)S(1)}, f32[192,256]{0,1:T(8,128)S(1)}, u32[]{:S(2)}, u32[]{:S(2)}) collective-permute-start(f32[192,256]{0,1:T(8,128)S(1)} %get-tuple-element.11), channel_id=1, source_target_pairs={{2,0},{3,1},{4,2},{5,3},{6,4},{7,5},{8,6},{9,7},{10,8},{11,9},{12,... | collective-permute-start | bytes 589832 | tf_op jit(solution)/shard_map/ppermute | solution.py:22
  44.2 10.5 %copy-start.12 = (f32[1,192]{1,0:T(1,128)}, f32[1,192]{1,0:T(1,128)S(1)}, u32[]{:S(2)}) copy-start(f32[1,192]{1,0:T(1,128)S(1)} %convert_multiply_fusion.1) | copy-start | bytes 2308
  57.4 19.7 %copy-start.4 = (bf16[7,192,768]{2,1,0:T(8,128)(2,1)S(1)}, bf16[7,192,768]{2,1,0:T(8,128)(2,1)}, u32[]{:S(2)}) copy-start(bf16[7,192,768]{2,1,0:T(8,128)(2,1)} %copy-done.3) | copy-start | bytes 6193156
  60.1 14.1 %collective-permute-start.5 = (bf16[192,256]{1,0:T(8,128)(2,1)S(1)}, bf16[192,256]{1,0:T(8,128)(2,1)S(1)}, u32[]{:S(2)}, u32[]{:S(2)}) collective-permute-start(bf16[192,256]{1,0:T(8,128)(2,1)S(1)} %convolution_convert_fusion), channel_id=1, source_target_pairs={{0,1},{1,2},{2,3},{3,4},{4,5},{5,6},{6,7},{7,8},{8,9},{9,10},{10,1... | collective-permute-start | bytes 294920 | tf_op jit(solution)/shard_map/ppermute | solution.py:22
  63.6 10.6 %collective-permute-start.4 = (bf16[192,256]{1,0:T(8,128)(2,1)S(1)}, bf16[192,256]{1,0:T(8,128)(2,1)S(1)}, u32[]{:S(2)}, u32[]{:S(2)}) collective-permute-start(bf16[192,256]{1,0:T(8,128)(2,1)S(1)} %convolution_convert_fusion), channel_id=1, source_target_pairs={{0,2},{1,3},{2,4},{3,5},{4,6},{5,7},{6,8},{7,9},{8,10},{9,11},{10,... | collective-permute-start | bytes 294920 | tf_op jit(solution)/shard_map/ppermute | solution.py:22
  69.6 6.7 %collective-permute-start.3 = (bf16[192,256]{1,0:T(8,128)(2,1)S(1)}, bf16[192,256]{1,0:T(8,128)(2,1)S(1)}, u32[]{:S(2)}, u32[]{:S(2)}) collective-permute-start(bf16[192,256]{1,0:T(8,128)(2,1)S(1)} %convolution_convert_fusion), channel_id=1, source_target_pairs={{0,3},{1,4},{2,5},{3,6},{4,7},{5,8},{6,9},{7,10},{8,11},{9,12},{10... | collective-permute-start | bytes 294920 | tf_op jit(solution)/shard_map/ppermute | solution.py:22
  76.3 2.2 %copy-start.2 = (f32[7,192,768]{2,1,0:T(8,128)S(1)}, f32[7,192,768]{2,1,0:T(8,128)}, u32[]{:S(2)}) copy-start(f32[7,192,768]{2,1,0:T(8,128)} %get-tuple-element.20) | copy-start | bytes 12386308
  78.4 1.1 copy-start.8
  79.5 2.3 %copy-start.1 = (f32[7,192,768]{2,1,0:T(8,128)S(1)}, f32[7,192,768]{2,1,0:T(8,128)}, u32[]{:S(2)}) copy-start(f32[7,192,768]{2,1,0:T(8,128)} %get-tuple-element.18) | copy-start | bytes 12386308
  83.5 7.4 %collective-permute-start.6 = (f32[192,256]{0,1:T(8,128)S(1)}, f32[192,256]{0,1:T(8,128)S(1)}, u32[]{:S(2)}, u32[]{:S(2)}) collective-permute-start(f32[192,256]{0,1:T(8,128)S(1)} %get-tuple-element.12), channel_id=1, source_target_pairs={{1,0},{2,1},{3,2},{4,3},{5,4},{6,5},{7,6},{8,7},{9,8},{10,9},{11,1... | collective-permute-start | bytes 589832 | tf_op jit(solution)/shard_map/ppermute | solution.py:22
  84.8 10.8 %collective-permute-start.8 = (f32[192,256]{0,1:T(8,128)S(1)}, f32[192,256]{0,1:T(8,128)S(1)}, u32[]{:S(2)}, u32[]{:S(2)}) collective-permute-start(f32[192,256]{0,1:T(8,128)S(1)} %get-tuple-element.13), channel_id=1, source_target_pairs={{3,0},{4,1},{5,2},{6,3},{7,4},{8,5},{9,6},{10,7},{11,8},{12,9},{13... | collective-permute-start | bytes 589832 | tf_op jit(solution)/shard_map/ppermute | solution.py:22
  86.1 11.0 %collective-permute-start.7 = (f32[192,256]{0,1:T(8,128)S(1)}, f32[192,256]{0,1:T(8,128)S(1)}, u32[]{:S(2)}, u32[]{:S(2)}) collective-permute-start(f32[192,256]{0,1:T(8,128)S(1)} %get-tuple-element.14), channel_id=1, source_target_pairs={{2,0},{3,1},{4,2},{5,3},{6,4},{7,5},{8,6},{9,7},{10,8},{11,9},{12,... | collective-permute-start | bytes 589832 | tf_op jit(solution)/shard_map/ppermute | solution.py:22
Sparse Core Ops, SparseCore 0:
  19.3 28.8 all-gather.1
  57.5 53.1 reduce-scatter.1
where the time goes:
time: 194 us; the launch traced here: 193 us
  blocking collectives  75.4 us (39%)
  starting transfers between devices  33.9 us (17%)
  waiting for transfers between devices  31.4 us (16%)
  matrix products  20.5 us (11%)
  between operations  14.5 us (7%)
  local copies, waits for them, and re-layouts  11.5 us (6%)
  other arithmetic  5.85 us (3%)
    psum x1, blocking collectives, body(): summed = lax.psum(whole_term, 'seq')  75.4 us
    ppermute x12, starting transfers between devices, shifted(): lax.ppermute(value, axis, [(source, source + steps) for source in range(f...  33.8 us
    ppermute x12, waiting for transfers between devices, shifted(): lax.ppermute(value, axis, [(source, source + steps) for source in range(f...  18.7 us
    reduce_scatter x1, waiting for transfers between devices, body(): owned = lax.psum_scatter(summed, 'dp', scatter_dimension=0, tiled=True)  12.7 us
    sub x2, matrix products, body(): expo = jnp.exp(scores - highest)  7.97 us
    unnamed x29, local copies, waits for them, and re-layouts  6.66 us
  transfers between devices with their start and end apart: 14, of which 6 were waited for; matrix products, arithmetic and copies ran while one was open for 17% of the time, Pallas kernels for 0%

commit v1 on v0

v1 whole, which is shorter than its diff:
```python
import math

import jax
import jax.numpy as jnp
from jax import lax
from jax.sharding import PartitionSpec as P

QH = 14
KVH = 2
HD = 128
WINDOW = 512
LEVELS = 4
GROUP = 7


masked_score = -1e30


def shifted(value, steps):
    count = lax.axis_size("seq")
    first, last = (max(0, -steps), min(count, count - steps))
    return lax.ppermute(value, "seq", [(source, source + steps) for source in range(first, last)])


def swapped(value, axis, flip):
    return lax.ppermute(value, axis, [(i, i ^ flip) for i in range(lax.axis_size(axis))])


def ordered(bit, own, other, axis=0):
    return jnp.where(
        bit == 0,
        jnp.concatenate([own, other], axis=axis),
        jnp.concatenate([other, own], axis=axis),
    )


def body(hidden_in, spike_level, value_weight, queries, key_states, spike_mask, out_grad):
    tok_rows = hidden_in.shape[1]
    chip_rows = 2 * tok_rows
    span = WINDOW + chip_rows
    n_dp, n_seq = lax.axis_size("dp"), lax.axis_size("seq")
    score_scale = 1.0 / math.sqrt(HD)
    place = lax.axis_index("seq")
    core, chip = place % 2, place // 2
    row = lax.axis_index("dp")
    reach = []
    left = WINDOW
    while left > 0:
        reach.append((min(left, chip_rows), len(reach) + 1))
        left -= chip_rows

    def head_half(value):
        half = value.shape[1] // 2
        mine = lax.dynamic_slice_in_dim(value, core * half, half, 1)
        theirs = lax.dynamic_slice_in_dim(value, (1 - core) * half, half, 1)
        return ordered(core, mine, swapped(theirs, "seq", 1))

    def with_past(value):
        pieces = [shifted(value[chip_rows - rows :], 2 * offset) for rows, offset in reach]
        return jnp.concatenate(pieces[::-1] + [value], axis=0)

    def with_future(terms):
        total = terms[WINDOW:]
        begin = WINDOW
        for rows, offset in reach:
            begin -= rows
            got = shifted(terms[begin : begin + rows].astype(jnp.bfloat16), -2 * offset)
            total = total + jnp.pad(got.astype(jnp.float32), ((chip_rows - rows, 0), (0, 0)))
        return total

    key_span = with_past(head_half(key_states[0]))
    weight_half = lax.dynamic_slice_in_dim(value_weight, core * HD, HD, 1)
    if n_dp == 2:
        weight = ordered(row, weight_half, swapped(weight_half, "dp", 1))
    else:
        weight = lax.all_gather(weight_half, "dp", axis=0, tiled=True)
    gated = (
        out_grad[0].reshape(tok_rows, QH, HD) * spike_mask[0][:, :, None].astype(jnp.bfloat16)
    ).reshape(tok_rows, QH * HD)
    gated = head_half(gated).reshape(chip_rows, GROUP, HD)
    query = head_half(queries[0]).reshape(chip_rows, GROUP, HD)
    own_spiked = (
        hidden_in[0].astype(jnp.float32) * (spike_level[0].astype(jnp.float32) / LEVELS)[:, None]
    ).astype(jnp.bfloat16)
    spiked = ordered(core, own_spiked, swapped(own_spiked, "seq", 1))

    query_pos = jnp.arange(chip_rows, dtype=jnp.int32)
    key_pos = jnp.arange(span, dtype=jnp.int32) - WINDOW
    allowed = (
        (key_pos[:, None] <= query_pos[None, :])
        & (key_pos[:, None] > query_pos[None, :] - WINDOW)
        & (key_pos[:, None] >= -chip * chip_rows)
    )
    scores = (
        jnp.einsum("jd,thd->hjt", key_span, query, preferred_element_type=jnp.float32)
        * score_scale
    )
    scores = jnp.where(allowed[None], scores, masked_score)
    expo = jnp.exp(scores - jnp.max(scores, axis=1, keepdims=True))
    probs = expo / jnp.sum(expo, axis=1, keepdims=True)
    rounded_probs = probs.astype(jnp.bfloat16)
    value_terms = jnp.einsum(
        "hjt,thd->jd", rounded_probs, gated, preferred_element_type=jnp.float32
    )
    value_grad = with_future(value_terms).astype(jnp.bfloat16)

    part = lax.dot_general(
        spiked, value_grad, (((0,), (0,)), ((), ())), preferred_element_type=jnp.float32
    )
    steps = [("dp", 1 << b, (row >> b) & 1) for b in range(n_dp.bit_length() - 2, -1, -1)]
    chip_steps = [
        ("seq", 2 << b, (chip >> b) & 1) for b in range((n_seq // 2).bit_length() - 1)
    ]
    for axis, flip, bit in steps + chip_steps:
        half = part.shape[0] // 2
        send = lax.dynamic_slice_in_dim(part, (1 - bit) * half, half, 0).astype(jnp.bfloat16)
        keep = lax.dynamic_slice_in_dim(part, bit * half, half, 0)
        part = keep + swapped(send, axis, flip).astype(jnp.float32)
    owned = part.astype(jnp.bfloat16)
    for axis, flip, bit in chip_steps[::-1]:
        owned = ordered(bit, owned, swapped(owned, axis, flip))
    weight_grad = ordered(core, owned, swapped(owned, "seq", 1), axis=1)

    values = jnp.dot(spiked, weight, preferred_element_type=jnp.float32).astype(jnp.bfloat16)
    value_span = with_past(values)
    prob_grad = jnp.einsum("jd,thd->hjt", value_span, gated, preferred_element_type=jnp.float32)
    delta = jnp.sum(rounded_probs.astype(jnp.float32) * prob_grad, axis=1, keepdims=True)
    score_grad = (probs * (prob_grad - delta)).astype(jnp.bfloat16)
    query_part = (
        jnp.einsum("hjt,jd->thd", score_grad, key_span, preferred_element_type=jnp.float32)
        * score_scale
    ).astype(jnp.bfloat16)
    key_terms = (
        jnp.einsum("hjt,thd->jd", score_grad, query, preferred_element_type=jnp.float32)
        * score_scale
    )
    key_grad = with_future(key_terms).astype(jnp.bfloat16)

    def token_half(value):
        mine = lax.dynamic_slice_in_dim(value, core * tok_rows, tok_rows, 0)
        theirs = lax.dynamic_slice_in_dim(value, (1 - core) * tok_rows, tok_rows, 0)
        return ordered(core, mine, swapped(theirs, "seq", 1), axis=1)

    query_grad = token_half(query_part.reshape(chip_rows, GROUP * HD))
    return (query_grad[None], token_half(key_grad)[None], weight_grad)


def solution(mesh):
    placed = (
        P("dp", "seq", None),
        P("dp", "seq"),
        P("dp", None),
        P("dp", "seq", None),
        P("dp", "seq", None),
        P("dp", "seq", None),
        P("dp", "seq", None),
    )
    return jax.shard_map(
        body,
        mesh=mesh,
        in_specs=placed,
        out_specs=(P("dp", "seq", None), P("dp", "seq", None), P("dp", None)),
        check_vma=False,
    )
```

time: 194 us -> 124 us (0.64)
  blocking collectives: 75.4 us -> 0 us
  between operations: 14.5 us -> 1.05 us
  other arithmetic: 5.85 us -> 18.8 us
  matrix products: 20.5 us -> 27.4 us
  starting transfers between devices: 33.9 us -> 37.5 us
  waiting for transfers between devices: 31.4 us -> 28.1 us
    psum x1 -> x0, blocking collectives: 75.4 us -> none  [body(): summed = lax.psum(whole_term, 'seq')]
    reduce_scatter x1 -> x0, waiting for transfers between devices: 12.7 us -> none  [body(): owned = lax.psum_scatter(summed, 'dp', scatter_dimension=0, tiled=True)]
    ppermute x12 -> x23, waiting for transfers between devices: 18.7 us -> 28.1 us  [the longest x15 20.9 us: swapped(): lax.ppermute(value, axis, [(i, i ^ flip) for i in range(lax.axis_size(axi...]
    convert_element_type x2 -> x4, other arithmetic: 2.81 us -> 9.7 us  [the longest x1 7.33 us: body(): score_grad = (probs * (prob_grad - delta)).astype(jnp.bfloat16)]
    dot_general x11 -> x5, matrix products: 9.86 us -> 15.4 us  [the longest x1 5.23 us: body(): jnp.einsum('jd,thd->hjt', value_span, gated, preferred_element_type=jnp.f...]
    unnamed x29 -> x11, local copies, waits for them, and re-layouts: 6.66 us -> 1.47 us
    another operation x4 -> x0, local copies, waits for them, and re-layouts: 4.73 us -> none  [the longest x1 1.9 us: body(): query_heads = queries[0].reshape(tok_rows, KVH, GROUP, HD)]
    select_n x0 -> x9, other arithmetic: none -> 4.7 us  [ordered(): jnp.where(bit == 0, jnp.concatenate([own, other], axis=axis), jnp.concate...]
  transfers between devices with their start and end apart: 14 -> 23, of which waited for: 6 -> 8; matrix products, arithmetic and copies ran while one was open for 17% -> 30% of each run, Pallas kernels for 0% -> 0%
where the time goes in v1:
time: 124 us
  starting transfers between devices  37.5 us (30%)
  waiting for transfers between devices  28.1 us (23%)
  matrix products  27.4 us (22%)
  other arithmetic  18.8 us (15%)
  local copies, waits for them, and re-layouts  10.7 us (9%)
    ppermute x15, waiting for transfers between devices, swapped(): lax.ppermute(value, axis, [(i, i ^ flip) for i in range(lax.axis_size(axi...  20.9 us
    ppermute x8, starting transfers between devices, shifted(): lax.ppermute(value, 'seq', [(source, source + steps) for source in range(...  19.3 us
    ppermute x15, starting transfers between devices, swapped(): lax.ppermute(value, axis, [(i, i ^ flip) for i in range(lax.axis_size(axi...  18.2 us
    sub x1, matrix products, body(): expo = jnp.exp(scores - jnp.max(scores, axis=1, keepdims=True))  8.51 us
    convert_element_type x1, other arithmetic, body(): score_grad = (probs * (prob_grad - delta)).astype(jnp.bfloat16)  7.33 us
    ppermute x8, waiting for transfers between devices, shifted(): lax.ppermute(value, 'seq', [(source, source + steps) for source in range(...  7.16 us
    dot_general x1, matrix products, body(): jnp.einsum('jd,thd->hjt', value_span, gated, preferred_element_type=jnp.f...  5.23 us
    select_n x9, other arithmetic, ordered(): jnp.where(bit == 0, jnp.concatenate([own, other], axis=axis), jnp.concate...  4.7 us
  transfers between devices with their start and end apart: 23, of which 8 were waited for; matrix products, arithmetic and copies ran while one was open for 30% of the time, Pallas kernels for 0%

profile of v1, /device:TPU:0, one launch (start us, length us, event | category | flops | bytes accessed | tf_op | source)
XLA Modules:
  0.0 123.6 jit_solution(5597669857033384085)
XLA Ops:
  0.7 2.0 %constant_dynamic-slice_fusion.6 = (bf16[1,192,896]{2,1,0:T(8,128)(2,1)S(1)}, bf16[192,896]{1,0:T(8,128)(2,1)}) fusion(bf16[1,192,1792]{2,1,0:T(8,128)(2,1)} %param.10, s32[]{:T(128)S(6)} %select_n.170, s32[]{:T(128)S(6)} %select_n.171), kind=kLoop, calls=%fused_computation.83 | loop fusion | bytes 1376264 | tf_op jit(solution)/shard_map/dynamic_slice | solution.py:54
  5.5 1.3 %bitcast_multiply_fusion.1 = bf16[192,1792]{1,0:T(8,128)(2,1)S(1)} fusion(bf16[24,8,14,128]{3,2,1,0:T(8,128)(2,1)S(1)} %bitcast.71, bf16[1,192,1792]{2,1,0:T(8,128)(2,1)} %param.13), kind=kLoop, calls=%fused_computation.39 | loop fusion | flops 344064 | bytes 2064384 | tf_op jit(solution)/shard_map/mul | solution.py:78
  8.0 1.4 %fusion.9 = bf16[192,3584]{1,0:T(8,128)(2,1)} fusion(bf16[1,192,3584]{2,1,0:T(8,128)(2,1)S(1)} %copy-done.2, f32[192]{0:T(256)S(1)} %bitcast.76), kind=kLoop, calls=%fused_computation.16 | loop fusion | flops 2064384 | bytes 2753280 | tf_op jit(solution)/shard_map/convert_element_type | solution.py:84
  9.5 3.0 %collective-permute-start.6 = (bf16[1792,128]{1,0:T(8,128)(2,1)S(1)}, bf16[1792,128]{1,0:T(8,128)(2,1)}, u32[]{:S(2)}, u32[]{:S(2)}) collective-permute-start(bf16[1792,128]{1,0:T(8,128)(2,1)S(1)} %constant_dynamic-slice_fusion.3), channel_id=1, source_target_pairs={{0,16},{16,0},{1,17},{17,1},{2,18},{18,2},{3,19},{19,3},{4,20},{20... | collective-permute-start | bytes 1376264 | tf_op jit(solution)/shard_map/ppermute | solution.py:26
  15.4 3.4 %collective-permute-start.2 = (bf16[384,128]{1,0:T(8,128)(2,1)S(1)}, bf16[384,128]{1,0:T(8,128)(2,1)S(1)}, u32[]{:S(2)}, u32[]{:S(2)}) collective-permute-start(bf16[384,128]{1,0:T(8,128)(2,1)S(1)} %maximum_select_fusion.12), channel_id=1, source_target_pairs={{0,2},{1,3},{2,4},{3,5},{4,6},{5,7},{6,8},{7,9},{8,10},{9,11},{10,... | collective-permute-start | bytes 294920 | tf_op jit(solution)/shard_map/ppermute | solution.py:22
  19.4 4.1 %collective-permute-start.1 = (bf16[128,128]{1,0:T(8,128)(2,1)}, bf16[128,128]{1,0:T(8,128)(2,1)}, u32[]{:S(2)}, u32[]{:S(2)}) collective-permute-start(bf16[128,128]{1,0:T(8,128)(2,1)} %slice.36), channel_id=1, source_target_pairs={{0,4},{1,5},{2,6},{3,7},{4,8},{5,9},{6,10},{7,11},{8,12},{9,13},{1... | collective-permute-start | bytes 98312 | tf_op jit(solution)/shard_map/ppermute | solution.py:22
  23.5 1.4 %concatenate.124 = bf16[192,7,128]{2,1,0:T(8,128)(2,1)S(1)} reshape(bf16[192,896]{1,0:T(8,128)(2,1)} %collective-permute-done.3) | data formatting | bytes 688128 | tf_op jit(solution)/shard_map/concatenate | solution.py:32
  25.3 1.4 %concatenate.128 = bf16[192,7,128]{2,1,0:T(8,128)(2,1)S(1)} reshape(bf16[192,896]{1,0:T(8,128)(2,1)} %collective-permute-done.4) | data formatting | bytes 688128 | tf_op jit(solution)/shard_map/concatenate | solution.py:32
  26.7 8.5 %fusion.56 = (f32[7,384]{1,0:T(8,128)S(1)}, f32[7,896,384]{1,2,0:T(8,128)}) fusion(pred[896,384]{0,1:T(8,128)(4,1)} %fusion.11, bf16[384,7,128]{2,1,0:T(8,128)(2,1)S(1)} %maximum_select_fusion.4, bf16[384,128]{1,0:T(8,128)(2,1)S(1)} %maximum_select_fusion.12, bf16[384,128]{1,0:T(8,128)(2,1)S(1)} %collective-permute-done.2, ...), kind=kOutput, calls=%fused_computation.97 | convolution fusion | flops 626885504 | bytes 10906112 | tf_op jit(solution)/shard_map/sub | solution.py:99
  35.2 4.2 %convolution_convert_fusion = bf16[384,128]{1,0:T(8,128)(2,1)S(1)} fusion(bf16[1792,128]{1,0:T(8,128)(2,1)} %collective-permute-done.6, bf16[1792,128]{1,0:T(8,128)(2,1)S(1)} %constant_dynamic-slice_fusion.3, pred[]{:T(512)S(6)} %eq.24, bf16[192,3584]{1,0:T(8,128)(2,1)} %collective-permute-done.5, bf16[192,3584]{1,0:T(8,128)(2,1)} %fusion.9, pred[]{:T(512)S(6)} %eq.12), kind=kOutput, calls=%fused_computation.25 | convolution fusion | flops 368885760 | bytes 3768322 | tf_op jit(solution)/shard_map/dot_general | solution.py:124
  39.4 3.6 %collective-permute-start.8 = (bf16[384,128]{1,0:T(8,128)(2,1)S(1)}, bf16[384,128]{1,0:T(8,128)(2,1)S(1)}, u32[]{:S(2)}, u32[]{:S(2)}) collective-permute-start(bf16[384,128]{1,0:T(8,128)(2,1)S(1)} %convolution_convert_fusion), channel_id=1, source_target_pairs={{0,2},{1,3},{2,4},{3,5},{4,6},{5,7},{6,8},{7,9},{8,10},{9,11},{10,... | collective-permute-start | bytes 294920 | tf_op jit(solution)/shard_map/ppermute | solution.py:22
  43.0 3.1 %collective-permute-start.7 = (bf16[128,128]{1,0:T(8,128)(2,1)S(1)}, bf16[128,128]{1,0:T(8,128)(2,1)S(1)}, u32[]{:S(2)}, u32[]{:S(2)}) collective-permute-start(bf16[128,128]{1,0:T(8,128)(2,1)S(1)} %slice.37), channel_id=1, source_target_pairs={{0,4},{1,5},{2,6},{3,7},{4,8},{5,9},{6,10},{7,11},{8,12},{9,13},{1... | collective-permute-start | bytes 98312 | tf_op jit(solution)/shard_map/ppermute | solution.py:22
  47.4 5.2 %fusion.1 = (f32[7,384]{1,0:T(8,128)S(1)}, bf16[7,896,384]{1,2,0:T(8,128)(2,1)S(1)}, f32[384,7,896]{2,0,1:T(8,128)}) fusion(f32[7,896,384]{1,2,0:T(8,128)S(1)} %copy-done.1, f32[7,384]{1,0:T(8,128)S(1)} %get-tuple-element.15, bf16[384,128]{1,0:T(8,128)(2,1)S(1)} %convolution_convert_fusion, bf16[384,128]{1,0:T(8,128)(2,1)S(1)} %collective-permute-done.8, ...), kind=kOutput, calls=%fused_computation.3 | convolution fusion | flops 629290368 | bytes 25023488 | tf_op jit(solution)/shard_map/jd,thd->hjt/dot_general | solution.py:126
  52.7 1.4 %fusion.62 = (bf16[896,128]{1,0:T(8,128)(2,1)S(1)}, f32[896,128]{1,0:T(8,128)S(1)}) fusion(bf16[7,896,384]{1,2,0:T(8,128)(2,1)S(1)} %get-tuple-element.4, bf16[384,7,128]{2,1,0:T(8,128)(2,1)S(1)} %maximum_select_fusion.5), kind=kOutput, calls=%fused_computation.99 | convolution fusion | flops 616677376 | bytes 6193152 | tf_op jit(solution)/shard_map/hjt,thd->jd/dot_general | solution.py:102
  54.1 1.3 %collective-permute-start.13 = (bf16[384,128]{1,0:T(8,128)(2,1)S(1)}, bf16[384,128]{1,0:T(8,128)(2,1)S(1)}, u32[]{:S(2)}, u32[]{:S(2)}) collective-permute-start(bf16[384,128]{1,0:T(8,128)(2,1)S(1)} %slice.42), channel_id=1, source_target_pairs={{2,0},{3,1},{4,2},{5,3},{6,4},{7,5},{8,6},{9,7},{10,8},{11,9},{12,... | collective-permute-start | bytes 294920 | tf_op jit(solution)/shard_map/ppermute | solution.py:22
  55.4 1.3 %collective-permute-start.14 = (bf16[128,128]{1,0:T(8,128)(2,1)S(1)}, bf16[128,128]{1,0:T(8,128)(2,1)S(1)}, u32[]{:S(2)}, u32[]{:S(2)}) collective-permute-start(bf16[128,128]{1,0:T(8,128)(2,1)S(1)} %slice.43), channel_id=1, source_target_pairs={{4,0},{5,1},{6,2},{7,3},{8,4},{9,5},{10,6},{11,7},{12,8},{13,9},{1... | collective-permute-start | bytes 98312 | tf_op jit(solution)/shard_map/ppermute | solution.py:22
  56.8 6.1 %collective-permute-done.14 = bf16[128,128]{1,0:T(8,128)(2,1)S(1)} collective-permute-done((bf16[128,128]{1,0:T(8,128)(2,1)S(1)}, bf16[128,128]{1,0:T(8,128)(2,1)S(1)}, u32[]{:S(2)}, u32[]{:S(2)}) %collective-permute-start.14) | collective-permute-done | bytes 32800 | tf_op jit(solution)/shard_map/ppermute | solution.py:22
  62.8 3.5 %fusion.25 = f32[3584,128]{1,0:T(8,128)S(1)} fusion(bf16[192,3584]{1,0:T(8,128)(2,1)} %collective-permute-done.5, bf16[192,3584]{1,0:T(8,128)(2,1)} %fusion.9, pred[]{:T(512)S(6)} %eq.12, f32[896,128]{1,0:T(8,128)S(1)} %get-tuple-element.21, bf16[384,128]{1,0:T(8,128)(2,1)S(1)} %collective-permute-done.13, bf16[128,128]{1,0:T(8,128)(2,1)S(1)} %collective-permute-done.14), kind=kOutput, calls=%fused_computation.44 | convolution fusion | flops 364953600 | bytes 4915201 | tf_op jit(solution)/shard_map/dot_general | solution.py:107
  68.2 9.1 %collective-permute-done.15 = bf16[1792,128]{1,0:T(8,128)(2,1)S(1)} collective-permute-done((bf16[1792,128]{1,0:T(8,128)(2,1)S(1)}, bf16[1792,128]{1,0:T(8,128)(2,1)S(1)}, u32[]{:S(2)}, u32[]{:S(2)}) %collective-permute-start.15) | collective-permute-done | bytes 458784 | tf_op jit(solution)/shard_map/ppermute | solution.py:26
  79.7 5.0 %collective-permute-done.16 = bf16[896,128]{1,0:T(8,128)(2,1)S(1)} collective-permute-done((bf16[896,128]{1,0:T(8,128)(2,1)S(1)}, bf16[896,128]{1,0:T(8,128)(2,1)S(1)}, u32[]{:S(2)}, u32[]{:S(2)}) %collective-permute-start.16) | collective-permute-done | bytes 229408 | tf_op jit(solution)/shard_map/ppermute | solution.py:26
  84.7 2.1 %collective-permute-start.17 = (bf16[448,128]{1,0:T(8,128)(2,1)S(1)}, bf16[448,128]{1,0:T(8,128)(2,1)S(1)}, u32[]{:S(2)}, u32[]{:S(2)}) collective-permute-start(bf16[448,128]{1,0:T(8,128)(2,1)S(1)} %dynamic-slice_convert_fusion.2), channel_id=1, source_target_pairs={{0,4},{1,5},{2,6},{3,7},{4,0},{5,1},{6,2},{7,3},{8,12},{9,13},{10,... | collective-permute-start | bytes 344072 | tf_op jit(solution)/shard_map/ppermute | solution.py:26
  86.8 7.3 %fusion.3 = bf16[7,896,384]{1,2,0:T(8,128)(2,1)S(1)} fusion(f32[384,7,896]{2,0,1:T(8,128)} %get-tuple-element.17, f32[7,384]{1,0:T(8,128)S(1)} %get-tuple-element.3, f32[7,896,384]{1,2,0:T(8,128)} %get-tuple-element.16, f32[7,384]{1,0:T(8,128)S(1)} %get-tuple-element.15), kind=kLoop, calls=%fused_computation.5 | loop fusion | flops 9633792 | bytes 24105984 | tf_op jit(solution)/shard_map/convert_element_type | solution.py:128
  94.2 1.3 %collective-permute-start.18 = (bf16[224,128]{1,0:T(8,128)(2,1)S(1)}, bf16[224,128]{1,0:T(8,128)(2,1)S(1)}, u32[]{:S(2)}, u32[]{:S(2)}) collective-permute-start(bf16[224,128]{1,0:T(8,128)(2,1)S(1)} %dynamic-slice_convert_fusion.3), channel_id=1, source_target_pairs={{0,8},{1,9},{2,10},{3,11},{4,12},{5,13},{6,14},{7,15},{8,0},{9,1},... | collective-permute-start | bytes 172040 | tf_op jit(solution)/shard_map/ppermute | solution.py:26
  95.5 2.2 %fusion.61 = (bf16[896,128]{1,0:T(8,128)(2,1)S(1)}, f32[896,128]{1,0:T(8,128)}) fusion(bf16[7,896,384]{1,2,0:T(8,128)(2,1)S(1)} %fusion.3, bf16[384,7,128]{2,1,0:T(8,128)(2,1)S(1)} %maximum_select_fusion.4), kind=kOutput, calls=%fused_computation.98 | convolution fusion | flops 616792064 | bytes 6193152 | tf_op jit(solution)/shard_map/hjt,thd->jd/dot_general | solution.py:134
  97.7 1.3 %collective-permute-start.10 = (bf16[384,128]{1,0:T(8,128)(2,1)S(1)}, bf16[384,128]{1,0:T(8,128)(2,1)S(1)}, u32[]{:S(2)}, u32[]{:S(2)}) collective-permute-start(bf16[384,128]{1,0:T(8,128)(2,1)S(1)} %slice.39), channel_id=1, source_target_pairs={{2,0},{3,1},{4,2},{5,3},{6,4},{7,5},{8,6},{9,7},{10,8},{11,9},{12,... | collective-permute-start | bytes 294920 | tf_op jit(solution)/shard_map/ppermute | solution.py:22
  99.0 1.3 %collective-permute-start.11 = (bf16[128,128]{1,0:T(8,128)(2,1)S(1)}, bf16[128,128]{1,0:T(8,128)(2,1)S(1)}, u32[]{:S(2)}, u32[]{:S(2)}) collective-permute-start(bf16[128,128]{1,0:T(8,128)(2,1)S(1)} %slice.40), channel_id=1, source_target_pairs={{4,0},{5,1},{6,2},{7,3},{8,4},{9,5},{10,6},{11,7},{12,8},{13,9},{1... | collective-permute-start | bytes 98312 | tf_op jit(solution)/shard_map/ppermute | solution.py:22
  100.4 4.8 %collective-permute-start.19 = (bf16[224,128]{1,0:T(8,128)(2,1)S(1)}, bf16[224,128]{1,0:T(8,128)(2,1)S(1)}, u32[]{:S(2)}, u32[]{:S(2)}) collective-permute-start(bf16[224,128]{1,0:T(8,128)(2,1)S(1)} %add_convert_fusion), channel_id=1, source_target_pairs={{0,8},{1,9},{2,10},{3,11},{4,12},{5,13},{6,14},{7,15},{8,0},{9,1},... | collective-permute-start | bytes 172040 | tf_op jit(solution)/shard_map/ppermute | solution.py:26
  105.1 2.3 %fusion.12 = bf16[128,7,384]{2,0,1:T(8,128)(2,1)S(1)} fusion(bf16[7,896,384]{1,2,0:T(8,128)(2,1)S(1)} %fusion.3, bf16[384,128]{1,0:T(8,128)(2,1)S(1)} %maximum_select_fusion.12, bf16[384,128]{1,0:T(8,128)(2,1)S(1)} %collective-permute-done.2, bf16[128,128]{1,0:T(8,128)(2,1)} %collective-permute-done.1), kind=kOutput, calls=%fused_computation.21 | convolution fusion | flops 617938944 | bytes 5734400 | tf_op jit(solution)/shard_map/hjt,jd->thd/dot_general | solution.py:130
  107.6 1.5 %collective-permute-start.20 = (bf16[448,128]{1,0:T(8,128)(2,1)S(1)}, bf16[448,128]{1,0:T(8,128)(2,1)S(1)}, u32[]{:S(2)}, u32[]{:S(2)}) collective-permute-start(bf16[448,128]{1,0:T(8,128)(2,1)S(1)} %maximum_select_fusion.11), channel_id=1, source_target_pairs={{0,4},{1,5},{2,6},{3,7},{4,0},{5,1},{6,2},{7,3},{8,12},{9,13},{10,... | collective-permute-start | bytes 344072 | tf_op jit(solution)/shard_map/ppermute | solution.py:26
  109.7 2.7 %collective-permute-done.20 = bf16[448,128]{1,0:T(8,128)(2,1)S(1)} collective-permute-done((bf16[448,128]{1,0:T(8,128)(2,1)S(1)}, bf16[448,128]{1,0:T(8,128)(2,1)S(1)}, u32[]{:S(2)}, u32[]{:S(2)}) %collective-permute-start.20) | collective-permute-done | bytes 114720 | tf_op jit(solution)/shard_map/ppermute | solution.py:26
  112.5 2.1 %collective-permute-start.21 = (bf16[896,128]{1,0:T(8,128)(2,1)S(1)}, bf16[896,128]{1,0:T(8,128)(2,1)S(1)}, u32[]{:S(2)}, u32[]{:S(2)}) collective-permute-start(bf16[896,128]{1,0:T(8,128)(2,1)S(1)} %maximum_select_fusion.10), channel_id=1, source_target_pairs={{0,2},{1,3},{2,0},{3,1},{4,6},{5,7},{6,4},{7,5},{8,10},{9,11},{10,... | collective-permute-start | bytes 688136 | tf_op jit(solution)/shard_map/ppermute | solution.py:26
  115.5 3.0 %collective-permute-done.21 = bf16[896,128]{1,0:T(8,128)(2,1)S(1)} collective-permute-done((bf16[896,128]{1,0:T(8,128)(2,1)S(1)}, bf16[896,128]{1,0:T(8,128)(2,1)S(1)}, u32[]{:S(2)}, u32[]{:S(2)}) %collective-permute-start.21) | collective-permute-done | bytes 229408 | tf_op jit(solution)/shard_map/ppermute | solution.py:26
  (78 shorter events, 20.5 us)
Async XLA Ops:
  0.6 8.8 %copy-start = (bf16[1792,256]{1,0:T(8,128)(2,1)S(1)}, bf16[1792,256]{1,0:T(8,128)(2,1)}, u32[]{:S(2)}) copy-start(bf16[1792,256]{1,0:T(8,128)(2,1)} %param.9) | copy-start | bytes 2752516
  0.7 7.3 %copy-start.4 = (s32[1,192]{1,0:T(1,128)S(1)}, s32[1,192]{1,0:T(1,128)}, u32[]{:S(2)}) copy-start(s32[1,192]{1,0:T(1,128)} %param.8) | copy-start | bytes 2308
  0.7 7.3 %copy-start.2 = (bf16[1,192,3584]{2,1,0:T(8,128)(2,1)S(1)}, bf16[1,192,3584]{2,1,0:T(8,128)(2,1)}, u32[]{:S(2)}) copy-start(bf16[1,192,3584]{2,1,0:T(8,128)(2,1)} %param.7) | copy-start | bytes 4128772
  2.7 16.7 %collective-permute-start.3 = (bf16[192,896]{1,0:T(8,128)(2,1)}, bf16[192,896]{1,0:T(8,128)(2,1)}, u32[]{:S(2)}, u32[]{:S(2)}) collective-permute-start(bf16[192,896]{1,0:T(8,128)(2,1)} %get-tuple-element.8), channel_id=1, source_target_pairs={{0,1},{1,0},{2,3},{3,2},{4,5},{5,4},{6,7},{7,6},{8,9},{9,8},{10,11... | collective-permute-start | bytes 1032200 | tf_op jit(solution)/shard_map/ppermute | solution.py:26
  4.0 10.5 %collective-permute-start = (bf16[192,128]{1,0:T(8,128)(2,1)S(1)}, bf16[192,128]{1,0:T(8,128)(2,1)}, u32[]{:S(2)}, u32[]{:S(2)}) collective-permute-start(bf16[192,128]{1,0:T(8,128)(2,1)S(1)} %get-tuple-element.14), channel_id=1, source_target_pairs={{0,1},{1,0},{2,3},{3,2},{4,5},{5,4},{6,7},{7,6},{8,9},{9,8},{10,11... | collective-permute-start | bytes 147464 | tf_op jit(solution)/shard_map/ppermute | solution.py:26
  7.6 17.7 %collective-permute-start.4 = (bf16[192,896]{1,0:T(8,128)(2,1)}, bf16[192,896]{1,0:T(8,128)(2,1)}, u32[]{:S(2)}, u32[]{:S(2)}) collective-permute-start(bf16[192,896]{1,0:T(8,128)(2,1)} %get-tuple-element.10), channel_id=1, source_target_pairs={{0,1},{1,0},{2,3},{3,2},{4,5},{5,4},{6,7},{7,6},{8,9},{9,8},{10,11... | collective-permute-start | bytes 1032200 | tf_op jit(solution)/shard_map/ppermute | solution.py:26
  9.4 25.8 %collective-permute-start.5 = (bf16[192,3584]{1,0:T(8,128)(2,1)}, bf16[192,3584]{1,0:T(8,128)(2,1)}, u32[]{:S(2)}, u32[]{:S(2)}) collective-permute-start(bf16[192,3584]{1,0:T(8,128)(2,1)} %fusion.9), channel_id=1, source_target_pairs={{0,1},{1,0},{2,3},{3,2},{4,5},{5,4},{6,7},{7,6},{8,9},{9,8},{10,11... | collective-permute-start | bytes 4128776 | tf_op jit(solution)/shard_map/ppermute | solution.py:26
  9.5 25.7 %collective-permute-start.6 = (bf16[1792,128]{1,0:T(8,128)(2,1)S(1)}, bf16[1792,128]{1,0:T(8,128)(2,1)}, u32[]{:S(2)}, u32[]{:S(2)}) collective-permute-start(bf16[1792,128]{1,0:T(8,128)(2,1)S(1)} %constant_dynamic-slice_fusion.3), channel_id=1, source_target_pairs={{0,16},{16,0},{1,17},{17,1},{2,18},{18,2},{3,19},{19,3},{4,20},{20... | collective-permute-start | bytes 1376264 | tf_op jit(solution)/shard_map/ppermute | solution.py:26
  15.4 11.3 %collective-permute-start.2 = (bf16[384,128]{1,0:T(8,128)(2,1)S(1)}, bf16[384,128]{1,0:T(8,128)(2,1)S(1)}, u32[]{:S(2)}, u32[]{:S(2)}) collective-permute-start(bf16[384,128]{1,0:T(8,128)(2,1)S(1)} %maximum_select_fusion.12), channel_id=1, source_target_pairs={{0,2},{1,3},{2,4},{3,5},{4,6},{5,7},{6,8},{7,9},{8,10},{9,11},{10,... | collective-permute-start | bytes 294920 | tf_op jit(solution)/shard_map/ppermute | solution.py:22
  19.4 7.2 %collective-permute-start.1 = (bf16[128,128]{1,0:T(8,128)(2,1)}, bf16[128,128]{1,0:T(8,128)(2,1)}, u32[]{:S(2)}, u32[]{:S(2)}) collective-permute-start(bf16[128,128]{1,0:T(8,128)(2,1)} %slice.36), channel_id=1, source_target_pairs={{0,4},{1,5},{2,6},{3,7},{4,8},{5,9},{6,10},{7,11},{8,12},{9,13},{1... | collective-permute-start | bytes 98312 | tf_op jit(solution)/shard_map/ppermute | solution.py:22
  35.2 12.3 %copy-start.1 = (f32[7,896,384]{1,2,0:T(8,128)S(1)}, f32[7,896,384]{1,2,0:T(8,128)}, u32[]{:S(2)}) copy-start(f32[7,896,384]{1,2,0:T(8,128)} %get-tuple-element.16) | copy-start | bytes 28901380
  39.4 8.1 %collective-permute-start.8 = (bf16[384,128]{1,0:T(8,128)(2,1)S(1)}, bf16[384,128]{1,0:T(8,128)(2,1)S(1)}, u32[]{:S(2)}, u32[]{:S(2)}) collective-permute-start(bf16[384,128]{1,0:T(8,128)(2,1)S(1)} %convolution_convert_fusion), channel_id=1, source_target_pairs={{0,2},{1,3},{2,4},{3,5},{4,6},{5,7},{6,8},{7,9},{8,10},{9,11},{10,... | collective-permute-start | bytes 294920 | tf_op jit(solution)/shard_map/ppermute | solution.py:22
  43.0 4.5 %collective-permute-start.7 = (bf16[128,128]{1,0:T(8,128)(2,1)S(1)}, bf16[128,128]{1,0:T(8,128)(2,1)S(1)}, u32[]{:S(2)}, u32[]{:S(2)}) collective-permute-start(bf16[128,128]{1,0:T(8,128)(2,1)S(1)} %slice.37), channel_id=1, source_target_pairs={{0,4},{1,5},{2,6},{3,7},{4,8},{5,9},{6,10},{7,11},{8,12},{9,13},{1... | collective-permute-start | bytes 98312 | tf_op jit(solution)/shard_map/ppermute | solution.py:22
  54.1 8.7 %collective-permute-start.13 = (bf16[384,128]{1,0:T(8,128)(2,1)S(1)}, bf16[384,128]{1,0:T(8,128)(2,1)S(1)}, u32[]{:S(2)}, u32[]{:S(2)}) collective-permute-start(bf16[384,128]{1,0:T(8,128)(2,1)S(1)} %slice.42), channel_id=1, source_target_pairs={{2,0},{3,1},{4,2},{5,3},{6,4},{7,5},{8,6},{9,7},{10,8},{11,9},{12,... | collective-permute-start | bytes 294920 | tf_op jit(solution)/shard_map/ppermute | solution.py:22
  55.4 7.4 %collective-permute-start.14 = (bf16[128,128]{1,0:T(8,128)(2,1)S(1)}, bf16[128,128]{1,0:T(8,128)(2,1)S(1)}, u32[]{:S(2)}, u32[]{:S(2)}) collective-permute-start(bf16[128,128]{1,0:T(8,128)(2,1)S(1)} %slice.43), channel_id=1, source_target_pairs={{4,0},{5,1},{6,2},{7,3},{8,4},{9,5},{10,6},{11,7},{12,8},{13,9},{1... | collective-permute-start | bytes 98312 | tf_op jit(solution)/shard_map/ppermute | solution.py:22
  66.3 1.2 %copy-start.3 = (f32[3584,128]{1,0:T(8,128)}, f32[3584,128]{1,0:T(8,128)S(1)}, u32[]{:S(2)}) copy-start(f32[3584,128]{1,0:T(8,128)S(1)} %fusion.25) | copy-start | bytes 5505028
  67.6 9.7 %collective-permute-start.15 = (bf16[1792,128]{1,0:T(8,128)(2,1)S(1)}, bf16[1792,128]{1,0:T(8,128)(2,1)S(1)}, u32[]{:S(2)}, u32[]{:S(2)}) collective-permute-start(bf16[1792,128]{1,0:T(8,128)(2,1)S(1)} %dynamic-slice_convert_fusion), channel_id=1, source_target_pairs={{0,16},{16,0},{1,17},{17,1},{2,18},{18,2},{3,19},{19,3},{4,20},{20... | collective-permute-start | bytes 1376264 | tf_op jit(solution)/shard_map/ppermute | solution.py:26
  78.6 6.1 %collective-permute-start.16 = (bf16[896,128]{1,0:T(8,128)(2,1)S(1)}, bf16[896,128]{1,0:T(8,128)(2,1)S(1)}, u32[]{:S(2)}, u32[]{:S(2)}) collective-permute-start(bf16[896,128]{1,0:T(8,128)(2,1)S(1)} %dynamic-slice_convert_fusion.1), channel_id=1, source_target_pairs={{0,2},{1,3},{2,0},{3,1},{4,6},{5,7},{6,4},{7,5},{8,10},{9,11},{10,... | collective-permute-start | bytes 688136 | tf_op jit(solution)/shard_map/ppermute | solution.py:26
  84.7 9.4 %collective-permute-start.17 = (bf16[448,128]{1,0:T(8,128)(2,1)S(1)}, bf16[448,128]{1,0:T(8,128)(2,1)S(1)}, u32[]{:S(2)}, u32[]{:S(2)}) collective-permute-start(bf16[448,128]{1,0:T(8,128)(2,1)S(1)} %dynamic-slice_convert_fusion.2), channel_id=1, source_target_pairs={{0,4},{1,5},{2,6},{3,7},{4,0},{5,1},{6,2},{7,3},{8,12},{9,13},{10,... | collective-permute-start | bytes 344072 | tf_op jit(solution)/shard_map/ppermute | solution.py:26
  94.2 6.1 %collective-permute-start.18 = (bf16[224,128]{1,0:T(8,128)(2,1)S(1)}, bf16[224,128]{1,0:T(8,128)(2,1)S(1)}, u32[]{:S(2)}, u32[]{:S(2)}) collective-permute-start(bf16[224,128]{1,0:T(8,128)(2,1)S(1)} %dynamic-slice_convert_fusion.3), channel_id=1, source_target_pairs={{0,8},{1,9},{2,10},{3,11},{4,12},{5,13},{6,14},{7,15},{8,0},{9,1},... | collective-permute-start | bytes 172040 | tf_op jit(solution)/shard_map/ppermute | solution.py:26
  97.7 16.8 %collective-permute-start.10 = (bf16[384,128]{1,0:T(8,128)(2,1)S(1)}, bf16[384,128]{1,0:T(8,128)(2,1)S(1)}, u32[]{:S(2)}, u32[]{:S(2)}) collective-permute-start(bf16[384,128]{1,0:T(8,128)(2,1)S(1)} %slice.39), channel_id=1, source_target_pairs={{2,0},{3,1},{4,2},{5,3},{6,4},{7,5},{8,6},{9,7},{10,8},{11,9},{12,... | collective-permute-start | bytes 294920 | tf_op jit(solution)/shard_map/ppermute | solution.py:22
  99.0 15.5 %collective-permute-start.11 = (bf16[128,128]{1,0:T(8,128)(2,1)S(1)}, bf16[128,128]{1,0:T(8,128)(2,1)S(1)}, u32[]{:S(2)}, u32[]{:S(2)}) collective-permute-start(bf16[128,128]{1,0:T(8,128)(2,1)S(1)} %slice.40), channel_id=1, source_target_pairs={{4,0},{5,1},{6,2},{7,3},{8,4},{9,5},{10,6},{11,7},{12,8},{13,9},{1... | collective-permute-start | bytes 98312 | tf_op jit(solution)/shard_map/ppermute | solution.py:22
  100.4 7.2 %collective-permute-start.19 = (bf16[224,128]{1,0:T(8,128)(2,1)S(1)}, bf16[224,128]{1,0:T(8,128)(2,1)S(1)}, u32[]{:S(2)}, u32[]{:S(2)}) collective-permute-start(bf16[224,128]{1,0:T(8,128)(2,1)S(1)} %add_convert_fusion), channel_id=1, source_target_pairs={{0,8},{1,9},{2,10},{3,11},{4,12},{5,13},{6,14},{7,15},{8,0},{9,1},... | collective-permute-start | bytes 172040 | tf_op jit(solution)/shard_map/ppermute | solution.py:26
  107.6 4.9 %collective-permute-start.20 = (bf16[448,128]{1,0:T(8,128)(2,1)S(1)}, bf16[448,128]{1,0:T(8,128)(2,1)S(1)}, u32[]{:S(2)}, u32[]{:S(2)}) collective-permute-start(bf16[448,128]{1,0:T(8,128)(2,1)S(1)} %maximum_select_fusion.11), channel_id=1, source_target_pairs={{0,4},{1,5},{2,6},{3,7},{4,0},{5,1},{6,2},{7,3},{8,12},{9,13},{10,... | collective-permute-start | bytes 344072 | tf_op jit(solution)/shard_map/ppermute | solution.py:26
  109.7 11.6 %collective-permute-start.9 = (bf16[192,896]{1,0:T(8,128)(2,1)S(1)}, bf16[192,896]{1,0:T(8,128)(2,1)S(1)}, u32[]{:S(2)}, u32[]{:S(2)}) collective-permute-start(bf16[192,896]{1,0:T(8,128)(2,1)S(1)} %copy.36), channel_id=1, source_target_pairs={{0,1},{1,0},{2,3},{3,2},{4,5},{5,4},{6,7},{7,6},{8,9},{9,8},{10,11... | collective-permute-start | bytes 1032200 | tf_op jit(solution)/shard_map/ppermute | solution.py:26
  112.5 6.1 %collective-permute-start.21 = (bf16[896,128]{1,0:T(8,128)(2,1)S(1)}, bf16[896,128]{1,0:T(8,128)(2,1)S(1)}, u32[]{:S(2)}, u32[]{:S(2)}) collective-permute-start(bf16[896,128]{1,0:T(8,128)(2,1)S(1)} %maximum_select_fusion.10), channel_id=1, source_target_pairs={{0,2},{1,3},{2,0},{3,1},{4,6},{5,7},{6,4},{7,5},{8,10},{9,11},{10,... | collective-permute-start | bytes 688136 | tf_op jit(solution)/shard_map/ppermute | solution.py:26
  118.7 3.6 %collective-permute-start.22 = (bf16[1792,128]{1,0:T(8,128)(2,1)S(1)}, bf16[1792,128]{1,0:T(8,128)(2,1)S(1)}, u32[]{:S(2)}, u32[]{:S(2)}) collective-permute-start(bf16[1792,128]{1,0:T(8,128)(2,1)S(1)} %maximum_select_fusion.9), channel_id=1, source_target_pairs={{0,1},{1,0},{2,3},{3,2},{4,5},{5,4},{6,7},{7,6},{8,9},{9,8},{10,11... | collective-permute-start | bytes 1376264 | tf_op jit(solution)/shard_map/ppermute | solution.py:26
  118.8 1.8 %collective-permute-start.12 = (bf16[192,128]{1,0:T(8,128)(2,1)S(1)}, bf16[192,128]{1,0:T(8,128)(2,1)S(1)}, u32[]{:S(2)}, u32[]{:S(2)}) collective-permute-start(bf16[192,128]{1,0:T(8,128)(2,1)S(1)} %get-tuple-element.12), channel_id=1, source_target_pairs={{0,1},{1,0},{2,3},{3,2},{4,5},{5,4},{6,7},{7,6},{8,9},{9,8},{10,11... | collective-permute-start | bytes 147464 | tf_op jit(solution)/shard_map/ppermute | solution.py:26

commit v2 on v1

v2 whole, which is shorter than its diff:
```python
import functools
import math

import jax
import jax.numpy as jnp
from jax import lax
from jax.experimental import pallas as pl
from jax.experimental.pallas import tpu as pltpu
from jax.sharding import PartitionSpec as P

QH = 14
KVH = 2
HD = 128
WINDOW = 512
LEVELS = 4
GROUP = 7
BLOCK = 128
SPAN = WINDOW + BLOCK

masked_score = -1e30
score_scale = 1.0 / math.sqrt(HD)
exp2_scale = score_scale * math.log2(math.e)

bf16 = jnp.bfloat16
f32 = jnp.float32
ANY = pl.BlockSpec(memory_space=pltpu.HBM)
VMEM = pl.BlockSpec(memory_space=pltpu.VMEM)


def limit(mib):
    return pltpu.CompilerParams(vmem_limit_bytes=mib * 1024 * 1024)


def shifted(value, steps, only=None):
    count = lax.axis_size("seq")
    first, last = (max(0, -steps), min(count, count - steps))
    pairs = [(source, source + steps) for source in range(first, last)]
    if only is not None:
        pairs = [pair for pair in pairs if pair[0] % 2 == only]
    return lax.ppermute(value, "seq", pairs)


def swapped(value, axis, flip):
    return lax.ppermute(value, axis, [(i, i ^ flip) for i in range(lax.axis_size(axis))])


def crossed(value, flips):
    count = lax.axis_size("dp") * lax.axis_size("seq")
    return lax.ppermute(value, ("dp", "seq"), [(i, i ^ flips[i % 2]) for i in range(count)])


def ordered(bit, own, other, axis=0):
    return jnp.where(
        bit == 0,
        jnp.concatenate([own, other], axis=axis),
        jnp.concatenate([other, own], axis=axis),
    )


def run_copies(pairs, sems):
    copies = [pltpu.make_async_copy(src, dst, sems.at[n]) for n, (src, dst) in enumerate(pairs)]
    for copy in copies:
        copy.start()
    return copies


def own_first(core, tok, own, oth, dst, begin=0):
    return [
        (own, dst.at[pl.ds(begin + core * tok, tok)]),
        (oth, dst.at[pl.ds(begin + (1 - core) * tok, tok)]),
    ]


def head_pairs(core, tok, raw, q_buf, g_buf, k_buf):
    q_own, q_oth, g_own, g_oth, k_own, k_oth, p_own, p_oth = raw
    wide = pl.ds(pl.multiple_of(core * GROUP * HD, HD), GROUP * HD)
    slim = pl.ds(pl.multiple_of(core * HD, HD), HD)
    rest = WINDOW - 2 * tok
    pairs = own_first(core, tok, q_own.at[:, wide], q_oth.at[:, wide], q_buf)
    pairs += own_first(core, tok, g_own.at[:, wide], g_oth.at[:, wide], g_buf)
    pairs += own_first(core, tok, k_own.at[:, slim], k_oth.at[:, slim], k_buf, WINDOW)
    pairs += own_first(core, tok, p_own.at[:, slim], p_oth.at[:, slim], k_buf, rest)
    return pairs


def tail_copy(core, tok, far_own, far_oth, k_buf, sem):
    slim = pl.ds(pl.multiple_of(core * HD, HD), HD)
    rest = WINDOW - 2 * tok
    rows = pl.ds(tok - rest, rest)

    @pl.when(core == 1)
    def _():
        pltpu.make_async_copy(far_own.at[rows, slim], k_buf.at[pl.ds(0, rest)], sem).start()

    @pl.when(core == 0)
    def _():
        pltpu.make_async_copy(far_oth.at[rows, slim], k_buf.at[pl.ds(0, rest)], sem).start()

    return pltpu.make_async_copy(far_own.at[rows, slim], k_buf.at[pl.ds(0, rest)], sem)


def head_masks(core, own, oth):
    spikes = jnp.where(
        core == 0,
        jnp.concatenate([own, oth], axis=1),
        jnp.concatenate([oth, own], axis=1),
    ).astype(f32)
    return jnp.where(core == 0, spikes[:GROUP], spikes[GROUP:])


def biases(chip, tok, block):
    later = lax.broadcasted_iota(jnp.int32, (BLOCK, BLOCK), 0)
    query = lax.broadcasted_iota(jnp.int32, (BLOCK, BLOCK), 1)
    first_key = WINDOW - chip * 2 * tok
    tiles = SPAN // BLOCK
    result = []
    for tile in range(tiles):
        begin = (block + tile) * BLOCK
        bias = None
        if begin < WINDOW:
            bias = jnp.where(begin >= first_key, 0.0, masked_score).astype(f32)
        if tile == 0:
            bias = jnp.where(later > query, bias if bias is not None else 0.0, masked_score)
        elif tile == tiles - 1:
            bias = jnp.where(later <= query, 0.0, masked_score)
        result.append(bias)
    return result


def dot_nt(a, b):
    return lax.dot_general(a, b, (((1,), (1,)), ((), ())), preferred_element_type=f32)


def dot_tn(a, b):
    return lax.dot_general(a, b, (((0,), (0,)), ((), ())), preferred_element_type=f32)


def masked(scores, bias):
    tiles = [scores[n * BLOCK : (n + 1) * BLOCK] for n in range(len(bias))]
    return jnp.concatenate(
        [tile if add is None else tile + add for tile, add in zip(tiles, bias)], axis=0
    )


def stacked(buf, block):
    rows = slice(block * BLOCK, (block + 1) * BLOCK)
    return jnp.concatenate(
        [buf[rows, head * HD : (head + 1) * HD] for head in range(GROUP)], axis=0
    )


def value_kernel(tok, *refs):
    raw, far_own, far_oth, m_own, m_oth = refs[:8], *refs[8:12]
    own_out, near_out, far_out, top_out, norm_out = refs[12:17]
    q_buf, g_buf, k_buf, p_buf, acc, sems = refs[17:]
    place = lax.axis_index("seq")
    core, chip = lax.rem(place, 2), lax.div(place, 2)
    copies = run_copies(head_pairs(core, tok, raw, q_buf, g_buf, k_buf), sems)
    copies.append(tail_copy(core, tok, far_own, far_oth, k_buf, sems.at[8]))
    spikes = head_masks(core, m_own[...], m_oth[...])
    acc[...] = jnp.zeros_like(acc)
    for copy in copies:
        copy.wait()
    for block in range(2 * tok // BLOCK):
        bias = biases(chip, tok, block)
        begin = block * BLOCK
        rows = slice(begin, begin + BLOCK)
        keys = k_buf[begin : begin + SPAN, :]
        for head in range(GROUP):
            cols = slice(head * HD, (head + 1) * HD)
            scores = masked(dot_nt(keys, q_buf[rows, cols]), bias)
            top = jnp.max(scores, axis=0, keepdims=True)
            expo = jnp.exp2((scores - top) * exp2_scale)
            norm = spikes[head : head + 1, rows] / jnp.sum(expo, axis=0, keepdims=True)
            p_buf[:, cols] = (expo * norm).astype(bf16)
            at = block * GROUP + head
            top_out[at : at + 1, :] = top
            norm_out[at : at + 1, :] = norm
        acc[begin : begin + SPAN, :] += jnp.dot(
            p_buf[...], stacked(g_buf, block), preferred_element_type=f32
        )
    rest = WINDOW - 2 * tok
    far_out[...] = acc[:rest, :].astype(bf16)
    near_out[...] = acc[rest:WINDOW, :].astype(bf16)
    own_out[...] = acc[WINDOW:, :]


def key_kernel(tok, *refs):
    raw, far_own, far_oth = refs[:8], refs[8], refs[9]
    top_in, norm_in, v_own, v_near, v_far = refs[10:15]
    own_out, near_out, far_out, mine_out, send_out = refs[15:20]
    q_buf, g_buf, k_buf, v_buf, d_buf, acc, r_buf, sems, out_sems = refs[20:]
    place = lax.axis_index("seq")
    core, chip = lax.rem(place, 2), lax.div(place, 2)
    rest = WINDOW - 2 * tok
    pairs = head_pairs(core, tok, raw, q_buf, g_buf, k_buf)
    pairs += [
        (v_far, v_buf.at[pl.ds(0, rest)]),
        (v_near, v_buf.at[pl.ds(rest, 2 * tok)]),
        (v_own, v_buf.at[pl.ds(WINDOW, 2 * tok)]),
    ]
    copies = run_copies(pairs, sems)
    copies.append(tail_copy(core, tok, far_own, far_oth, k_buf, sems.at[len(pairs)]))
    acc[...] = jnp.zeros_like(acc)
    for copy in copies:
        copy.wait()
    for block in range(2 * tok // BLOCK):
        bias = biases(chip, tok, block)
        begin = block * BLOCK
        rows = slice(begin, begin + BLOCK)
        keys = k_buf[begin : begin + SPAN, :]
        values = v_buf[begin : begin + SPAN, :]
        for head in range(GROUP):
            cols = slice(head * HD, (head + 1) * HD)
            at = block * GROUP + head
            scores = masked(dot_nt(keys, q_buf[rows, cols]), bias)
            probs = jnp.exp2((scores - top_in[at : at + 1, :]) * exp2_scale)
            probs = probs * norm_in[at : at + 1, :]
            prob_grad = dot_nt(values, g_buf[rows, cols])
            delta = jnp.sum(probs.astype(bf16).astype(f32) * prob_grad, axis=0, keepdims=True)
            d_buf[:, cols] = (probs * (prob_grad - delta)).astype(bf16)
        acc[begin : begin + SPAN, :] += jnp.dot(
            d_buf[...], stacked(q_buf, block), preferred_element_type=f32
        )
        query_part = dot_tn(d_buf[...], keys) * score_scale
        for head in range(GROUP):
            cols = slice(head * HD, (head + 1) * HD)
            r_buf[rows, cols] = query_part[head * BLOCK : (head + 1) * BLOCK].astype(bf16)
    mine = pltpu.make_async_copy(r_buf.at[pl.ds(core * tok, tok)], mine_out, out_sems.at[0])
    send = pltpu.make_async_copy(r_buf.at[pl.ds((1 - core) * tok, tok)], send_out, out_sems.at[1])
    mine.start()
    send.start()
    far_out[...] = (acc[:rest, :] * score_scale).astype(bf16)
    near_out[...] = (acc[rest:WINDOW, :] * score_scale).astype(bf16)
    own_out[...] = acc[WINDOW:, :] * score_scale
    mine.wait()
    send.wait()


def head_scratch(tok):
    return [
        pltpu.VMEM((2 * tok, GROUP * HD), bf16),
        pltpu.VMEM((2 * tok, GROUP * HD), bf16),
        pltpu.VMEM((WINDOW + 2 * tok, HD), bf16),
    ]


def term_shapes(tok):
    return [
        jax.ShapeDtypeStruct((2 * tok, HD), f32),
        jax.ShapeDtypeStruct((2 * tok, HD), bf16),
        jax.ShapeDtypeStruct((WINDOW - 2 * tok, HD), bf16),
    ]


def value_terms(tok, raw, spikes):
    stats = jax.ShapeDtypeStruct((2 * tok // BLOCK * GROUP, BLOCK), f32)
    return pl.pallas_call(
        functools.partial(value_kernel, tok),
        out_shape=term_shapes(tok) + [stats, stats],
        in_specs=[ANY] * 10 + [VMEM] * 2,
        out_specs=[VMEM] * 5,
        scratch_shapes=head_scratch(tok)
        + [
            pltpu.VMEM((SPAN, GROUP * HD), bf16),
            pltpu.VMEM((WINDOW + 2 * tok, HD), f32),
            pltpu.SemaphoreType.DMA((9,)),
        ],
        compiler_params=limit(12),
        name="value_terms",
    )(*raw, *spikes)


def key_terms(tok, raw, top, norm, values):
    half = jax.ShapeDtypeStruct((tok, GROUP * HD), bf16)
    return pl.pallas_call(
        functools.partial(key_kernel, tok),
        out_shape=term_shapes(tok) + [half, half],
        in_specs=[ANY] * 10 + [VMEM] * 2 + [ANY] * 3,
        out_specs=[VMEM] * 3 + [ANY] * 2,
        scratch_shapes=head_scratch(tok)
        + [
            pltpu.VMEM((WINDOW + 2 * tok, HD), bf16),
            pltpu.VMEM((SPAN, GROUP * HD), bf16),
            pltpu.VMEM((WINDOW + 2 * tok, HD), f32),
            pltpu.VMEM((2 * tok, GROUP * HD), bf16),
            pltpu.SemaphoreType.DMA((12,)),
            pltpu.SemaphoreType.DMA((2,)),
        ],
        compiler_params=limit(14),
        name="key_terms",
    )(*raw, top, norm, *values)


def column(row):
    size = row.shape[1]
    diagonal = lax.broadcasted_iota(jnp.int32, (size, size), 0) == lax.broadcasted_iota(
        jnp.int32, (size, size), 1
    )
    return jnp.sum(jnp.where(diagonal, row, 0.0), axis=1, keepdims=True)


def project_kernel(tok, split, h_own, h_oth, l_own, l_oth, w_own, w_oth, out, tail, spiked, w_buf, sems):
    core = lax.rem(lax.axis_index("seq"), 2)
    if split:
        row = lax.axis_index("dp")
        depth = w_own.shape[0]
        pairs = [
            (w_own, w_buf.at[pl.ds(pl.multiple_of(row * depth, depth), depth)]),
            (w_oth, w_buf.at[pl.ds(pl.multiple_of((1 - row) * depth, depth), depth)]),
        ]
    else:
        pairs = [(w_own, w_buf)]
    copies = run_copies(pairs, sems)
    for source, level, place in ((h_own, l_own, core), (h_oth, l_oth, 1 - core)):
        factor = column(level[...].astype(f32) / LEVELS)
        rows = pl.ds(pl.multiple_of(place * tok, 64), tok)
        spiked[rows, :] = (source[...].astype(f32) * factor).astype(bf16)
    for copy in copies:
        copy.wait()
    values = jnp.dot(spiked[...], w_buf[...], preferred_element_type=f32).astype(bf16)
    out[...] = values
    tail[...] = values[4 * tok - WINDOW :, :]


def project(tok, hidden, levels, weight):
    depth = hidden[0].shape[1]
    split = len(weight) == 2
    return pl.pallas_call(
        functools.partial(project_kernel, tok, split),
        out_shape=[
            jax.ShapeDtypeStruct((2 * tok, HD), bf16),
            jax.ShapeDtypeStruct((WINDOW - 2 * tok, HD), bf16),
            jax.ShapeDtypeStruct((2 * tok, depth), bf16),
        ],
        in_specs=[VMEM] * 4 + [ANY] * 2,
        out_specs=[VMEM] * 3,
        scratch_shapes=[pltpu.VMEM((depth, HD), bf16), pltpu.SemaphoreType.DMA((2,))],
        compiler_params=limit(14),
        name="project",
    )(*hidden, *levels, weight[0], weight[-1])


def value_sum(tok, own, near, far):
    late = own[4 * tok - WINDOW :] + far.astype(f32)
    early = own[: 4 * tok - WINDOW]
    return jnp.concatenate([early, late], axis=0) + near.astype(f32)


def weight_kernel(tok, spiked, own, near, far, keep, send, w_buf):
    core = lax.rem(lax.axis_index("seq"), 2)
    rows = spiked.shape[1] // 16
    value_grad = value_sum(tok, own[...], near[...], far[...]).astype(bf16)
    mine = block_code(core)
    for part in range(4):
        term = dot_tn(spiked[:, part * 4 * rows : (part + 1) * 4 * rows], value_grad)
        for piece in range(4):
            index = part * 4 + piece
            other = (index & 3) | ((index & 4) << 1) | ((index & 8) >> 1)
            at = jnp.where(core == 0, index, other) ^ mine
            w_buf[pl.ds(pl.multiple_of(at * rows, 16), rows), :] = term[
                piece * rows : (piece + 1) * rows
            ]
    keep[...] = w_buf[: 8 * rows, :]
    send[...] = w_buf[8 * rows :, :].astype(bf16)


def chip_bits():
    chip = lax.div(lax.axis_index("seq"), 2)
    return chip & 1, (chip >> 1) & 1, (chip >> 2) & 1


def block_code(core):
    y, near, far = chip_bits()
    row = lax.axis_index("dp")
    return jnp.where(
        core == 0,
        row * 8 + y * 4 + near * 2 + far,
        near * 8 + row * 4 + y * 2 + far,
    )


def chip_code(core):
    y, near, far = chip_bits()
    return jnp.where(core == 0, y * 4 + near * 2 + far, near * 4 + y * 2 + far)


def weight_terms(tok, spiked, terms):
    depth = spiked.shape[1]
    return pl.pallas_call(
        functools.partial(weight_kernel, tok),
        out_shape=[
            jax.ShapeDtypeStruct((depth // 2, HD), f32),
            jax.ShapeDtypeStruct((depth // 2, HD), bf16),
        ],
        in_specs=[VMEM] * 4,
        out_specs=[VMEM] * 2,
        scratch_shapes=[pltpu.VMEM((depth, HD), f32)],
        compiler_params=limit(14),
        name="weight_terms",
    )(spiked, *terms)


def halve_kernel(held, got, *outs):
    total = held[...] + got[...].astype(f32)
    half = total.shape[0] // 2
    if len(outs) == 2:
        outs[0][...] = total[:half]
        outs[1][...] = total[half:].astype(bf16)
    else:
        outs[0][...] = total.astype(bf16)


def halve(held, got, last=False):
    rows = held.shape[0]
    if last:
        shapes = [jax.ShapeDtypeStruct((rows, HD), bf16)]
    else:
        shapes = [
            jax.ShapeDtypeStruct((rows // 2, HD), f32),
            jax.ShapeDtypeStruct((rows // 2, HD), bf16),
        ]
    return pl.pallas_call(
        halve_kernel,
        out_shape=shapes,
        in_specs=[VMEM] * 2,
        out_specs=[VMEM] * len(shapes),
        compiler_params=limit(6),
        name="halve",
    )(held, got)


def join_kernel(first, second, out):
    rows = first.shape[0]
    out[:rows, :] = first[...]
    out[rows:, :] = second[...]


def join(first, second):
    return pl.pallas_call(
        join_kernel,
        out_shape=jax.ShapeDtypeStruct((2 * first.shape[0], HD), bf16),
        in_specs=[VMEM] * 2,
        out_specs=VMEM,
        compiler_params=limit(4),
        name="join",
    )(first, second)


def place_weight_kernel(own_low, own_high, oth_low, oth_high, out, sems):
    core = lax.rem(lax.axis_index("seq"), 2)
    rows = own_low.shape[0] // 4
    pairs = []
    for halves, side in (((own_low, own_high), core), ((oth_low, oth_high), 1 - core)):
        code = chip_code(side)
        cols = pl.ds(pl.multiple_of(side * HD, HD), HD)
        for index in range(8):
            source = halves[index // 4].at[pl.ds(index % 4 * rows, rows)]
            at = pl.ds(pl.multiple_of((index ^ code) * rows, 16), rows)
            pairs.append((source, out.at[at, cols]))
    for copy in run_copies(pairs, sems):
        copy.wait()


def place_weight(*pieces):
    return pl.pallas_call(
        place_weight_kernel,
        out_shape=jax.ShapeDtypeStruct((2 * pieces[0].shape[0], KVH * HD), bf16),
        in_specs=[ANY] * 4,
        out_specs=ANY,
        scratch_shapes=[pltpu.SemaphoreType.DMA((16,))],
        compiler_params=limit(2),
        name="place_weight",
    )(*pieces)


def place_tokens_kernel(q_own, q_oth, k_own, k_oth, q_out, k_out, sems):
    core = lax.rem(lax.axis_index("seq"), 2)
    pairs = []
    for own, oth, out in ((q_own, q_oth, q_out), (k_own, k_oth, k_out)):
        width = own.shape[1]
        for source, side in ((own, core), (oth, 1 - core)):
            cols = pl.ds(pl.multiple_of(side * width, HD), width)
            pairs.append((source, out.at[:, cols]))
    for copy in run_copies(pairs, sems):
        copy.wait()


def place_tokens(q_own, q_oth, k_own, k_oth):
    return pl.pallas_call(
        place_tokens_kernel,
        out_shape=[
            jax.ShapeDtypeStruct((own.shape[0], 2 * own.shape[1]), bf16) for own in (q_own, k_own)
        ],
        in_specs=[ANY] * 4,
        out_specs=[ANY] * 2,
        scratch_shapes=[pltpu.SemaphoreType.DMA((4,))],
        compiler_params=limit(2),
        name="place_tokens",
    )(q_own, q_oth, k_own, k_oth)


def reduce_any(spiked, value_grad, core, place, row):
    n_dp, n_seq = lax.axis_size("dp"), lax.axis_size("seq")
    chip = place // 2
    part = lax.dot_general(
        spiked, value_grad, (((0,), (0,)), ((), ())), preferred_element_type=f32
    )
    steps = [("dp", 1 << b, (row >> b) & 1) for b in range(n_dp.bit_length() - 2, -1, -1)]
    chip_steps = [
        ("seq", 2 << b, (chip >> b) & 1) for b in range((n_seq // 2).bit_length() - 1)
    ]
    for axis, flip, bit in steps + chip_steps:
        half = part.shape[0] // 2
        send = lax.dynamic_slice_in_dim(part, (1 - bit) * half, half, 0).astype(bf16)
        keep = lax.dynamic_slice_in_dim(part, bit * half, half, 0)
        part = keep + swapped(send, axis, flip).astype(f32)
    owned = part.astype(bf16)
    for axis, flip, bit in chip_steps[::-1]:
        owned = ordered(bit, owned, swapped(owned, axis, flip))
    return ordered(core, owned, swapped(owned, "seq", 1), axis=1)


def after(value, *others):
    return lax.optimization_barrier((value, *others))[0]


def body(hidden_in, spike_level, value_weight, queries, key_states, spike_mask, out_grad):
    tok = hidden_in.shape[1]
    n_dp, n_seq = lax.axis_size("dp"), lax.axis_size("seq")
    place, row = lax.axis_index("seq"), lax.axis_index("dp")
    core = place % 2
    assert 0 < WINDOW - 2 * tok <= tok and 2 * tok % BLOCK == 0

    def both(value):
        return value, swapped(value, "seq", 1)

    own_keys = key_states[0]
    near_keys, far_keys = lax.optimization_barrier(
        (shifted(own_keys, 2), shifted(own_keys, 4, only=1))
    )
    weight_half = lax.dynamic_slice_in_dim(value_weight, core * HD, HD, 1)
    raw = []
    for mine in (queries[0], out_grad[0], own_keys, near_keys, far_keys):
        raw += both(mine)
    if n_dp == 2:
        weight = (weight_half, swapped(weight_half, "dp", 1))
    else:
        weight = (lax.all_gather(weight_half, "dp", axis=0, tiled=True),)

    own, near, far, top, norm = value_terms(tok, raw, both(jnp.transpose(spike_mask[0])))
    near, far = shifted(near, -2), shifted(far, -4)
    values, tail, spiked = project(tok, both(hidden_in[0]), both(spike_level), weight)

    fast = n_dp == 2 and n_seq == 16 and hidden_in.shape[2] % 256 == 0
    if fast:
        keep, send = weight_terms(tok, spiked, (own, near, far))
        values, tail = lax.optimization_barrier((values, tail, send))[:2]
        got = crossed(send, (n_seq, 4))
    window = (values, shifted(values, 2), shifted(tail, 4))
    if fast:
        keep, send = halve(keep, after(got, *window))
        window = lax.optimization_barrier((*window, send))[:3]
        got = crossed(send, (2, n_seq))
    own_k, near_k, far_k, query_mine, query_send = key_terms(tok, raw, top, norm, window)
    if fast:
        keep, send = halve(keep, after(got, own_k))
        near_k, far_k = lax.optimization_barrier((near_k, far_k, send))[:2]
        got = crossed(send, (4, 2))
    near_k, far_k = shifted(near_k, -2), shifted(far_k, -4)
    query_got = swapped(query_send, "seq", 1)
    if fast:
        keep, send = halve(keep, after(got, near_k, far_k))
        near_k, far_k = lax.optimization_barrier((near_k, far_k, send))[:2]
        got = crossed(send, (8, 8))
    key_grad = value_sum(tok, own_k, near_k, far_k).astype(bf16)
    key_mine = lax.dynamic_slice_in_dim(key_grad, core * tok, tok, 0)
    key_send = lax.dynamic_slice_in_dim(key_grad, (1 - core) * tok, tok, 0)
    query_grad, key_grad = place_tokens(
        query_mine, query_got, key_mine, swapped(key_send, "seq", 1)
    )
    if fast:
        (owned,) = halve(keep, after(got, query_grad), last=True)
        owned = join(owned, crossed(owned, (8, 8)))
        owned = join(owned, crossed(owned, (4, 2)))
        rest = crossed(owned, (2, 4))
        weight_grad = place_weight(
            owned, rest, swapped(owned, "seq", 1), swapped(rest, "seq", 1)
        )
    else:
        value_grad = value_sum(tok, own, near, far).astype(bf16)
        weight_grad = reduce_any(spiked, value_grad, core, place, row)
    return (query_grad[None], key_grad[None], weight_grad)


def solution(mesh):
    placed = (
        P("dp", "seq", None),
        P("dp", "seq"),
        P("dp", None),
        P("dp", "seq", None),
        P("dp", "seq", None),
        P("dp", "seq", None),
        P("dp", "seq", None),
    )
    return jax.shard_map(
        body,
        mesh=mesh,
        in_specs=placed,
        out_specs=(P("dp", "seq", None), P("dp", "seq", None), P("dp", None)),
        check_vma=False,
    )
```

time: 124 us -> 88 us (0.71)
  matrix products: 27.4 us -> 0 us
  other arithmetic: 18.8 us -> 0.87 us
  Pallas kernels: 0 us -> 17.1 us
  local copies, waits for them, and re-layouts: 10.7 us -> 4.41 us
  waiting for transfers between devices: 28.1 us -> 26 us
    dot_general x6 -> x0, matrix products: 18.8 us -> none  [the longest x1 5.23 us: body(): jnp.einsum('jd,thd->hjt', value_span, gated, preferred_element_type=jnp.f...]
    pallas_call x0 -> x12, Pallas kernels: none -> 17.1 us  [the longest x1 6.63 us: key_terms(): pl.pallas_call(functools.partial(key_kernel, tok), out_shape=term_shapes(...]
    ppermute x15 -> x13, waiting for transfers between devices: 20.9 us -> 6.57 us  [swapped(): lax.ppermute(value, axis, [(i, i ^ flip) for i in range(lax.axis_size(axi...]
    ppermute x8 -> x15, starting transfers between devices: 19.3 us -> 33.1 us  [the longest x8 18.2 us: shifted(): return lax.ppermute(value, 'seq', pairs)]
    ppermute x15 -> x13, starting transfers between devices: 18.2 us -> 4.77 us  [swapped(): lax.ppermute(value, axis, [(i, i ^ flip) for i in range(lax.axis_size(axi...]
    ppermute x8 -> x15, waiting for transfers between devices: 7.16 us -> 19.5 us  [the longest x7 10.6 us: crossed(): lax.ppermute(value, ('dp', 'seq'), [(i, i ^ flips[i % 2]) for i in range(...]
    convert_element_type x5 -> x1, other arithmetic: 10.4 us -> 0.02 us  [body(): key_grad = value_sum(tok, own_k, near_k, far_k).astype(bf16)]
    sub x1 -> x0, matrix products: 8.51 us -> none  [body(): expo = jnp.exp(scores - jnp.max(scores, axis=1, keepdims=True))]
  transfers between devices with their start and end apart: 23 -> 28, of which waited for: 8 -> 13; matrix products, arithmetic and copies ran while one was open for 30% -> 3% of each run, Pallas kernels for 0% -> 17%
where the time goes in v2:
time: 88 us; the launch traced here: 87.5 us
  starting transfers between devices  37.9 us (43%)
  waiting for transfers between devices  26 us (30%)
  Pallas kernels  17.1 us (19%)
  local copies, waits for them, and re-layouts  4.41 us (5%)
  between operations  1.14 us (1%)
    ppermute x8, starting transfers between devices, shifted(): return lax.ppermute(value, 'seq', pairs)  18.2 us
    ppermute x7, starting transfers between devices, crossed(): lax.ppermute(value, ('dp', 'seq'), [(i, i ^ flips[i % 2]) for i in range(...  14.9 us
    ppermute x7, waiting for transfers between devices, crossed(): lax.ppermute(value, ('dp', 'seq'), [(i, i ^ flips[i % 2]) for i in range(...  10.6 us
    ppermute x8, waiting for transfers between devices, shifted(): return lax.ppermute(value, 'seq', pairs)  8.87 us
    pallas_call x1, Pallas kernels, key_terms(): pl.pallas_call(functools.partial(key_kernel, tok), out_shape=term_shapes(...  6.63 us
    ppermute x13, waiting for transfers between devices, swapped(): lax.ppermute(value, axis, [(i, i ^ flip) for i in range(lax.axis_size(axi...  6.57 us
    ppermute x13, starting transfers between devices, swapped(): lax.ppermute(value, axis, [(i, i ^ flip) for i in range(lax.axis_size(axi...  4.77 us
    pallas_call x1, Pallas kernels, value_terms(): pl.pallas_call(functools.partial(value_kernel, tok), out_shape=term_shape...  4.05 us
  transfers between devices with their start and end apart: 28, of which 13 were waited for; matrix products, arithmetic and copies ran while one was open for 3% of the time, Pallas kernels for 17%

profile of v2, /device:TPU:0, one launch (start us, length us, event | category | flops | bytes accessed | tf_op | source)
XLA Modules:
  0.0 87.5 jit_solution(16549574210728685883)
XLA Ops:
  2.5 4.8 %collective-permute-start.3 = (bf16[192,256]{1,0:T(8,128)(2,1)}, bf16[192,256]{1,0:T(8,128)(2,1)S(1)}, u32[]{:S(2)}, u32[]{:S(2)}) collective-permute-start(bf16[192,256]{1,0:T(8,128)(2,1)} %bitcast.19), channel_id=1, source_target_pairs={{0,2},{1,3},{2,4},{3,5},{4,6},{5,7},{6,8},{7,9},{8,10},{9,11},{10,... | collective-permute-start | bytes 294920 | tf_op jit(solution)/shard_map/ppermute | solution.py:40
  8.1 1.8 %collective-permute-done.3.refs_6_ = bf16[192,256]{1,0:T(8,128)(2,1)S(1)} collective-permute-done((bf16[192,256]{1,0:T(8,128)(2,1)}, bf16[192,256]{1,0:T(8,128)(2,1)S(1)}, u32[]{:S(2)}, u32[]{:S(2)}) %collective-permute-start.3) | collective-permute-done | bytes 98336 | tf_op jit(solution)/shard_map/ppermute | solution.py:40
  9.9 1.5 %collective-permute-start.10 = (bf16[1792,128]{1,0:T(8,128)(2,1)S(1)}, bf16[1792,128]{1,0:T(8,128)(2,1)S(1)}, u32[]{:S(2)}, u32[]{:S(2)}) collective-permute-start(bf16[1792,128]{1,0:T(8,128)(2,1)S(1)} %constant_dynamic-slice_fusion.2.w_own), channel_id=1, source_target_pairs={{0,16},{16,0},{1,17},{17,1},{2,18},{18,2},{3,19},{19,3},{4,20},{20... | collective-permute-start | bytes 1376264 | tf_op jit(solution)/shard_map/ppermute | solution.py:44
  12.3 1.2 %collective-permute-done.2.refs_5_ = bf16[192,256]{1,0:T(8,128)(2,1)S(1)} collective-permute-done((bf16[192,256]{1,0:T(8,128)(2,1)}, bf16[192,256]{1,0:T(8,128)(2,1)S(1)}, u32[]{:S(2)}, u32[]{:S(2)}) %collective-permute-start.2) | collective-permute-done | bytes 98336 | tf_op jit(solution)/shard_map/ppermute | solution.py:44
  15.1 0.9 %collective-permute-done.6.refs_9_ = bf16[192,256]{1,0:T(8,128)(2,1)S(1)} collective-permute-done((bf16[192,256]{1,0:T(8,128)(2,1)S(1)}, bf16[192,256]{1,0:T(8,128)(2,1)S(1)}, u32[]{:S(2)}, u32[]{:S(2)}) %collective-permute-start.6) | collective-permute-done | bytes 98336 | tf_op jit(solution)/shard_map/ppermute | solution.py:44
  16.1 1.1 %copy-done.2 = bf16[1,192,1792]{2,1,0:T(8,128)(2,1)S(1)} copy-done((bf16[1,192,1792]{2,1,0:T(8,128)(2,1)S(1)}, bf16[1,192,1792]{2,1,0:T(8,128)(2,1)}, u32[]{:S(2)}) %copy-start.2) | copy-done | bytes 688152
  18.1 4.1 %value_terms.1 = (f32[384,128]{1,0:T(8,128)S(1)}, bf16[384,128]{1,0:T(8,128)(2,1)S(1)}, bf16[128,128]{1,0:T(8,128)(2,1)S(1)}, f32[21,128]{1,0:T(8,128)S(1)}, f32[21,128]{1,0:T(8,128)S(1)}) custom-call(bf16[192,1792]{1,0:T(8,128)(2,1)S(1)} %bitcast.12, bf16[192,1792]{1,0:T(8,128)(2,1)S(1)} %collective-permute-done.refs_1_, bf16[192,1792]{1,0:T(8,128)(2,1)S(1)} %bitcast.15, ...), custom_call_target="tpu_custom_call" | custom-call | tf_op jit(solution)/shard_map/value_terms/pallas_call | solution.py:258
  22.1 1.3 %collective-permute-start.11 = (bf16[384,128]{1,0:T(8,128)(2,1)S(1)}, bf16[384,128]{1,0:T(8,128)(2,1)S(1)}, u32[]{:S(2)}, u32[]{:S(2)}) collective-permute-start(bf16[384,128]{1,0:T(8,128)(2,1)S(1)} %get-tuple-element.49), channel_id=1, source_target_pairs={{2,0},{3,1},{4,2},{5,3},{6,4},{7,5},{8,6},{9,7},{10,8},{11,9},{12,... | collective-permute-start | bytes 294920 | tf_op jit(solution)/shard_map/ppermute | solution.py:40
  23.4 1.3 %collective-permute-start.12 = (bf16[128,128]{1,0:T(8,128)(2,1)S(1)}, bf16[128,128]{1,0:T(8,128)(2,1)S(1)}, u32[]{:S(2)}, u32[]{:S(2)}) collective-permute-start(bf16[128,128]{1,0:T(8,128)(2,1)S(1)} %get-tuple-element.50), channel_id=1, source_target_pairs={{4,0},{5,1},{6,2},{7,3},{8,4},{9,5},{10,6},{11,7},{12,8},{13,9},{1... | collective-permute-start | bytes 98312 | tf_op jit(solution)/shard_map/ppermute | solution.py:40
  26.0 3.3 %project.1 = (bf16[384,128]{1,0:T(8,128)(2,1)S(1)}, bf16[128,128]{1,0:T(8,128)(2,1)S(1)}, bf16[384,3584]{1,0:T(8,128)(2,1)S(1)}) custom-call(bf16[192,3584]{1,0:T(8,128)(2,1)S(1)} %bitcast.18, bf16[192,3584]{1,0:T(8,128)(2,1)} %collective-permute-done.8.h_oth, s32[1,192]{1,0:T(1,128)S(1)} %copy-done.8, s32[1,192]{1,0:T(1,128)S(1)} %collective-permute-done.9.l_oth, ...), custom_call_target="tpu_custom_call" | custom-call | tf_op jit(solution)/shard_map/project/pallas_call | solution.py:329
  29.3 1.9 %collective-permute-done.12.far = bf16[128,128]{1,0:T(8,128)(2,1)S(1)} collective-permute-done((bf16[128,128]{1,0:T(8,128)(2,1)S(1)}, bf16[128,128]{1,0:T(8,128)(2,1)S(1)}, u32[]{:S(2)}, u32[]{:S(2)}) %collective-permute-start.12) | collective-permute-done | bytes 32800 | tf_op jit(solution)/shard_map/ppermute | solution.py:40
  31.2 1.0 %weight_terms.1 = (f32[1792,128]{1,0:T(8,128)S(1)}, bf16[1792,128]{1,0:T(8,128)(2,1)S(1)}) custom-call(bf16[384,3584]{1,0:T(8,128)(2,1)S(1)} %get-tuple-element.47.spiked, f32[384,128]{1,0:T(8,128)S(1)} %get-tuple-element.48.own, bf16[384,128]{1,0:T(8,128)(2,1)S(1)} %collective-permute-done.11.near, bf16[128,128]{1,0:T(8,128)(2,1)S(1)} %collective-permute-done.12.far), custom_call_target="tpu_custom_call" | custom-call | tf_op jit(solution)/shard_map/weight_terms/pallas_call | solution.py:390
  32.2 1.2 %collective-permute-start.15 = (bf16[1792,128]{1,0:T(8,128)(2,1)S(1)}, bf16[1792,128]{1,0:T(8,128)(2,1)S(1)}, u32[]{:S(2)}, u32[]{:S(2)}) collective-permute-start(bf16[1792,128]{1,0:T(8,128)(2,1)S(1)} %get-tuple-element.51), channel_id=1, source_target_pairs={{0,16},{1,5},{2,18},{3,7},{4,20},{5,1},{6,22},{7,3},{8,24},{9,13},... | collective-permute-start | bytes 1376264 | tf_op jit(solution)/shard_map/ppermute | solution.py:49
  33.5 3.0 %collective-permute-start.13 = (bf16[384,128]{1,0:T(8,128)(2,1)S(1)}, bf16[384,128]{1,0:T(8,128)(2,1)S(1)}, u32[]{:S(2)}, u32[]{:S(2)}) collective-permute-start(bf16[384,128]{1,0:T(8,128)(2,1)S(1)} %get-tuple-element.57.refs_12_), channel_id=1, source_target_pairs={{0,2},{1,3},{2,4},{3,5},{4,6},{5,7},{6,8},{7,9},{8,10},{9,11},{10,... | collective-permute-start | bytes 294920 | tf_op jit(solution)/shard_map/ppermute | solution.py:40
  36.5 4.5 %collective-permute-start.14 = (bf16[128,128]{1,0:T(8,128)(2,1)S(1)}, bf16[128,128]{1,0:T(8,128)(2,1)S(1)}, u32[]{:S(2)}, u32[]{:S(2)}) collective-permute-start(bf16[128,128]{1,0:T(8,128)(2,1)S(1)} %get-tuple-element.53), channel_id=1, source_target_pairs={{0,4},{1,5},{2,6},{3,7},{4,8},{5,9},{6,10},{7,11},{8,12},{9,13},{1... | collective-permute-start | bytes 98312 | tf_op jit(solution)/shard_map/ppermute | solution.py:40
  41.0 1.6 %collective-permute-done.14.refs_14_ = bf16[128,128]{1,0:T(8,128)(2,1)S(1)} collective-permute-done((bf16[128,128]{1,0:T(8,128)(2,1)S(1)}, bf16[128,128]{1,0:T(8,128)(2,1)S(1)}, u32[]{:S(2)}, u32[]{:S(2)}) %collective-permute-start.14) | collective-permute-done | bytes 32800 | tf_op jit(solution)/shard_map/ppermute | solution.py:40
  42.7 2.5 %collective-permute-start.17 = (bf16[896,128]{1,0:T(8,128)(2,1)S(1)}, bf16[896,128]{1,0:T(8,128)(2,1)S(1)}, u32[]{:S(2)}, u32[]{:S(2)}) collective-permute-start(bf16[896,128]{1,0:T(8,128)(2,1)S(1)} %get-tuple-element.56), channel_id=1, source_target_pairs={{0,2},{1,17},{2,0},{3,19},{4,6},{5,21},{6,4},{7,23},{8,10},{9,25},... | collective-permute-start | bytes 688136 | tf_op jit(solution)/shard_map/ppermute | solution.py:49
  45.2 6.6 %key_terms.1 = (f32[384,128]{1,0:T(8,128)S(1)}, bf16[384,128]{1,0:T(8,128)(2,1)S(1)}, bf16[128,128]{1,0:T(8,128)(2,1)S(1)}, bf16[192,896]{1,0:T(8,128)(2,1)S(1)}, bf16[192,896]{1,0:T(8,128)(2,1)S(1)}) custom-call(bf16[192,1792]{1,0:T(8,128)(2,1)S(1)} %bitcast.13, bf16[192,1792]{1,0:T(8,128)(2,1)S(1)} %collective-permute-done.refs_1_, ...), custom_call_target="tpu_custom_call" | custom-call | tf_op jit(solution)/shard_map/key_terms/pallas_call | solution.py:276
  52.6 2.3 %collective-permute-start.20 = (bf16[448,128]{1,0:T(8,128)(2,1)S(1)}, bf16[448,128]{1,0:T(8,128)(2,1)S(1)}, u32[]{:S(2)}, u32[]{:S(2)}) collective-permute-start(bf16[448,128]{1,0:T(8,128)(2,1)S(1)} %get-tuple-element.67), channel_id=1, source_target_pairs={{0,4},{1,3},{2,6},{3,1},{4,0},{5,7},{6,2},{7,5},{8,12},{9,11},{10,... | collective-permute-start | bytes 344072 | tf_op jit(solution)/shard_map/ppermute | solution.py:49
  54.9 1.3 %collective-permute-start.18 = (bf16[384,128]{1,0:T(8,128)(2,1)S(1)}, bf16[384,128]{1,0:T(8,128)(2,1)S(1)}, u32[]{:S(2)}, u32[]{:S(2)}) collective-permute-start(bf16[384,128]{1,0:T(8,128)(2,1)S(1)} %get-tuple-element.68), channel_id=1, source_target_pairs={{2,0},{3,1},{4,2},{5,3},{6,4},{7,5},{8,6},{9,7},{10,8},{11,9},{12,... | collective-permute-start | bytes 294920 | tf_op jit(solution)/shard_map/ppermute | solution.py:40
  56.2 1.3 %collective-permute-start.19 = (bf16[128,128]{1,0:T(8,128)(2,1)S(1)}, bf16[128,128]{1,0:T(8,128)(2,1)S(1)}, u32[]{:S(2)}, u32[]{:S(2)}) collective-permute-start(bf16[128,128]{1,0:T(8,128)(2,1)S(1)} %get-tuple-element.69), channel_id=1, source_target_pairs={{4,0},{5,1},{6,2},{7,3},{8,4},{9,5},{10,6},{11,7},{12,8},{13,9},{1... | collective-permute-start | bytes 98312 | tf_op jit(solution)/shard_map/ppermute | solution.py:40
  58.5 3.6 %collective-permute-done.19 = bf16[128,128]{1,0:T(8,128)(2,1)S(1)} collective-permute-done((bf16[128,128]{1,0:T(8,128)(2,1)S(1)}, bf16[128,128]{1,0:T(8,128)(2,1)S(1)}, u32[]{:S(2)}, u32[]{:S(2)}) %collective-permute-start.19) | collective-permute-done | bytes 32800 | tf_op jit(solution)/shard_map/ppermute | solution.py:40
  62.2 2.6 %collective-permute-start.22 = (bf16[224,128]{1,0:T(8,128)(2,1)S(1)}, bf16[224,128]{1,0:T(8,128)(2,1)S(1)}, u32[]{:S(2)}, u32[]{:S(2)}) collective-permute-start(bf16[224,128]{1,0:T(8,128)(2,1)S(1)} %get-tuple-element.72), channel_id=1, source_target_pairs={{0,8},{1,9},{2,10},{3,11},{4,12},{5,13},{6,14},{7,15},{8,0},{9,1},... | collective-permute-start | bytes 172040 | tf_op jit(solution)/shard_map/ppermute | solution.py:49
  65.8 1.2 %collective-permute-done.21.k_oth = bf16[192,128]{1,0:T(8,128)(2,1)S(1)} collective-permute-done((bf16[192,128]{1,0:T(8,128)(2,1)S(1)}, bf16[192,128]{1,0:T(8,128)(2,1)S(1)}, u32[]{:S(2)}, u32[]{:S(2)}) %collective-permute-start.21) | collective-permute-done | bytes 49184 | tf_op jit(solution)/shard_map/ppermute | solution.py:44
  67.9 2.0 %collective-permute-start.23 = (bf16[224,128]{1,0:T(8,128)(2,1)S(1)}, bf16[224,128]{1,0:T(8,128)(2,1)S(1)}, u32[]{:S(2)}, u32[]{:S(2)}) collective-permute-start(bf16[224,128]{1,0:T(8,128)(2,1)S(1)} %halve.7.first), channel_id=1, source_target_pairs={{0,8},{1,9},{2,10},{3,11},{4,12},{5,13},{6,14},{7,15},{8,0},{9,1},... | collective-permute-start | bytes 172040 | tf_op jit(solution)/shard_map/ppermute | solution.py:49
  69.9 3.2 %collective-permute-done.23.second = bf16[224,128]{1,0:T(8,128)(2,1)S(1)} collective-permute-done((bf16[224,128]{1,0:T(8,128)(2,1)S(1)}, bf16[224,128]{1,0:T(8,128)(2,1)S(1)}, u32[]{:S(2)}, u32[]{:S(2)}) %collective-permute-start.23) | collective-permute-done | bytes 57376 | tf_op jit(solution)/shard_map/ppermute | solution.py:49
  73.1 1.4 %collective-permute-start.24 = (bf16[448,128]{1,0:T(8,128)(2,1)S(1)}, bf16[448,128]{1,0:T(8,128)(2,1)S(1)}, u32[]{:S(2)}, u32[]{:S(2)}) collective-permute-start(bf16[448,128]{1,0:T(8,128)(2,1)S(1)} %join.2.first), channel_id=1, source_target_pairs={{0,4},{1,3},{2,6},{3,1},{4,0},{5,7},{6,2},{7,5},{8,12},{9,11},{10,... | collective-permute-start | bytes 344072 | tf_op jit(solution)/shard_map/ppermute | solution.py:49
  74.6 3.4 %collective-permute-done.24.second = bf16[448,128]{1,0:T(8,128)(2,1)S(1)} collective-permute-done((bf16[448,128]{1,0:T(8,128)(2,1)S(1)}, bf16[448,128]{1,0:T(8,128)(2,1)S(1)}, u32[]{:S(2)}, u32[]{:S(2)}) %collective-permute-start.24) | collective-permute-done | bytes 114720 | tf_op jit(solution)/shard_map/ppermute | solution.py:49
  78.0 2.8 %collective-permute-start.25 = (bf16[896,128]{1,0:T(8,128)(2,1)S(1)}, bf16[896,128]{1,0:T(8,128)(2,1)S(1)}, u32[]{:S(2)}, u32[]{:S(2)}) collective-permute-start(bf16[896,128]{1,0:T(8,128)(2,1)S(1)} %join.3.own_low), channel_id=1, source_target_pairs={{0,2},{1,5},{2,0},{3,7},{4,6},{5,1},{6,4},{7,3},{8,10},{9,13},{10,... | collective-permute-start | bytes 688136 | tf_op jit(solution)/shard_map/ppermute | solution.py:49
  80.8 4.0 %collective-permute-done.25.own_high = bf16[896,128]{1,0:T(8,128)(2,1)S(1)} collective-permute-done((bf16[896,128]{1,0:T(8,128)(2,1)S(1)}, bf16[896,128]{1,0:T(8,128)(2,1)S(1)}, u32[]{:S(2)}, u32[]{:S(2)}) %collective-permute-start.25) | collective-permute-done | bytes 229408 | tf_op jit(solution)/shard_map/ppermute | solution.py:49
  84.8 1.5 %collective-permute-done.27.oth_high = bf16[896,128]{1,0:T(8,128)(2,1)S(1)} collective-permute-done((bf16[896,128]{1,0:T(8,128)(2,1)S(1)}, bf16[896,128]{1,0:T(8,128)(2,1)S(1)}, u32[]{:S(2)}, u32[]{:S(2)}) %collective-permute-start.27) | collective-permute-done | bytes 229408 | tf_op jit(solution)/shard_map/ppermute | solution.py:44
  86.3 1.0 %place_weight.1 = bf16[1792,256]{1,0:T(8,128)(2,1)} custom-call(bf16[896,128]{1,0:T(8,128)(2,1)S(1)} %join.3.own_low, bf16[896,128]{1,0:T(8,128)(2,1)S(1)} %collective-permute-done.25.own_high, bf16[896,128]{1,0:T(8,128)(2,1)S(1)} %collective-permute-done.26.oth_low, bf16[896,128]{1,0:T(8,128)(2,1)S(1)} %collective-permute-done.27.oth_high), custom_call_target="tpu_custom_call" | custom-call | tf_op jit(solution)/shard_map/place_weight/pallas_call | solution.py:466
  (62 shorter events, 11.0 us)
Async XLA Ops:
  0.6 15.4 %copy-start.1 = (bf16[1,192,1792]{2,1,0:T(8,128)(2,1)S(1)}, bf16[1,192,1792]{2,1,0:T(8,128)(2,1)}, u32[]{:S(2)}) copy-start(bf16[1,192,1792]{2,1,0:T(8,128)(2,1)} %param.10) | copy-start | bytes 2064388
  0.7 25.3 %collective-permute-start.8 = (bf16[192,3584]{1,0:T(8,128)(2,1)}, bf16[192,3584]{1,0:T(8,128)(2,1)}, u32[]{:S(2)}, u32[]{:S(2)}) collective-permute-start(bf16[192,3584]{1,0:T(8,128)(2,1)} %bitcast.17), channel_id=1, source_target_pairs={{0,1},{1,0},{2,3},{3,2},{4,5},{5,4},{6,7},{7,6},{8,9},{9,8},{10,11... | collective-permute-start | bytes 4128776 | tf_op jit(solution)/shard_map/ppermute | solution.py:44
  1.2 14.9 %collective-permute-start = (bf16[192,1792]{1,0:T(8,128)(2,1)}, bf16[192,1792]{1,0:T(8,128)(2,1)S(1)}, u32[]{:S(2)}, u32[]{:S(2)}) collective-permute-start(bf16[192,1792]{1,0:T(8,128)(2,1)} %bitcast.11), channel_id=1, source_target_pairs={{0,1},{1,0},{2,3},{3,2},{4,5},{5,4},{6,7},{7,6},{8,9},{9,8},{10,11... | collective-permute-start | bytes 2064392 | tf_op jit(solution)/shard_map/ppermute | solution.py:44
  1.3 14.8 %collective-permute-start.1 = (bf16[192,1792]{1,0:T(8,128)(2,1)}, bf16[192,1792]{1,0:T(8,128)(2,1)S(1)}, u32[]{:S(2)}, u32[]{:S(2)}) collective-permute-start(bf16[192,1792]{1,0:T(8,128)(2,1)} %bitcast.14), channel_id=1, source_target_pairs={{0,1},{1,0},{2,3},{3,2},{4,5},{5,4},{6,7},{7,6},{8,9},{9,8},{10,11... | collective-permute-start | bytes 2064392 | tf_op jit(solution)/shard_map/ppermute | solution.py:44
  2.4 5.0 %collective-permute-start.7 = (s32[14,192]{1,0:T(8,128)S(1)}, s32[14,192]{1,0:T(8,128)S(1)}, u32[]{:S(2)}, u32[]{:S(2)}) collective-permute-start(s32[14,192]{1,0:T(8,128)S(1)} %bitcast.24), channel_id=1, source_target_pairs={{0,1},{1,0},{2,3},{3,2},{4,5},{5,4},{6,7},{7,6},{8,9},{9,8},{10,11... | collective-permute-start | bytes 32264 | tf_op jit(solution)/shard_map/ppermute | solution.py:44
  2.5 7.4 %collective-permute-start.3 = (bf16[192,256]{1,0:T(8,128)(2,1)}, bf16[192,256]{1,0:T(8,128)(2,1)S(1)}, u32[]{:S(2)}, u32[]{:S(2)}) collective-permute-start(bf16[192,256]{1,0:T(8,128)(2,1)} %bitcast.19), channel_id=1, source_target_pairs={{0,2},{1,3},{2,4},{3,5},{4,6},{5,7},{6,8},{7,9},{8,10},{9,11},{10,... | collective-permute-start | bytes 294920 | tf_op jit(solution)/shard_map/ppermute | solution.py:40
  7.4 4.1 %collective-permute-start.4 = (bf16[192,256]{1,0:T(8,128)(2,1)}, bf16[192,256]{1,0:T(8,128)(2,1)S(1)}, u32[]{:S(2)}, u32[]{:S(2)}) collective-permute-start(bf16[192,256]{1,0:T(8,128)(2,1)} %bitcast.20), channel_id=1, source_target_pairs={{1,5},{3,7},{5,9},{7,11},{9,13},{11,15},{17,21},{19,23},{21,25},{2... | collective-permute-start | bytes 294920 | tf_op jit(solution)/shard_map/ppermute | solution.py:40
  8.0 16.7 %copy-start.8 = (s32[1,192]{1,0:T(1,128)S(1)}, s32[1,192]{1,0:T(1,128)}, u32[]{:S(2)}) copy-start(s32[1,192]{1,0:T(1,128)} %l_own.1) | copy-start | bytes 2308
  9.9 16.1 %collective-permute-start.10 = (bf16[1792,128]{1,0:T(8,128)(2,1)S(1)}, bf16[1792,128]{1,0:T(8,128)(2,1)S(1)}, u32[]{:S(2)}, u32[]{:S(2)}) collective-permute-start(bf16[1792,128]{1,0:T(8,128)(2,1)S(1)} %constant_dynamic-slice_fusion.2.w_own), channel_id=1, source_target_pairs={{0,16},{16,0},{1,17},{17,1},{2,18},{18,2},{3,19},{19,3},{4,20},{20... | collective-permute-start | bytes 1376264 | tf_op jit(solution)/shard_map/ppermute | solution.py:44
  11.4 2.0 %collective-permute-start.2 = (bf16[192,256]{1,0:T(8,128)(2,1)}, bf16[192,256]{1,0:T(8,128)(2,1)S(1)}, u32[]{:S(2)}, u32[]{:S(2)}) collective-permute-start(bf16[192,256]{1,0:T(8,128)(2,1)} %bitcast.21), channel_id=1, source_target_pairs={{0,1},{1,0},{2,3},{3,2},{4,5},{5,4},{6,7},{7,6},{8,9},{9,8},{10,11... | collective-permute-start | bytes 294920 | tf_op jit(solution)/shard_map/ppermute | solution.py:44
  13.5 1.3 %collective-permute-start.5 = (bf16[192,256]{1,0:T(8,128)(2,1)S(1)}, bf16[192,256]{1,0:T(8,128)(2,1)S(1)}, u32[]{:S(2)}, u32[]{:S(2)}) collective-permute-start(bf16[192,256]{1,0:T(8,128)(2,1)S(1)} %collective-permute-done.3.refs_6_), channel_id=1, source_target_pairs={{0,1},{1,0},{2,3},{3,2},{4,5},{5,4},{6,7},{7,6},{8,9},{9,8},{10,11... | collective-permute-start | bytes 294920 | tf_op jit(solution)/shard_map/ppermute | solution.py:44
  14.8 1.3 %collective-permute-start.6 = (bf16[192,256]{1,0:T(8,128)(2,1)S(1)}, bf16[192,256]{1,0:T(8,128)(2,1)S(1)}, u32[]{:S(2)}, u32[]{:S(2)}) collective-permute-start(bf16[192,256]{1,0:T(8,128)(2,1)S(1)} %collective-permute-done.4.refs_8_), channel_id=1, source_target_pairs={{0,1},{1,0},{2,3},{3,2},{4,5},{5,4},{6,7},{7,6},{8,9},{9,8},{10,11... | collective-permute-start | bytes 294920 | tf_op jit(solution)/shard_map/ppermute | solution.py:44
  22.1 9.0 %collective-permute-start.11 = (bf16[384,128]{1,0:T(8,128)(2,1)S(1)}, bf16[384,128]{1,0:T(8,128)(2,1)S(1)}, u32[]{:S(2)}, u32[]{:S(2)}) collective-permute-start(bf16[384,128]{1,0:T(8,128)(2,1)S(1)} %get-tuple-element.49), channel_id=1, source_target_pairs={{2,0},{3,1},{4,2},{5,3},{6,4},{7,5},{8,6},{9,7},{10,8},{11,9},{12,... | collective-permute-start | bytes 294920 | tf_op jit(solution)/shard_map/ppermute | solution.py:40
  23.4 7.7 %collective-permute-start.12 = (bf16[128,128]{1,0:T(8,128)(2,1)S(1)}, bf16[128,128]{1,0:T(8,128)(2,1)S(1)}, u32[]{:S(2)}, u32[]{:S(2)}) collective-permute-start(bf16[128,128]{1,0:T(8,128)(2,1)S(1)} %get-tuple-element.50), channel_id=1, source_target_pairs={{4,0},{5,1},{6,2},{7,3},{8,4},{9,5},{10,6},{11,7},{12,8},{13,9},{1... | collective-permute-start | bytes 98312 | tf_op jit(solution)/shard_map/ppermute | solution.py:40
  24.8 1.2 %collective-permute-start.9 = (s32[1,192]{1,0:T(1,128)S(1)}, s32[1,192]{1,0:T(1,128)S(1)}, u32[]{:S(2)}, u32[]{:S(2)}) collective-permute-start(s32[1,192]{1,0:T(1,128)S(1)} %copy-done.8), channel_id=1, source_target_pairs={{0,1},{1,0},{2,3},{3,2},{4,5},{5,4},{6,7},{7,6},{8,9},{9,8},{10,11... | collective-permute-start | bytes 2312 | tf_op jit(solution)/shard_map/ppermute | solution.py:44
  32.2 13.0 %copy-start.3 = (bf16[1,192,1792]{2,1,0:T(8,128)(2,1)S(1)}, bf16[1,192,1792]{2,1,0:T(8,128)(2,1)}, u32[]{:S(2)}) copy-start(bf16[1,192,1792]{2,1,0:T(8,128)(2,1)} %param.13) | copy-start | bytes 2064388
  32.2 13.0 %copy-start.6 = (bf16[1,192,256]{2,1,0:T(8,128)(2,1)S(1)}, bf16[1,192,256]{2,1,0:T(8,128)(2,1)}, u32[]{:S(2)}) copy-start(bf16[1,192,256]{2,1,0:T(8,128)(2,1)} %param.11) | copy-start | bytes 294916
  32.2 10.4 %collective-permute-start.15 = (bf16[1792,128]{1,0:T(8,128)(2,1)S(1)}, bf16[1792,128]{1,0:T(8,128)(2,1)S(1)}, u32[]{:S(2)}, u32[]{:S(2)}) collective-permute-start(bf16[1792,128]{1,0:T(8,128)(2,1)S(1)} %get-tuple-element.51), channel_id=1, source_target_pairs={{0,16},{1,5},{2,18},{3,7},{4,20},{5,1},{6,22},{7,3},{8,24},{9,13},... | collective-permute-start | bytes 1376264 | tf_op jit(solution)/shard_map/ppermute | solution.py:49
  33.5 9.1 %collective-permute-start.13 = (bf16[384,128]{1,0:T(8,128)(2,1)S(1)}, bf16[384,128]{1,0:T(8,128)(2,1)S(1)}, u32[]{:S(2)}, u32[]{:S(2)}) collective-permute-start(bf16[384,128]{1,0:T(8,128)(2,1)S(1)} %get-tuple-element.57.refs_12_), channel_id=1, source_target_pairs={{0,2},{1,3},{2,4},{3,5},{4,6},{5,7},{6,8},{7,9},{8,10},{9,11},{10,... | collective-permute-start | bytes 294920 | tf_op jit(solution)/shard_map/ppermute | solution.py:40
  36.5 6.1 %collective-permute-start.14 = (bf16[128,128]{1,0:T(8,128)(2,1)S(1)}, bf16[128,128]{1,0:T(8,128)(2,1)S(1)}, u32[]{:S(2)}, u32[]{:S(2)}) collective-permute-start(bf16[128,128]{1,0:T(8,128)(2,1)S(1)} %get-tuple-element.53), channel_id=1, source_target_pairs={{0,4},{1,5},{2,6},{3,7},{4,8},{5,9},{6,10},{7,11},{8,12},{9,13},{1... | collective-permute-start | bytes 98312 | tf_op jit(solution)/shard_map/ppermute | solution.py:40
  42.7 9.2 %collective-permute-start.17 = (bf16[896,128]{1,0:T(8,128)(2,1)S(1)}, bf16[896,128]{1,0:T(8,128)(2,1)S(1)}, u32[]{:S(2)}, u32[]{:S(2)}) collective-permute-start(bf16[896,128]{1,0:T(8,128)(2,1)S(1)} %get-tuple-element.56), channel_id=1, source_target_pairs={{0,2},{1,17},{2,0},{3,19},{4,6},{5,21},{6,4},{7,23},{8,10},{9,25},... | collective-permute-start | bytes 688136 | tf_op jit(solution)/shard_map/ppermute | solution.py:49
  52.6 9.5 %collective-permute-start.20 = (bf16[448,128]{1,0:T(8,128)(2,1)S(1)}, bf16[448,128]{1,0:T(8,128)(2,1)S(1)}, u32[]{:S(2)}, u32[]{:S(2)}) collective-permute-start(bf16[448,128]{1,0:T(8,128)(2,1)S(1)} %get-tuple-element.67), channel_id=1, source_target_pairs={{0,4},{1,3},{2,6},{3,1},{4,0},{5,7},{6,2},{7,5},{8,12},{9,11},{10,... | collective-permute-start | bytes 344072 | tf_op jit(solution)/shard_map/ppermute | solution.py:49
  54.9 7.2 %collective-permute-start.18 = (bf16[384,128]{1,0:T(8,128)(2,1)S(1)}, bf16[384,128]{1,0:T(8,128)(2,1)S(1)}, u32[]{:S(2)}, u32[]{:S(2)}) collective-permute-start(bf16[384,128]{1,0:T(8,128)(2,1)S(1)} %get-tuple-element.68), channel_id=1, source_target_pairs={{2,0},{3,1},{4,2},{5,3},{6,4},{7,5},{8,6},{9,7},{10,8},{11,9},{12,... | collective-permute-start | bytes 294920 | tf_op jit(solution)/shard_map/ppermute | solution.py:40
  56.2 5.9 %collective-permute-start.19 = (bf16[128,128]{1,0:T(8,128)(2,1)S(1)}, bf16[128,128]{1,0:T(8,128)(2,1)S(1)}, u32[]{:S(2)}, u32[]{:S(2)}) collective-permute-start(bf16[128,128]{1,0:T(8,128)(2,1)S(1)} %get-tuple-element.69), channel_id=1, source_target_pairs={{4,0},{5,1},{6,2},{7,3},{8,4},{9,5},{10,6},{11,7},{12,8},{13,9},{1... | collective-permute-start | bytes 98312 | tf_op jit(solution)/shard_map/ppermute | solution.py:40
  58.4 7.3 %collective-permute-start.16 = (bf16[192,896]{1,0:T(8,128)(2,1)}, bf16[192,896]{1,0:T(8,128)(2,1)S(1)}, u32[]{:S(2)}, u32[]{:S(2)}) collective-permute-start(bf16[192,896]{1,0:T(8,128)(2,1)} %copy-done.9), channel_id=1, source_target_pairs={{0,1},{1,0},{2,3},{3,2},{4,5},{5,4},{6,7},{7,6},{8,9},{9,8},{10,11... | collective-permute-start | bytes 1032200 | tf_op jit(solution)/shard_map/ppermute | solution.py:44
  62.2 5.7 %collective-permute-start.22 = (bf16[224,128]{1,0:T(8,128)(2,1)S(1)}, bf16[224,128]{1,0:T(8,128)(2,1)S(1)}, u32[]{:S(2)}, u32[]{:S(2)}) collective-permute-start(bf16[224,128]{1,0:T(8,128)(2,1)S(1)} %get-tuple-element.72), channel_id=1, source_target_pairs={{0,8},{1,9},{2,10},{3,11},{4,12},{5,13},{6,14},{7,15},{8,0},{9,1},... | collective-permute-start | bytes 172040 | tf_op jit(solution)/shard_map/ppermute | solution.py:49
  65.7 1.3 %collective-permute-start.21 = (bf16[192,128]{1,0:T(8,128)(2,1)S(1)}, bf16[192,128]{1,0:T(8,128)(2,1)S(1)}, u32[]{:S(2)}, u32[]{:S(2)}) collective-permute-start(bf16[192,128]{1,0:T(8,128)(2,1)S(1)} %get-tuple-element.79), channel_id=1, source_target_pairs={{0,1},{1,0},{2,3},{3,2},{4,5},{5,4},{6,7},{7,6},{8,9},{9,8},{10,11... | collective-permute-start | bytes 147464 | tf_op jit(solution)/shard_map/ppermute | solution.py:44
  67.9 5.2 %collective-permute-start.23 = (bf16[224,128]{1,0:T(8,128)(2,1)S(1)}, bf16[224,128]{1,0:T(8,128)(2,1)S(1)}, u32[]{:S(2)}, u32[]{:S(2)}) collective-permute-start(bf16[224,128]{1,0:T(8,128)(2,1)S(1)} %halve.7.first), channel_id=1, source_target_pairs={{0,8},{1,9},{2,10},{3,11},{4,12},{5,13},{6,14},{7,15},{8,0},{9,1},... | collective-permute-start | bytes 172040 | tf_op jit(solution)/shard_map/ppermute | solution.py:49
  73.1 4.9 %collective-permute-start.24 = (bf16[448,128]{1,0:T(8,128)(2,1)S(1)}, bf16[448,128]{1,0:T(8,128)(2,1)S(1)}, u32[]{:S(2)}, u32[]{:S(2)}) collective-permute-start(bf16[448,128]{1,0:T(8,128)(2,1)S(1)} %join.2.first), channel_id=1, source_target_pairs={{0,4},{1,3},{2,6},{3,1},{4,0},{5,7},{6,2},{7,5},{8,12},{9,11},{10,... | collective-permute-start | bytes 344072 | tf_op jit(solution)/shard_map/ppermute | solution.py:49
  78.0 6.8 %collective-permute-start.25 = (bf16[896,128]{1,0:T(8,128)(2,1)S(1)}, bf16[896,128]{1,0:T(8,128)(2,1)S(1)}, u32[]{:S(2)}, u32[]{:S(2)}) collective-permute-start(bf16[896,128]{1,0:T(8,128)(2,1)S(1)} %join.3.own_low), channel_id=1, source_target_pairs={{0,2},{1,5},{2,0},{3,7},{4,6},{5,1},{6,4},{7,3},{8,10},{9,13},{10,... | collective-permute-start | bytes 688136 | tf_op jit(solution)/shard_map/ppermute | solution.py:49
  80.8 4.0 %collective-permute-start.26 = (bf16[896,128]{1,0:T(8,128)(2,1)S(1)}, bf16[896,128]{1,0:T(8,128)(2,1)S(1)}, u32[]{:S(2)}, u32[]{:S(2)}) collective-permute-start(bf16[896,128]{1,0:T(8,128)(2,1)S(1)} %join.3.own_low), channel_id=1, source_target_pairs={{0,1},{1,0},{2,3},{3,2},{4,5},{5,4},{6,7},{7,6},{8,9},{9,8},{10,11... | collective-permute-start | bytes 688136 | tf_op jit(solution)/shard_map/ppermute | solution.py:44
  84.8 1.5 %collective-permute-start.27 = (bf16[896,128]{1,0:T(8,128)(2,1)S(1)}, bf16[896,128]{1,0:T(8,128)(2,1)S(1)}, u32[]{:S(2)}, u32[]{:S(2)}) collective-permute-start(bf16[896,128]{1,0:T(8,128)(2,1)S(1)} %collective-permute-done.25.own_high), channel_id=1, source_target_pairs={{0,1},{1,0},{2,3},{3,2},{4,5},{5,4},{6,7},{7,6},{8,9},{9,8},{10,11... | collective-permute-start | bytes 688136 | tf_op jit(solution)/shard_map/ppermute | solution.py:44
  (6 other events, 18.8 us)

commit v3 on v2

--- a/solution.py
+++ b/solution.py
@@ -31,13 +31,9 @@
     return pltpu.CompilerParams(vmem_limit_bytes=mib * 1024 * 1024)
 
 
-def shifted(value, steps, only=None):
+def shifted(value, steps):
     count = lax.axis_size("seq")
-    first, last = (max(0, -steps), min(count, count - steps))
-    pairs = [(source, source + steps) for source in range(first, last)]
-    if only is not None:
-        pairs = [pair for pair in pairs if pair[0] % 2 == only]
-    return lax.ppermute(value, "seq", pairs)
+    return lax.ppermute(value, "seq", [(i, (i + steps) % count) for i in range(count)])
 
 
 def swapped(value, axis, flip):
@@ -64,39 +60,88 @@
     return copies
 
 
-def own_first(core, tok, own, oth, dst, begin=0):
-    return [
-        (own, dst.at[pl.ds(begin + core * tok, tok)]),
-        (oth, dst.at[pl.ds(begin + (1 - core) * tok, tok)]),
-    ]
-
-
-def head_pairs(core, tok, raw, q_buf, g_buf, k_buf):
-    q_own, q_oth, g_own, g_oth, k_own, k_oth, p_own, p_oth = raw
-    wide = pl.ds(pl.multiple_of(core * GROUP * HD, HD), GROUP * HD)
-    slim = pl.ds(pl.multiple_of(core * HD, HD), HD)
+def split_kernel(
+    tok, q_ref, g_ref, m_ref, l_ref, q_own, q_send, g_own, g_send, marks, m_buf, l_buf, sems
+):
+    core = lax.rem(lax.axis_index("seq"), 2)
+    wide = GROUP * HD
+    pairs = [(m_ref, m_buf), (l_ref, l_buf)]
+    for source, own, send in ((q_ref, q_own, q_send), (g_ref, g_own, g_send)):
+        for target, side in ((own, core), (send, 1 - core)):
+            pairs.append((source.at[:, pl.ds(pl.multiple_of(side * wide, HD), wide)], target))
+    copies = run_copies(pairs, sems)
+    for copy in copies:
+        copy.wait()
+    for head in range(QH):
+        marks[head : head + 1, :] = m_buf[head]
+    marks[QH : QH + 1, :] = l_buf[...]
+
+
+def in_hbm(value):
+    return pltpu.with_memory_space_constraint(value, pltpu.HBM)
+
+
+def split(tok, query, grad, spikes, level):
+    half = jax.ShapeDtypeStruct((tok, GROUP * HD), bf16)
+    return pl.pallas_call(
+        functools.partial(split_kernel, tok),
+        out_shape=[half] * 4 + [jax.ShapeDtypeStruct((QH + 1, tok), jnp.int32)],
+        in_specs=[ANY] * 4,
+        out_specs=[VMEM] * 5,
+        scratch_shapes=[
+            pltpu.VMEM((QH, 1, tok), jnp.int32),
+            pltpu.VMEM((1, tok), jnp.int32),
+            pltpu.SemaphoreType.DMA((6,)),
+        ],
+        compiler_params=limit(4),
+        name="split",
+    )(in_hbm(query), in_hbm(grad), in_hbm(spikes), in_hbm(level))
+
+
+def pack_kernel(tok, own, near, far, mine, send, sems):
+    core = lax.rem(lax.axis_index("seq"), 2)
     rest = WINDOW - 2 * tok
-    pairs = own_first(core, tok, q_own.at[:, wide], q_oth.at[:, wide], q_buf)
-    pairs += own_first(core, tok, g_own.at[:, wide], g_oth.at[:, wide], g_buf)
-    pairs += own_first(core, tok, k_own.at[:, slim], k_oth.at[:, slim], k_buf, WINDOW)
-    pairs += own_first(core, tok, p_own.at[:, slim], p_oth.at[:, slim], k_buf, rest)
-    return pairs
-
-
-def tail_copy(core, tok, far_own, far_oth, k_buf, sem):
-    slim = pl.ds(pl.multiple_of(core * HD, HD), HD)
+    sides = ((mine, core), (send, 1 - core))
+    pairs = []
+    for target, side in sides:
+        cols = pl.ds(pl.multiple_of(side * HD, HD), HD)
+        pairs.append((own.at[:, cols], target.at[pl.ds(rest + tok, tok)]))
+    copies = run_copies(pairs, sems)
+    for target, side in sides:
+        cols = pl.ds(pl.multiple_of(side * HD, HD), HD)
+        target[:rest, :] = far[tok - rest :, cols]
+        target[rest : rest + tok, :] = near[:, cols]
+    for copy in copies:
+        copy.wait()
+
+
+def pack(tok, own, near, far):
+    half = jax.ShapeDtypeStruct((WINDOW, HD), bf16)
+    return pl.pallas_call(
+        functools.partial(pack_kernel, tok),
+        out_shape=[half] * 2,
+        in_specs=[ANY] + [VMEM] * 2,
+        out_specs=[VMEM] * 2,
+        scratch_shapes=[pltpu.SemaphoreType.DMA((2,))],
+        compiler_params=limit(4),
+        name="pack",
+    )(in_hbm(own), near, far)
+
+
+def lay_out(core, tok, raw, q_buf, g_buf, k_buf):
+    q_own, q_oth, g_own, g_oth, k_own, k_oth = raw
     rest = WINDOW - 2 * tok
-    rows = pl.ds(tok - rest, rest)
-
-    @pl.when(core == 1)
-    def _():
-        pltpu.make_async_copy(far_own.at[rows, slim], k_buf.at[pl.ds(0, rest)], sem).start()
-
-    @pl.when(core == 0)
-    def _():
-        pltpu.make_async_copy(far_oth.at[rows, slim], k_buf.at[pl.ds(0, rest)], sem).start()
-
-    return pltpu.make_async_copy(far_own.at[rows, slim], k_buf.at[pl.ds(0, rest)], sem)
+    for own, oth, buf, first, begin in (
+        (k_own, k_oth, k_buf, rest, rest),
+        (k_own, k_oth, k_buf, rest + tok, WINDOW),
+        (q_own, q_oth, q_buf, 0, 0),
+        (g_own, g_oth, g_buf, 0, 0),
+    ):
+        buf[pl.ds(pl.multiple_of(begin + core * tok, 64), tok), :] = own[first : first + tok, :]
+        buf[pl.ds(pl.multiple_of(begin + (1 - core) * tok, 64), tok), :] = oth[
+            first : first + tok, :
+        ]
+    k_buf[:rest, :] = jnp.where(core == 1, k_own[:rest, :], k_oth[:rest, :])
 
 
 def head_masks(core, own, oth):
@@ -150,17 +195,14 @@
 
 
 def value_kernel(tok, *refs):
-    raw, far_own, far_oth, m_own, m_oth = refs[:8], *refs[8:12]
-    own_out, near_out, far_out, top_out, norm_out = refs[12:17]
-    q_buf, g_buf, k_buf, p_buf, acc, sems = refs[17:]
+    raw, m_own, m_oth = refs[:6], *refs[6:8]
+    own_out, near_out, far_out, top_out, norm_out = refs[8:13]
+    q_buf, g_buf, k_buf, p_buf, acc = refs[13:]
     place = lax.axis_index("seq")
     core, chip = lax.rem(place, 2), lax.div(place, 2)
-    copies = run_copies(head_pairs(core, tok, raw, q_buf, g_buf, k_buf), sems)
-    copies.append(tail_copy(core, tok, far_own, far_oth, k_buf, sems.at[8]))
-    spikes = head_masks(core, m_own[...], m_oth[...])
+    lay_out(core, tok, raw, q_buf, g_buf, k_buf)
+    spikes = head_masks(core, m_own[:QH, :], m_oth[:QH, :])
     acc[...] = jnp.zeros_like(acc)
-    for copy in copies:
-        copy.wait()
     for block in range(2 * tok // BLOCK):
         bias = biases(chip, tok, block)
         begin = block * BLOCK
@@ -186,24 +228,18 @@
 
 
 def key_kernel(tok, *refs):
-    raw, far_own, far_oth = refs[:8], refs[8], refs[9]
-    top_in, norm_in, v_own, v_near, v_far = refs[10:15]
-    own_out, near_out, far_out, mine_out, send_out = refs[15:20]
-    q_buf, g_buf, k_buf, v_buf, d_buf, acc, r_buf, sems, out_sems = refs[20:]
+    raw = refs[:6]
+    top_in, norm_in, v_own, v_near, v_far = refs[6:11]
+    own_out, near_out, far_out, mine_out, send_out = refs[11:16]
+    q_buf, g_buf, k_buf, v_buf, d_buf, acc, r_buf = refs[16:]
     place = lax.axis_index("seq")
     core, chip = lax.rem(place, 2), lax.div(place, 2)
     rest = WINDOW - 2 * tok
-    pairs = head_pairs(core, tok, raw, q_buf, g_buf, k_buf)
-    pairs += [
-        (v_far, v_buf.at[pl.ds(0, rest)]),
-        (v_near, v_buf.at[pl.ds(rest, 2 * tok)]),
-        (v_own, v_buf.at[pl.ds(WINDOW, 2 * tok)]),
-    ]
-    copies = run_copies(pairs, sems)
-    copies.append(tail_copy(core, tok, far_own, far_oth, k_buf, sems.at[len(pairs)]))
+    lay_out(core, tok, raw, q_buf, g_buf, k_buf)
+    v_buf[:rest, :] = v_far[...]
+    v_buf[rest:WINDOW, :] = v_near[...]
+    v_buf[WINDOW:, :] = v_own[...]
     acc[...] = jnp.zeros_like(acc)
-    for copy in copies:
-        copy.wait()
     for block in range(2 * tok // BLOCK):
         bias = biases(chip, tok, block)
         begin = block * BLOCK
@@ -226,15 +262,11 @@
         for head in range(GROUP):
             cols = slice(head * HD, (head + 1) * HD)
             r_buf[rows, cols] = query_part[head * BLOCK : (head + 1) * BLOCK].astype(bf16)
-    mine = pltpu.make_async_copy(r_buf.at[pl.ds(core * tok, tok)], mine_out, out_sems.at[0])
-    send = pltpu.make_async_copy(r_buf.at[pl.ds((1 - core) * tok, tok)], send_out, out_sems.at[1])
-    mine.start()
-    send.start()
+    mine_out[...] = r_buf[pl.ds(pl.multiple_of(core * tok, 64), tok), :]
+    send_out[...] = r_buf[pl.ds(pl.multiple_of((1 - core) * tok, 64), tok), :]
     far_out[...] = (acc[:rest, :] * score_scale).astype(bf16)
     near_out[...] = (acc[rest:WINDOW, :] * score_scale).astype(bf16)
     own_out[...] = acc[WINDOW:, :] * score_scale
-    mine.wait()
-    send.wait()
 
 
 def head_scratch(tok):
@@ -258,13 +290,12 @@
     return pl.pallas_call(
         functools.partial(value_kernel, tok),
         out_shape=term_shapes(tok) + [stats, stats],
-        in_specs=[ANY] * 10 + [VMEM] * 2,
+        in_specs=[VMEM] * 8,
         out_specs=[VMEM] * 5,
         scratch_shapes=head_scratch(tok)
         + [
             pltpu.VMEM((SPAN, GROUP * HD), bf16),
             pltpu.VMEM((WINDOW + 2 * tok, HD), f32),
-            pltpu.SemaphoreType.DMA((9,)),
         ],
         compiler_params=limit(12),
         name="value_terms",
@@ -276,20 +307,38 @@
     return pl.pallas_call(
         functools.partial(key_kernel, tok),
         out_shape=term_shapes(tok) + [half, half],
-        in_specs=[ANY] * 10 + [VMEM] * 2 + [ANY] * 3,
-        out_specs=[VMEM] * 3 + [ANY] * 2,
+        in_specs=[VMEM] * 11,
+        out_specs=[VMEM] * 5,
         scratch_shapes=head_scratch(tok)
         + [
             pltpu.VMEM((WINDOW + 2 * tok, HD), bf16),
             pltpu.VMEM((SPAN, GROUP * HD), bf16),
             pltpu.VMEM((WINDOW + 2 * tok, HD), f32),
             pltpu.VMEM((2 * tok, GROUP * HD), bf16),
-            pltpu.SemaphoreType.DMA((12,)),
-            pltpu.SemaphoreType.DMA((2,)),
         ],
         compiler_params=limit(14),
         name="key_terms",
     )(*raw, top, norm, *values)
+
+
+def sum_keys_kernel(tok, own, near, far, mine, send, buf):
+    core = lax.rem(lax.axis_index("seq"), 2)
+    buf[...] = value_sum(tok, own[...], near[...], far[...])
+    mine[...] = buf[pl.ds(pl.multiple_of(core * tok, 64), tok), :].astype(bf16)
+    send[...] = buf[pl.ds(pl.multiple_of((1 - core) * tok, 64), tok), :].astype(bf16)
+
+
+def sum_keys(tok, own, near, far):
+    half = jax.ShapeDtypeStruct((tok, HD), bf16)
+    return pl.pallas_call(
+        functools.partial(sum_keys_kernel, tok),
+        out_shape=[half, half],
+        in_specs=[VMEM] * 3,
+        out_specs=[VMEM] * 2,
+        scratch_shapes=[pltpu.VMEM((2 * tok, HD), f32)],
+        compiler_params=limit(4),
+        name="sum_keys",
+    )(own, near, far)
 
 
 def column(row):
@@ -313,7 +362,7 @@
         pairs = [(w_own, w_buf)]
     copies = run_copies(pairs, sems)
     for source, level, place in ((h_own, l_own, core), (h_oth, l_oth, 1 - core)):
-        factor = column(level[...].astype(f32) / LEVELS)
+        factor = column(level[QH : QH + 1, :].astype(f32) / LEVELS)
         rows = pl.ds(pl.multiple_of(place * tok, 64), tok)
         spiked[rows, :] = (source[...].astype(f32) * factor).astype(bf16)
     for copy in copies:
@@ -355,9 +404,7 @@
     for part in range(4):
         term = dot_tn(spiked[:, part * 4 * rows : (part + 1) * 4 * rows], value_grad)
         for piece in range(4):
-            index = part * 4 + piece
-            other = (index & 3) | ((index & 4) << 1) | ((index & 8) >> 1)
-            at = jnp.where(core == 0, index, other) ^ mine
+            at = (part * 4 + piece) ^ mine
             w_buf[pl.ds(pl.multiple_of(at * rows, 16), rows), :] = term[
                 piece * rows : (piece + 1) * rows
             ]
@@ -371,13 +418,7 @@
 
 
 def block_code(core):
-    y, near, far = chip_bits()
-    row = lax.axis_index("dp")
-    return jnp.where(
-        core == 0,
-        row * 8 + y * 4 + near * 2 + far,
-        near * 8 + row * 4 + y * 2 + far,
-    )
+    return lax.axis_index("dp") * 8 + chip_code(core)
 
 
 def chip_code(core):
@@ -536,56 +577,59 @@
         return value, swapped(value, "seq", 1)
 
     own_keys = key_states[0]
-    near_keys, far_keys = lax.optimization_barrier(
-        (shifted(own_keys, 2), shifted(own_keys, 4, only=1))
-    )
+    near_keys, far_keys = lax.optimization_barrier((shifted(own_keys, 2), shifted(own_keys, 4)))
+    query_own, query_out, grad_own, grad_out, marks = split(
+        tok, queries[0], out_grad[0], jnp.transpose(spike_mask, (2, 0, 1)), spike_level
+    )
+    near_keys, far_keys, _ = lax.optimization_barrier((near_keys, far_keys, query_out))
+    keys, keys_out = pack(tok, own_keys, near_keys, far_keys)
     weight_half = lax.dynamic_slice_in_dim(value_weight, core * HD, HD, 1)
-    raw = []
-    for mine in (queries[0], out_grad[0], own_keys, near_keys, far_keys):
-        raw += both(mine)
+    raw = [query_own, swapped(query_out, "seq", 1), grad_own, swapped(grad_out, "seq", 1)]
+    raw += [keys, swapped(keys_out, "seq", 1)]
+    marks = both(marks)
     if n_dp == 2:
         weight = (weight_half, swapped(weight_half, "dp", 1))
     else:
         weight = (lax.all_gather(weight_half, "dp", axis=0, tiled=True),)
 
-    own, near, far, top, norm = value_terms(tok, raw, both(jnp.transpose(spike_mask[0])))
+    own, near, far, top, norm = value_terms(tok, raw, marks)
     near, far = shifted(near, -2), shifted(far, -4)
-    values, tail, spiked = project(tok, both(hidden_in[0]), both(spike_level), weight)
+    values, tail, spiked = project(tok, both(after(hidden_in[0], keys_out)), marks, weight)
 
     fast = n_dp == 2 and n_seq == 16 and hidden_in.shape[2] % 256 == 0
     if fast:
         keep, send = weight_terms(tok, spiked, (own, near, far))
         values, tail = lax.optimization_barrier((values, tail, send))[:2]
-        got = crossed(send, (n_seq, 4))
+        got = crossed(send, (n_seq, n_seq))
     window = (values, shifted(values, 2), shifted(tail, 4))
-    if fast:
-        keep, send = halve(keep, after(got, *window))
-        window = lax.optimization_barrier((*window, send))[:3]
-        got = crossed(send, (2, n_seq))
     own_k, near_k, far_k, query_mine, query_send = key_terms(tok, raw, top, norm, window)
     if fast:
         keep, send = halve(keep, after(got, own_k))
         near_k, far_k = lax.optimization_barrier((near_k, far_k, send))[:2]
+        got = crossed(send, (2, 4))
+    near_k, far_k = shifted(near_k, -2), shifted(far_k, -4)
+    if fast:
+        keep, send = halve(keep, got)
+        query_send = after(query_send, send)
         got = crossed(send, (4, 2))
-    near_k, far_k = shifted(near_k, -2), shifted(far_k, -4)
     query_got = swapped(query_send, "seq", 1)
     if fast:
-        keep, send = halve(keep, after(got, near_k, far_k))
+        keep, send = halve(keep, after(got, near_k, far_k, query_got))
         near_k, far_k = lax.optimization_barrier((near_k, far_k, send))[:2]
         got = crossed(send, (8, 8))
-    key_grad = value_sum(tok, own_k, near_k, far_k).astype(bf16)
-    key_mine = lax.dynamic_slice_in_dim(key_grad, core * tok, tok, 0)
-    key_send = lax.dynamic_slice_in_dim(key_grad, (1 - core) * tok, tok, 0)
-    query_grad, key_grad = place_tokens(
-        query_mine, query_got, key_mine, swapped(key_send, "seq", 1)
-    )
+    key_mine, key_send = sum_keys(tok, own_k, near_k, far_k)
+    key_got = swapped(key_send, "seq", 1)
     if fast:
-        (owned,) = halve(keep, after(got, query_grad), last=True)
-        owned = join(owned, crossed(owned, (8, 8)))
+        (owned,) = halve(keep, after(got, key_got), last=True)
+        key_got = after(key_got, owned)
+        got = crossed(owned, (8, 8))
+    query_grad, key_grad = place_tokens(query_mine, query_got, key_mine, key_got)
+    if fast:
+        owned = join(owned, after(got, query_grad))
         owned = join(owned, crossed(owned, (4, 2)))
-        rest = crossed(owned, (2, 4))
+        other = crossed(owned, (2, 4))
         weight_grad = place_weight(
-            owned, rest, swapped(owned, "seq", 1), swapped(rest, "seq", 1)
+            owned, other, swapped(owned, "seq", 1), swapped(other, "seq", 1)
         )
     else:
         value_grad = value_sum(tok, own, near, far).astype(bf16)

time: 88 us -> 83.8 us (0.952)
  starting transfers between devices: 37.9 us -> 21.5 us
  waiting for transfers between devices: 26 us -> 41.5 us
  local copies, waits for them, and re-layouts: 4.41 us -> 1.43 us
  Pallas kernels: 17.1 us -> 18.2 us
    ppermute x7, waiting for transfers between devices: 10.6 us -> 22.9 us  [crossed(): lax.ppermute(value, ('dp', 'seq'), [(i, i ^ flips[i % 2]) for i in range(...]
    ppermute x7, starting transfers between devices: 14.9 us -> 5.07 us  [crossed(): lax.ppermute(value, ('dp', 'seq'), [(i, i ^ flips[i % 2]) for i in range(...]
    ppermute x8, starting transfers between devices: 18.2 us -> 13.7 us  [shifted(): lax.ppermute(value, 'seq', [(i, (i + steps) % count) for i in range(count)])]
    ppermute x8, waiting for transfers between devices: 8.87 us -> 12.7 us  [shifted(): lax.ppermute(value, 'seq', [(i, (i + steps) % count) for i in range(count)])]
    pallas_call x0 -> x3, Pallas kernels: none -> 2.26 us  [the longest x1 1.38 us: split(): pl.pallas_call(functools.partial(split_kernel, tok), out_shape=[half] * 4...]
    ppermute x13 -> x10, starting transfers between devices: 4.77 us -> 2.67 us  [swapped(): lax.ppermute(value, axis, [(i, i ^ flip) for i in range(lax.axis_size(axi...]
    unnamed x21 -> x8, local copies, waits for them, and re-layouts: 3.44 us -> 1.39 us
    slice x1 -> x0, local copies, waits for them, and re-layouts: 0.92 us -> none  [value_sum(): early = own[:4 * tok - WINDOW]]
  transfers between devices with their start and end apart: 28 -> 25, of which waited for: 13 -> 13; matrix products, arithmetic and copies ran while one was open for 3% -> 0% of each run, Pallas kernels for 17% -> 18%
where the time goes in v3:
time: 83.8 us; the launch traced here: 83.6 us
  waiting for transfers between devices  41.5 us (50%)
  starting transfers between devices  21.5 us (26%)
  Pallas kernels  18.2 us (22%)
  local copies, waits for them, and re-layouts  1.43 us (2%)
  between operations  0.98 us (1%)
    ppermute x7, waiting for transfers between devices, crossed(): lax.ppermute(value, ('dp', 'seq'), [(i, i ^ flips[i % 2]) for i in range(...  22.9 us
    ppermute x8, starting transfers between devices, shifted(): lax.ppermute(value, 'seq', [(i, (i + steps) % count) for i in range(count)])  13.7 us
    ppermute x8, waiting for transfers between devices, shifted(): lax.ppermute(value, 'seq', [(i, (i + steps) % count) for i in range(count)])  12.7 us
    ppermute x10, waiting for transfers between devices, swapped(): lax.ppermute(value, axis, [(i, i ^ flip) for i in range(lax.axis_size(axi...  5.84 us
    pallas_call x1, Pallas kernels, key_terms(): pl.pallas_call(functools.partial(key_kernel, tok), out_shape=term_shapes(...  5.73 us
    ppermute x7, starting transfers between devices, crossed(): lax.ppermute(value, ('dp', 'seq'), [(i, i ^ flips[i % 2]) for i in range(...  5.07 us
    pallas_call x1, Pallas kernels, value_terms(): pl.pallas_call(functools.partial(value_kernel, tok), out_shape=term_shape...  3.81 us
    pallas_call x1, Pallas kernels, project(): pl.pallas_call(functools.partial(project_kernel, tok, split), out_shape=[...  3.29 us
  transfers between devices with their start and end apart: 25, of which 13 were waited for; matrix products, arithmetic and copies ran while one was open for 0% of the time, Pallas kernels for 18%

profile of v3, /device:TPU:0, one launch (start us, length us, event | category | flops | bytes accessed | tf_op | source)
XLA Modules:
  0.0 83.6 jit_solution(17644140479672196853)
XLA Ops:
  0.7 3.0 %collective-permute-start.2 = (bf16[192,256]{1,0:T(8,128)(2,1)}, bf16[192,256]{1,0:T(8,128)(2,1)S(1)}, u32[]{:S(2)}, u32[]{:S(2)}) collective-permute-start(bf16[192,256]{1,0:T(8,128)(2,1)} %bitcast.11), channel_id=1, source_target_pairs={{0,2},{1,3},{2,4},{3,5},{4,6},{5,7},{6,8},{7,9},{8,10},{9,11},{10,... | collective-permute-start | bytes 294920 | tf_op jit(solution)/shard_map/ppermute | solution.py:36
  3.7 1.6 %collective-permute-start.3 = (bf16[192,256]{1,0:T(8,128)(2,1)}, bf16[192,256]{1,0:T(8,128)(2,1)S(1)}, u32[]{:S(2)}, u32[]{:S(2)}) collective-permute-start(bf16[192,256]{1,0:T(8,128)(2,1)} %bitcast.12), channel_id=1, source_target_pairs={{0,4},{1,5},{2,6},{3,7},{4,8},{5,9},{6,10},{7,11},{8,12},{9,13},{1... | collective-permute-start | bytes 294920 | tf_op jit(solution)/shard_map/ppermute | solution.py:36
  5.3 1.4 %split.1 = (bf16[192,896]{1,0:T(8,128)(2,1)S(1)}, bf16[192,896]{1,0:T(8,128)(2,1)S(1)}, bf16[192,896]{1,0:T(8,128)(2,1)S(1)}, bf16[192,896]{1,0:T(8,128)(2,1)S(1)}, s32[15,192]{1,0:T(8,128)S(1)}) custom-call(bf16[192,1792]{1,0:T(8,128)(2,1)} %bitcast.9, bf16[192,1792]{1,0:T(8,128)(2,1)} %bitcast.10, s32[14,1,192]{2,1,0:T(1,128)} %bitcast.14, s32[1,192]{1,0:T(1,128)} %l_ref.1), custom_call_target="tpu_custom_call" | custom-call | tf_op jit(solution)/shard_map/split/pallas_call | solution.py:86
  6.7 0.7 copy-done.2
  7.4 3.2 %collective-permute-done.2.near = bf16[192,256]{1,0:T(8,128)(2,1)S(1)} collective-permute-done((bf16[192,256]{1,0:T(8,128)(2,1)}, bf16[192,256]{1,0:T(8,128)(2,1)S(1)}, u32[]{:S(2)}, u32[]{:S(2)}) %collective-permute-start.2) | collective-permute-done | bytes 98336 | tf_op jit(solution)/shard_map/ppermute | solution.py:36
  10.6 0.8 %pack.1 = (bf16[512,128]{1,0:T(8,128)(2,1)S(1)}, bf16[512,128]{1,0:T(8,128)(2,1)S(1)}) custom-call(bf16[192,256]{1,0:T(8,128)(2,1)} %bitcast.13, bf16[192,256]{1,0:T(8,128)(2,1)S(1)} %collective-permute-done.2.near, bf16[192,256]{1,0:T(8,128)(2,1)S(1)} %collective-permute-done.3.far), custom_call_target="tpu_custom_call" | custom-call | tf_op jit(solution)/shard_map/pack/pallas_call | solution.py:120
  11.4 0.6 copy-done.3
  12.1 1.7 %collective-permute-start.7 = (bf16[1792,128]{1,0:T(8,128)(2,1)S(1)}, bf16[1792,128]{1,0:T(8,128)(2,1)S(1)}, u32[]{:S(2)}, u32[]{:S(2)}) collective-permute-start(bf16[1792,128]{1,0:T(8,128)(2,1)S(1)} %constant_dynamic-slice_fusion.w_own), channel_id=1, source_target_pairs={{0,16},{16,0},{1,17},{17,1},{2,18},{18,2},{3,19},{19,3},{4,20},{20... | collective-permute-start | bytes 1376264 | tf_op jit(solution)/shard_map/ppermute | solution.py:40
  14.5 1.7 %collective-permute-done.5.refs_7_.l_oth = s32[15,192]{1,0:T(8,128)S(1)} collective-permute-done((s32[15,192]{1,0:T(8,128)S(1)}, s32[15,192]{1,0:T(8,128)S(1)}, u32[]{:S(2)}, u32[]{:S(2)}) %collective-permute-start.5) | collective-permute-done | bytes 11552 | tf_op jit(solution)/shard_map/ppermute | solution.py:40
  16.3 1.4 %collective-permute-done.4.refs_5_ = bf16[512,128]{1,0:T(8,128)(2,1)S(1)} collective-permute-done((bf16[512,128]{1,0:T(8,128)(2,1)}, bf16[512,128]{1,0:T(8,128)(2,1)S(1)}, u32[]{:S(2)}, u32[]{:S(2)}) %collective-permute-start.4) | collective-permute-done | bytes 131104 | tf_op jit(solution)/shard_map/ppermute | solution.py:40
  17.8 3.8 %value_terms.1 = (f32[384,128]{1,0:T(8,128)S(1)}, bf16[384,128]{1,0:T(8,128)(2,1)S(1)}, bf16[128,128]{1,0:T(8,128)(2,1)S(1)}, f32[21,128]{1,0:T(8,128)S(1)}, f32[21,128]{1,0:T(8,128)S(1)}) custom-call(bf16[192,896]{1,0:T(8,128)(2,1)S(1)} %get-tuple-element.52.refs_0_, bf16[192,896]{1,0:T(8,128)(2,1)S(1)} %collective-permute-done.refs_1_, ...), custom_call_target="tpu_custom_call" | custom-call | tf_op jit(solution)/shard_map/value_terms/pallas_call | solution.py:290
  21.6 3.0 %collective-permute-start.8 = (bf16[384,128]{1,0:T(8,128)(2,1)S(1)}, bf16[384,128]{1,0:T(8,128)(2,1)S(1)}, u32[]{:S(2)}, u32[]{:S(2)}) collective-permute-start(bf16[384,128]{1,0:T(8,128)(2,1)S(1)} %get-tuple-element.70), channel_id=1, source_target_pairs={{0,14},{1,15},{2,0},{3,1},{4,2},{5,3},{6,4},{7,5},{8,6},{9,7},{10,... | collective-permute-start | bytes 294920 | tf_op jit(solution)/shard_map/ppermute | solution.py:36
  25.1 3.3 %project.1 = (bf16[384,128]{1,0:T(8,128)(2,1)S(1)}, bf16[128,128]{1,0:T(8,128)(2,1)S(1)}, bf16[384,3584]{1,0:T(8,128)(2,1)S(1)}) custom-call(bf16[192,3584]{1,0:T(8,128)(2,1)S(1)} %bitcast.8, bf16[192,3584]{1,0:T(8,128)(2,1)} %collective-permute-done.6.h_oth, s32[15,192]{1,0:T(8,128)S(1)} %get-tuple-element.62.refs_6_.l_own, ...), custom_call_target="tpu_custom_call" | custom-call | tf_op jit(solution)/shard_map/project/pallas_call | solution.py:378
  28.5 1.0 %weight_terms.1 = (f32[1792,128]{1,0:T(8,128)S(1)}, bf16[1792,128]{1,0:T(8,128)(2,1)S(1)}) custom-call(bf16[384,3584]{1,0:T(8,128)(2,1)S(1)} %get-tuple-element.68.spiked, f32[384,128]{1,0:T(8,128)S(1)} %get-tuple-element.69.own, bf16[384,128]{1,0:T(8,128)(2,1)S(1)} %collective-permute-done.8.near, bf16[128,128]{1,0:T(8,128)(2,1)S(1)} %collective-permute-done.9.far), custom_call_target="tpu_custom_call" | custom-call | tf_op jit(solution)/shard_map/weight_terms/pallas_call | solution.py:431
  29.5 1.6 %collective-permute-start.12 = (bf16[1792,128]{1,0:T(8,128)(2,1)S(1)}, bf16[1792,128]{1,0:T(8,128)(2,1)S(1)}, u32[]{:S(2)}, u32[]{:S(2)}) collective-permute-start(bf16[1792,128]{1,0:T(8,128)(2,1)S(1)} %get-tuple-element.72), channel_id=1, source_target_pairs={{0,16},{1,17},{2,18},{3,19},{4,20},{5,21},{6,22},{7,23},{8,24},{9,... | collective-permute-start | bytes 1376264 | tf_op jit(solution)/shard_map/ppermute | solution.py:45
  31.1 1.7 %collective-permute-start.10 = (bf16[384,128]{1,0:T(8,128)(2,1)S(1)}, bf16[384,128]{1,0:T(8,128)(2,1)S(1)}, u32[]{:S(2)}, u32[]{:S(2)}) collective-permute-start(bf16[384,128]{1,0:T(8,128)(2,1)S(1)} %get-tuple-element.73.refs_8_), channel_id=1, source_target_pairs={{0,2},{1,3},{2,4},{3,5},{4,6},{5,7},{6,8},{7,9},{8,10},{9,11},{10,... | collective-permute-start | bytes 294920 | tf_op jit(solution)/shard_map/ppermute | solution.py:36
  32.8 5.7 %collective-permute-done.11.refs_10_ = bf16[128,128]{1,0:T(8,128)(2,1)S(1)} collective-permute-done((bf16[128,128]{1,0:T(8,128)(2,1)S(1)}, bf16[128,128]{1,0:T(8,128)(2,1)S(1)}, u32[]{:S(2)}, u32[]{:S(2)}) %collective-permute-start.11) | collective-permute-done | bytes 32800 | tf_op jit(solution)/shard_map/ppermute | solution.py:36
  38.6 5.7 %key_terms.1 = (f32[384,128]{1,0:T(8,128)S(1)}, bf16[384,128]{1,0:T(8,128)(2,1)S(1)}, bf16[128,128]{1,0:T(8,128)(2,1)S(1)}, bf16[192,896]{1,0:T(8,128)(2,1)S(1)}, bf16[192,896]{1,0:T(8,128)(2,1)S(1)}) custom-call(bf16[192,896]{1,0:T(8,128)(2,1)S(1)} %get-tuple-element.52.refs_0_, bf16[192,896]{1,0:T(8,128)(2,1)S(1)} %collective-permute-done.refs_1_, ...), custom_call_target="tpu_custom_call" | custom-call | tf_op jit(solution)/shard_map/key_terms/pallas_call | solution.py:307
  44.4 1.2 %collective-permute-start.13 = (bf16[896,128]{1,0:T(8,128)(2,1)S(1)}, bf16[896,128]{1,0:T(8,128)(2,1)S(1)}, u32[]{:S(2)}, u32[]{:S(2)}) collective-permute-start(bf16[896,128]{1,0:T(8,128)(2,1)S(1)} %get-tuple-element.81), channel_id=1, source_target_pairs={{0,2},{1,5},{2,0},{3,7},{4,6},{5,1},{6,4},{7,3},{8,10},{9,13},{10,... | collective-permute-start | bytes 688136 | tf_op jit(solution)/shard_map/ppermute | solution.py:45
  45.6 4.9 %collective-permute-done.13.got = bf16[896,128]{1,0:T(8,128)(2,1)S(1)} collective-permute-done((bf16[896,128]{1,0:T(8,128)(2,1)S(1)}, bf16[896,128]{1,0:T(8,128)(2,1)S(1)}, u32[]{:S(2)}, u32[]{:S(2)}) %collective-permute-start.13) | collective-permute-done | bytes 229408 | tf_op jit(solution)/shard_map/ppermute | solution.py:45
  50.7 2.8 %collective-permute-start.15 = (bf16[384,128]{1,0:T(8,128)(2,1)S(1)}, bf16[384,128]{1,0:T(8,128)(2,1)S(1)}, u32[]{:S(2)}, u32[]{:S(2)}) collective-permute-start(bf16[384,128]{1,0:T(8,128)(2,1)S(1)} %get-tuple-element.86), channel_id=1, source_target_pairs={{0,14},{1,15},{2,0},{3,1},{4,2},{5,3},{6,4},{7,5},{8,6},{9,7},{10,... | collective-permute-start | bytes 294920 | tf_op jit(solution)/shard_map/ppermute | solution.py:36
  53.5 1.0 %collective-permute-start.16 = (bf16[128,128]{1,0:T(8,128)(2,1)S(1)}, bf16[128,128]{1,0:T(8,128)(2,1)S(1)}, u32[]{:S(2)}, u32[]{:S(2)}) collective-permute-start(bf16[128,128]{1,0:T(8,128)(2,1)S(1)} %get-tuple-element.87), channel_id=1, source_target_pairs={{0,12},{1,13},{2,14},{3,15},{4,0},{5,1},{6,2},{7,3},{8,4},{9,5},{1... | collective-permute-start | bytes 98312 | tf_op jit(solution)/shard_map/ppermute | solution.py:36
  54.5 3.7 %collective-permute-done.16.far = bf16[128,128]{1,0:T(8,128)(2,1)S(1)} collective-permute-done((bf16[128,128]{1,0:T(8,128)(2,1)S(1)}, bf16[128,128]{1,0:T(8,128)(2,1)S(1)}, u32[]{:S(2)}, u32[]{:S(2)}) %collective-permute-start.16) | collective-permute-done | bytes 32800 | tf_op jit(solution)/shard_map/ppermute | solution.py:36
  58.9 1.2 %collective-permute-done.18.k_oth = bf16[192,128]{1,0:T(8,128)(2,1)S(1)} collective-permute-done((bf16[192,128]{1,0:T(8,128)(2,1)S(1)}, bf16[192,128]{1,0:T(8,128)(2,1)S(1)}, u32[]{:S(2)}, u32[]{:S(2)}) %collective-permute-start.18) | collective-permute-done | bytes 49184 | tf_op jit(solution)/shard_map/ppermute | solution.py:40
  60.1 3.7 %collective-permute-done.19.got = bf16[224,128]{1,0:T(8,128)(2,1)S(1)} collective-permute-done((bf16[224,128]{1,0:T(8,128)(2,1)S(1)}, bf16[224,128]{1,0:T(8,128)(2,1)S(1)}, u32[]{:S(2)}, u32[]{:S(2)}) %collective-permute-start.19) | collective-permute-done | bytes 57376 | tf_op jit(solution)/shard_map/ppermute | solution.py:45
  64.0 0.9 %place_tokens.1 = (bf16[192,1792]{1,0:T(8,128)(2,1)}, bf16[192,256]{1,0:T(8,128)(2,1)}) custom-call(bf16[192,896]{1,0:T(8,128)(2,1)S(1)} %get-tuple-element.75.q_own, bf16[192,896]{1,0:T(8,128)(2,1)S(1)} %collective-permute-done.14.q_oth, bf16[192,128]{1,0:T(8,128)(2,1)S(1)} %get-tuple-element.93.k_own, bf16[192,128]{1,0:T(8,128)(2,1)S(1)} %collective-permute-done.18.k_oth), custom_call_target="tpu_custom_call" | custom-call | tf_op jit(solution)/shard_map/place_tokens/pallas_call | solution.py:531
  64.9 4.1 %collective-permute-done.20.second = bf16[224,128]{1,0:T(8,128)(2,1)S(1)} collective-permute-done((bf16[224,128]{1,0:T(8,128)(2,1)S(1)}, bf16[224,128]{1,0:T(8,128)(2,1)S(1)}, u32[]{:S(2)}, u32[]{:S(2)}) %collective-permute-start.20) | collective-permute-done | bytes 57376 | tf_op jit(solution)/shard_map/ppermute | solution.py:45
  69.1 5.6 %collective-permute-done.21.second = bf16[448,128]{1,0:T(8,128)(2,1)S(1)} collective-permute-done((bf16[448,128]{1,0:T(8,128)(2,1)S(1)}, bf16[448,128]{1,0:T(8,128)(2,1)S(1)}, u32[]{:S(2)}, u32[]{:S(2)}) %collective-permute-start.21) | collective-permute-done | bytes 114720 | tf_op jit(solution)/shard_map/ppermute | solution.py:45
  74.8 1.5 %collective-permute-start.22 = (bf16[896,128]{1,0:T(8,128)(2,1)S(1)}, bf16[896,128]{1,0:T(8,128)(2,1)S(1)}, u32[]{:S(2)}, u32[]{:S(2)}) collective-permute-start(bf16[896,128]{1,0:T(8,128)(2,1)S(1)} %join.3.own_low), channel_id=1, source_target_pairs={{0,2},{1,5},{2,0},{3,7},{4,6},{5,1},{6,4},{7,3},{8,10},{9,13},{10,... | collective-permute-start | bytes 688136 | tf_op jit(solution)/shard_map/ppermute | solution.py:45
  76.3 4.5 %collective-permute-done.22.own_high = bf16[896,128]{1,0:T(8,128)(2,1)S(1)} collective-permute-done((bf16[896,128]{1,0:T(8,128)(2,1)S(1)}, bf16[896,128]{1,0:T(8,128)(2,1)S(1)}, u32[]{:S(2)}, u32[]{:S(2)}) %collective-permute-start.22) | collective-permute-done | bytes 229408 | tf_op jit(solution)/shard_map/ppermute | solution.py:45
  80.9 1.5 %collective-permute-done.24.oth_high = bf16[896,128]{1,0:T(8,128)(2,1)S(1)} collective-permute-done((bf16[896,128]{1,0:T(8,128)(2,1)S(1)}, bf16[896,128]{1,0:T(8,128)(2,1)S(1)}, u32[]{:S(2)}, u32[]{:S(2)}) %collective-permute-start.24) | collective-permute-done | bytes 229408 | tf_op jit(solution)/shard_map/ppermute | solution.py:40
  82.4 1.0 %place_weight.1 = bf16[1792,256]{1,0:T(8,128)(2,1)} custom-call(bf16[896,128]{1,0:T(8,128)(2,1)S(1)} %join.3.own_low, bf16[896,128]{1,0:T(8,128)(2,1)S(1)} %collective-permute-done.22.own_high, bf16[896,128]{1,0:T(8,128)(2,1)S(1)} %collective-permute-done.23.oth_low, bf16[896,128]{1,0:T(8,128)(2,1)S(1)} %collective-permute-done.24.oth_high), custom_call_target="tpu_custom_call" | custom-call | tf_op jit(solution)/shard_map/place_weight/pallas_call | solution.py:507
  (42 shorter events, 2.7 us)
Async XLA Ops:
  0.6 11.4 %copy-start = (bf16[1792,256]{1,0:T(8,128)(2,1)S(1)}, bf16[1792,256]{1,0:T(8,128)(2,1)}, u32[]{:S(2)}) copy-start(bf16[1792,256]{1,0:T(8,128)(2,1)} %param.9) | copy-start | bytes 2752516
  0.6 11.4 %copy-start.1 = (bf16[1,192,3584]{2,1,0:T(8,128)(2,1)S(1)}, bf16[1,192,3584]{2,1,0:T(8,128)(2,1)}, u32[]{:S(2)}) copy-start(bf16[1,192,3584]{2,1,0:T(8,128)(2,1)} %param.7) | copy-start | bytes 4128772
  0.7 9.9 %collective-permute-start.2 = (bf16[192,256]{1,0:T(8,128)(2,1)}, bf16[192,256]{1,0:T(8,128)(2,1)S(1)}, u32[]{:S(2)}, u32[]{:S(2)}) collective-permute-start(bf16[192,256]{1,0:T(8,128)(2,1)} %bitcast.11), channel_id=1, source_target_pairs={{0,2},{1,3},{2,4},{3,5},{4,6},{5,7},{6,8},{7,9},{8,10},{9,11},{10,... | collective-permute-start | bytes 294920 | tf_op jit(solution)/shard_map/ppermute | solution.py:36
  3.7 6.9 %collective-permute-start.3 = (bf16[192,256]{1,0:T(8,128)(2,1)}, bf16[192,256]{1,0:T(8,128)(2,1)S(1)}, u32[]{:S(2)}, u32[]{:S(2)}) collective-permute-start(bf16[192,256]{1,0:T(8,128)(2,1)} %bitcast.12), channel_id=1, source_target_pairs={{0,4},{1,5},{2,6},{3,7},{4,8},{5,9},{6,10},{7,11},{8,12},{9,13},{1... | collective-permute-start | bytes 294920 | tf_op jit(solution)/shard_map/ppermute | solution.py:36
  6.6 0.7 copy-start.2
  11.4 0.7 copy-start.3
  12.1 13.1 %collective-permute-start.6 = (bf16[192,3584]{1,0:T(8,128)(2,1)S(1)}, bf16[192,3584]{1,0:T(8,128)(2,1)}, u32[]{:S(2)}, u32[]{:S(2)}) collective-permute-start(bf16[192,3584]{1,0:T(8,128)(2,1)S(1)} %bitcast.7), channel_id=1, source_target_pairs={{0,1},{1,0},{2,3},{3,2},{4,5},{5,4},{6,7},{7,6},{8,9},{9,8},{10,11... | collective-permute-start | bytes 4128776 | tf_op jit(solution)/shard_map/ppermute | solution.py:40
  12.1 13.0 %collective-permute-start.7 = (bf16[1792,128]{1,0:T(8,128)(2,1)S(1)}, bf16[1792,128]{1,0:T(8,128)(2,1)S(1)}, u32[]{:S(2)}, u32[]{:S(2)}) collective-permute-start(bf16[1792,128]{1,0:T(8,128)(2,1)S(1)} %constant_dynamic-slice_fusion.w_own), channel_id=1, source_target_pairs={{0,16},{16,0},{1,17},{17,1},{2,18},{18,2},{3,19},{19,3},{4,20},{20... | collective-permute-start | bytes 1376264 | tf_op jit(solution)/shard_map/ppermute | solution.py:40
  13.8 4.0 %collective-permute-start = (bf16[192,896]{1,0:T(8,128)(2,1)}, bf16[192,896]{1,0:T(8,128)(2,1)S(1)}, u32[]{:S(2)}, u32[]{:S(2)}) collective-permute-start(bf16[192,896]{1,0:T(8,128)(2,1)} %copy-done.2), channel_id=1, source_target_pairs={{0,1},{1,0},{2,3},{3,2},{4,5},{5,4},{6,7},{7,6},{8,9},{9,8},{10,11... | collective-permute-start | bytes 1032200 | tf_op jit(solution)/shard_map/ppermute | solution.py:40
  14.0 3.8 %collective-permute-start.1 = (bf16[192,896]{1,0:T(8,128)(2,1)S(1)}, bf16[192,896]{1,0:T(8,128)(2,1)S(1)}, u32[]{:S(2)}, u32[]{:S(2)}) collective-permute-start(bf16[192,896]{1,0:T(8,128)(2,1)S(1)} %get-tuple-element.55), channel_id=1, source_target_pairs={{0,1},{1,0},{2,3},{3,2},{4,5},{5,4},{6,7},{7,6},{8,9},{9,8},{10,11... | collective-permute-start | bytes 1032200 | tf_op jit(solution)/shard_map/ppermute | solution.py:40
  14.3 1.9 %collective-permute-start.5 = (s32[15,192]{1,0:T(8,128)S(1)}, s32[15,192]{1,0:T(8,128)S(1)}, u32[]{:S(2)}, u32[]{:S(2)}) collective-permute-start(s32[15,192]{1,0:T(8,128)S(1)} %get-tuple-element.62.refs_6_.l_own), channel_id=1, source_target_pairs={{0,1},{1,0},{2,3},{3,2},{4,5},{5,4},{6,7},{7,6},{8,9},{9,8},{10,11... | collective-permute-start | bytes 34568 | tf_op jit(solution)/shard_map/ppermute | solution.py:40
  16.2 1.6 %collective-permute-start.4 = (bf16[512,128]{1,0:T(8,128)(2,1)}, bf16[512,128]{1,0:T(8,128)(2,1)S(1)}, u32[]{:S(2)}, u32[]{:S(2)}) collective-permute-start(bf16[512,128]{1,0:T(8,128)(2,1)} %copy-done.3), channel_id=1, source_target_pairs={{0,1},{1,0},{2,3},{3,2},{4,5},{5,4},{6,7},{7,6},{8,9},{9,8},{10,11... | collective-permute-start | bytes 393224 | tf_op jit(solution)/shard_map/ppermute | solution.py:40
  21.6 6.9 %collective-permute-start.8 = (bf16[384,128]{1,0:T(8,128)(2,1)S(1)}, bf16[384,128]{1,0:T(8,128)(2,1)S(1)}, u32[]{:S(2)}, u32[]{:S(2)}) collective-permute-start(bf16[384,128]{1,0:T(8,128)(2,1)S(1)} %get-tuple-element.70), channel_id=1, source_target_pairs={{0,14},{1,15},{2,0},{3,1},{4,2},{5,3},{6,4},{7,5},{8,6},{9,7},{10,... | collective-permute-start | bytes 294920 | tf_op jit(solution)/shard_map/ppermute | solution.py:36
  24.6 3.9 %collective-permute-start.9 = (bf16[128,128]{1,0:T(8,128)(2,1)S(1)}, bf16[128,128]{1,0:T(8,128)(2,1)S(1)}, u32[]{:S(2)}, u32[]{:S(2)}) collective-permute-start(bf16[128,128]{1,0:T(8,128)(2,1)S(1)} %get-tuple-element.71), channel_id=1, source_target_pairs={{0,12},{1,13},{2,14},{3,15},{4,0},{5,1},{6,2},{7,3},{8,4},{9,5},{1... | collective-permute-start | bytes 98312 | tf_op jit(solution)/shard_map/ppermute | solution.py:36
  29.5 14.8 %collective-permute-start.12 = (bf16[1792,128]{1,0:T(8,128)(2,1)S(1)}, bf16[1792,128]{1,0:T(8,128)(2,1)S(1)}, u32[]{:S(2)}, u32[]{:S(2)}) collective-permute-start(bf16[1792,128]{1,0:T(8,128)(2,1)S(1)} %get-tuple-element.72), channel_id=1, source_target_pairs={{0,16},{1,17},{2,18},{3,19},{4,20},{5,21},{6,22},{7,23},{8,24},{9,... | collective-permute-start | bytes 1376264 | tf_op jit(solution)/shard_map/ppermute | solution.py:45
  31.1 7.5 %collective-permute-start.10 = (bf16[384,128]{1,0:T(8,128)(2,1)S(1)}, bf16[384,128]{1,0:T(8,128)(2,1)S(1)}, u32[]{:S(2)}, u32[]{:S(2)}) collective-permute-start(bf16[384,128]{1,0:T(8,128)(2,1)S(1)} %get-tuple-element.73.refs_8_), channel_id=1, source_target_pairs={{0,2},{1,3},{2,4},{3,5},{4,6},{5,7},{6,8},{7,9},{8,10},{9,11},{10,... | collective-permute-start | bytes 294920 | tf_op jit(solution)/shard_map/ppermute | solution.py:36
  32.8 5.7 %collective-permute-start.11 = (bf16[128,128]{1,0:T(8,128)(2,1)S(1)}, bf16[128,128]{1,0:T(8,128)(2,1)S(1)}, u32[]{:S(2)}, u32[]{:S(2)}) collective-permute-start(bf16[128,128]{1,0:T(8,128)(2,1)S(1)} %get-tuple-element.74), channel_id=1, source_target_pairs={{0,4},{1,5},{2,6},{3,7},{4,8},{5,9},{6,10},{7,11},{8,12},{9,13},{1... | collective-permute-start | bytes 98312 | tf_op jit(solution)/shard_map/ppermute | solution.py:36
  44.4 6.1 %collective-permute-start.13 = (bf16[896,128]{1,0:T(8,128)(2,1)S(1)}, bf16[896,128]{1,0:T(8,128)(2,1)S(1)}, u32[]{:S(2)}, u32[]{:S(2)}) collective-permute-start(bf16[896,128]{1,0:T(8,128)(2,1)S(1)} %get-tuple-element.81), channel_id=1, source_target_pairs={{0,2},{1,5},{2,0},{3,7},{4,6},{5,1},{6,4},{7,3},{8,10},{9,13},{10,... | collective-permute-start | bytes 688136 | tf_op jit(solution)/shard_map/ppermute | solution.py:45
  50.5 7.8 %collective-permute-start.14 = (bf16[192,896]{1,0:T(8,128)(2,1)S(1)}, bf16[192,896]{1,0:T(8,128)(2,1)S(1)}, u32[]{:S(2)}, u32[]{:S(2)}) collective-permute-start(bf16[192,896]{1,0:T(8,128)(2,1)S(1)} %get-tuple-element.83), channel_id=1, source_target_pairs={{0,1},{1,0},{2,3},{3,2},{4,5},{5,4},{6,7},{7,6},{8,9},{9,8},{10,11... | collective-permute-start | bytes 1032200 | tf_op jit(solution)/shard_map/ppermute | solution.py:40
  50.6 7.7 %collective-permute-start.17 = (bf16[448,128]{1,0:T(8,128)(2,1)S(1)}, bf16[448,128]{1,0:T(8,128)(2,1)S(1)}, u32[]{:S(2)}, u32[]{:S(2)}) collective-permute-start(bf16[448,128]{1,0:T(8,128)(2,1)S(1)} %get-tuple-element.82), channel_id=1, source_target_pairs={{0,4},{1,3},{2,6},{3,1},{4,0},{5,7},{6,2},{7,5},{8,12},{9,11},{10,... | collective-permute-start | bytes 344072 | tf_op jit(solution)/shard_map/ppermute | solution.py:45
  50.7 7.6 %collective-permute-start.15 = (bf16[384,128]{1,0:T(8,128)(2,1)S(1)}, bf16[384,128]{1,0:T(8,128)(2,1)S(1)}, u32[]{:S(2)}, u32[]{:S(2)}) collective-permute-start(bf16[384,128]{1,0:T(8,128)(2,1)S(1)} %get-tuple-element.86), channel_id=1, source_target_pairs={{0,14},{1,15},{2,0},{3,1},{4,2},{5,3},{6,4},{7,5},{8,6},{9,7},{10,... | collective-permute-start | bytes 294920 | tf_op jit(solution)/shard_map/ppermute | solution.py:36
  53.5 4.8 %collective-permute-start.16 = (bf16[128,128]{1,0:T(8,128)(2,1)S(1)}, bf16[128,128]{1,0:T(8,128)(2,1)S(1)}, u32[]{:S(2)}, u32[]{:S(2)}) collective-permute-start(bf16[128,128]{1,0:T(8,128)(2,1)S(1)} %get-tuple-element.87), channel_id=1, source_target_pairs={{0,12},{1,13},{2,14},{3,15},{4,0},{5,1},{6,2},{7,3},{8,4},{9,5},{1... | collective-permute-start | bytes 98312 | tf_op jit(solution)/shard_map/ppermute | solution.py:36
  58.3 5.5 %collective-permute-start.19 = (bf16[224,128]{1,0:T(8,128)(2,1)S(1)}, bf16[224,128]{1,0:T(8,128)(2,1)S(1)}, u32[]{:S(2)}, u32[]{:S(2)}) collective-permute-start(bf16[224,128]{1,0:T(8,128)(2,1)S(1)} %get-tuple-element.90), channel_id=1, source_target_pairs={{0,8},{1,9},{2,10},{3,11},{4,12},{5,13},{6,14},{7,15},{8,0},{9,1},... | collective-permute-start | bytes 172040 | tf_op jit(solution)/shard_map/ppermute | solution.py:45
  58.8 1.3 %collective-permute-start.18 = (bf16[192,128]{1,0:T(8,128)(2,1)S(1)}, bf16[192,128]{1,0:T(8,128)(2,1)S(1)}, u32[]{:S(2)}, u32[]{:S(2)}) collective-permute-start(bf16[192,128]{1,0:T(8,128)(2,1)S(1)} %get-tuple-element.94), channel_id=1, source_target_pairs={{0,1},{1,0},{2,3},{3,2},{4,5},{5,4},{6,7},{7,6},{8,9},{9,8},{10,11... | collective-permute-start | bytes 147464 | tf_op jit(solution)/shard_map/ppermute | solution.py:40
  63.9 5.2 %collective-permute-start.20 = (bf16[224,128]{1,0:T(8,128)(2,1)S(1)}, bf16[224,128]{1,0:T(8,128)(2,1)S(1)}, u32[]{:S(2)}, u32[]{:S(2)}) collective-permute-start(bf16[224,128]{1,0:T(8,128)(2,1)S(1)} %halve.7.first), channel_id=1, source_target_pairs={{0,8},{1,9},{2,10},{3,11},{4,12},{5,13},{6,14},{7,15},{8,0},{9,1},... | collective-permute-start | bytes 172040 | tf_op jit(solution)/shard_map/ppermute | solution.py:45
  69.0 5.7 %collective-permute-start.21 = (bf16[448,128]{1,0:T(8,128)(2,1)S(1)}, bf16[448,128]{1,0:T(8,128)(2,1)S(1)}, u32[]{:S(2)}, u32[]{:S(2)}) collective-permute-start(bf16[448,128]{1,0:T(8,128)(2,1)S(1)} %join.2.first), channel_id=1, source_target_pairs={{0,4},{1,3},{2,6},{3,1},{4,0},{5,7},{6,2},{7,5},{8,12},{9,11},{10,... | collective-permute-start | bytes 344072 | tf_op jit(solution)/shard_map/ppermute | solution.py:45
  74.8 6.1 %collective-permute-start.22 = (bf16[896,128]{1,0:T(8,128)(2,1)S(1)}, bf16[896,128]{1,0:T(8,128)(2,1)S(1)}, u32[]{:S(2)}, u32[]{:S(2)}) collective-permute-start(bf16[896,128]{1,0:T(8,128)(2,1)S(1)} %join.3.own_low), channel_id=1, source_target_pairs={{0,2},{1,5},{2,0},{3,7},{4,6},{5,1},{6,4},{7,3},{8,10},{9,13},{10,... | collective-permute-start | bytes 688136 | tf_op jit(solution)/shard_map/ppermute | solution.py:45
  76.3 4.5 %collective-permute-start.23 = (bf16[896,128]{1,0:T(8,128)(2,1)S(1)}, bf16[896,128]{1,0:T(8,128)(2,1)S(1)}, u32[]{:S(2)}, u32[]{:S(2)}) collective-permute-start(bf16[896,128]{1,0:T(8,128)(2,1)S(1)} %join.3.own_low), channel_id=1, source_target_pairs={{0,1},{1,0},{2,3},{3,2},{4,5},{5,4},{6,7},{7,6},{8,9},{9,8},{10,11... | collective-permute-start | bytes 688136 | tf_op jit(solution)/shard_map/ppermute | solution.py:40
  80.9 1.5 %collective-permute-start.24 = (bf16[896,128]{1,0:T(8,128)(2,1)S(1)}, bf16[896,128]{1,0:T(8,128)(2,1)S(1)}, u32[]{:S(2)}, u32[]{:S(2)}) collective-permute-start(bf16[896,128]{1,0:T(8,128)(2,1)S(1)} %collective-permute-done.22.own_high), channel_id=1, source_target_pairs={{0,1},{1,0},{2,3},{3,2},{4,5},{5,4},{6,7},{7,6},{8,9},{9,8},{10,11... | collective-permute-start | bytes 688136 | tf_op jit(solution)/shard_map/ppermute | solution.py:40

commit v4 on v3

--- a/solution.py
+++ b/solution.py
@@ -31,18 +31,19 @@
     return pltpu.CompilerParams(vmem_limit_bytes=mib * 1024 * 1024)
 
 
-def shifted(value, steps):
+def shifted(value, steps, cores=(0, 1)):
     count = lax.axis_size("seq")
-    return lax.ppermute(value, "seq", [(i, (i + steps) % count) for i in range(count)])
+    pairs = [(i, (i + steps) % count) for i in range(count) if i % 2 in cores]
+    return lax.ppermute(value, "seq", pairs)
 
 
 def swapped(value, axis, flip):
     return lax.ppermute(value, axis, [(i, i ^ flip) for i in range(lax.axis_size(axis))])
 
 
-def crossed(value, flips):
+def crossed(value, flip):
     count = lax.axis_size("dp") * lax.axis_size("seq")
-    return lax.ppermute(value, ("dp", "seq"), [(i, i ^ flips[i % 2]) for i in range(count)])
+    return lax.ppermute(value, ("dp", "seq"), [(i, i ^ flip) for i in range(count)])
 
 
 def ordered(bit, own, other, axis=0):
@@ -61,11 +62,15 @@
 
 
 def split_kernel(
-    tok, q_ref, g_ref, m_ref, l_ref, q_own, q_send, g_own, g_send, marks, m_buf, l_buf, sems
+    tok, q_ref, g_ref, m_ref, l_ref, w_ref, k_ref, *rest
 ):
+    q_own, q_send, g_own, g_send, marks, w_half, k_tail, m_buf, l_buf, sems = rest
     core = lax.rem(lax.axis_index("seq"), 2)
     wide = GROUP * HD
-    pairs = [(m_ref, m_buf), (l_ref, l_buf)]
+    slim = pl.ds(pl.multiple_of(core * HD, HD), HD)
+    pairs = [(m_ref, m_buf), (l_ref, l_buf), (w_ref.at[:, slim], w_half)]
+    tail = k_tail.shape[0]
+    pairs.append((k_ref.at[pl.ds(tok - tail, tail)], k_tail))
     for source, own, send in ((q_ref, q_own, q_send), (g_ref, g_own, g_send)):
         for target, side in ((own, core), (send, 1 - core)):
             pairs.append((source.at[:, pl.ds(pl.multiple_of(side * wide, HD), wide)], target))
@@ -81,21 +86,27 @@
     return pltpu.with_memory_space_constraint(value, pltpu.HBM)
 
 
-def split(tok, query, grad, spikes, level):
+def split(tok, *values):
+    weight_rows = values[4].shape[0]
     half = jax.ShapeDtypeStruct((tok, GROUP * HD), bf16)
     return pl.pallas_call(
         functools.partial(split_kernel, tok),
-        out_shape=[half] * 4 + [jax.ShapeDtypeStruct((QH + 1, tok), jnp.int32)],
-        in_specs=[ANY] * 4,
-        out_specs=[VMEM] * 5,
+        out_shape=[half] * 4
+        + [
+            jax.ShapeDtypeStruct((QH + 1, tok), jnp.int32),
+            jax.ShapeDtypeStruct((weight_rows, HD), bf16),
+            jax.ShapeDtypeStruct((WINDOW - 2 * tok, KVH * HD), bf16),
+        ],
+        in_specs=[ANY] * 6,
+        out_specs=[VMEM] * 7,
         scratch_shapes=[
             pltpu.VMEM((QH, 1, tok), jnp.int32),
             pltpu.VMEM((1, tok), jnp.int32),
-            pltpu.SemaphoreType.DMA((6,)),
+            pltpu.SemaphoreType.DMA((8,)),
         ],
-        compiler_params=limit(4),
+        compiler_params=limit(6),
         name="split",
-    )(in_hbm(query), in_hbm(grad), in_hbm(spikes), in_hbm(level))
+    )(*[in_hbm(value) for value in values])
 
 
 def pack_kernel(tok, own, near, far, mine, send, sems):
@@ -109,7 +120,7 @@
     copies = run_copies(pairs, sems)
     for target, side in sides:
         cols = pl.ds(pl.multiple_of(side * HD, HD), HD)
-        target[:rest, :] = far[tok - rest :, cols]
+        target[:rest, :] = far[:, cols]
         target[rest : rest + tok, :] = near[:, cols]
     for copy in copies:
         copy.wait()
@@ -397,10 +408,9 @@
 
 
 def weight_kernel(tok, spiked, own, near, far, keep, send, w_buf):
-    core = lax.rem(lax.axis_index("seq"), 2)
     rows = spiked.shape[1] // 16
     value_grad = value_sum(tok, own[...], near[...], far[...]).astype(bf16)
-    mine = block_code(core)
+    mine = block_code()
     for part in range(4):
         term = dot_tn(spiked[:, part * 4 * rows : (part + 1) * 4 * rows], value_grad)
         for piece in range(4):
@@ -417,13 +427,13 @@
     return chip & 1, (chip >> 1) & 1, (chip >> 2) & 1
 
 
-def block_code(core):
-    return lax.axis_index("dp") * 8 + chip_code(core)
-
-
-def chip_code(core):
+def block_code():
+    return lax.axis_index("dp") * 8 + chip_code()
+
+
+def chip_code():
     y, near, far = chip_bits()
-    return jnp.where(core == 0, y * 4 + near * 2 + far, near * 4 + y * 2 + far)
+    return y * 4 + near * 2 + far
 
 
 def weight_terms(tok, spiked, terms):
@@ -442,33 +452,30 @@
     )(spiked, *terms)
 
 
-def halve_kernel(held, got, *outs):
-    total = held[...] + got[...].astype(f32)
-    half = total.shape[0] // 2
-    if len(outs) == 2:
-        outs[0][...] = total[:half]
-        outs[1][...] = total[half:].astype(bf16)
-    else:
-        outs[0][...] = total.astype(bf16)
-
-
-def halve(held, got, last=False):
-    rows = held.shape[0]
-    if last:
-        shapes = [jax.ShapeDtypeStruct((rows, HD), bf16)]
-    else:
-        shapes = [
-            jax.ShapeDtypeStruct((rows // 2, HD), f32),
-            jax.ShapeDtypeStruct((rows // 2, HD), bf16),
-        ]
-    return pl.pallas_call(
-        halve_kernel,
+def reduce_kernel(count, held, *refs):
+    total = held[...]
+    for got in refs[:count]:
+        total = total + got[...].astype(f32)
+    outs = refs[count:]
+    rows = total.shape[0] // len(outs)
+    outs[0][...] = total[:rows].astype(outs[0].dtype)
+    for part in range(1, len(outs)):
+        outs[part][...] = total[part * rows : (part + 1) * rows].astype(bf16)
+
+
+def reduce_step(held, got, parts):
+    rows = held.shape[0] // parts
+    shapes = [jax.ShapeDtypeStruct((rows, HD), bf16)] * parts
+    if parts > 1:
+        shapes[0] = jax.ShapeDtypeStruct((rows, HD), f32)
+    return pl.pallas_call(
+        functools.partial(reduce_kernel, len(got)),
         out_shape=shapes,
-        in_specs=[VMEM] * 2,
-        out_specs=[VMEM] * len(shapes),
+        in_specs=[VMEM] * (1 + len(got)),
+        out_specs=[VMEM] * parts,
         compiler_params=limit(6),
-        name="halve",
-    )(held, got)
+        name="reduce_step",
+    )(held, *got)
 
 
 def join_kernel(first, second, out):
@@ -488,15 +495,16 @@
     )(first, second)
 
 
-def place_weight_kernel(own_low, own_high, oth_low, oth_high, out, sems):
+def place_weight_kernel(*refs):
+    out, sems = refs[8:]
     core = lax.rem(lax.axis_index("seq"), 2)
-    rows = own_low.shape[0] // 4
+    code = chip_code()
+    rows = refs[0].shape[0] // 2
     pairs = []
-    for halves, side in (((own_low, own_high), core), ((oth_low, oth_high), 1 - core)):
-        code = chip_code(side)
+    for pieces, side in ((refs[:4], core), (refs[4:8], 1 - core)):
         cols = pl.ds(pl.multiple_of(side * HD, HD), HD)
         for index in range(8):
-            source = halves[index // 4].at[pl.ds(index % 4 * rows, rows)]
+            source = pieces[index // 2].at[pl.ds(index % 2 * rows, rows)]
             at = pl.ds(pl.multiple_of((index ^ code) * rows, 16), rows)
             pairs.append((source, out.at[at, cols]))
     for copy in run_copies(pairs, sems):
@@ -506,8 +514,8 @@
 def place_weight(*pieces):
     return pl.pallas_call(
         place_weight_kernel,
-        out_shape=jax.ShapeDtypeStruct((2 * pieces[0].shape[0], KVH * HD), bf16),
-        in_specs=[ANY] * 4,
+        out_shape=jax.ShapeDtypeStruct((4 * pieces[0].shape[0], KVH * HD), bf16),
+        in_specs=[ANY] * 8,
         out_specs=ANY,
         scratch_shapes=[pltpu.SemaphoreType.DMA((16,))],
         compiler_params=limit(2),
@@ -541,9 +549,10 @@
     )(q_own, q_oth, k_own, k_oth)
 
 
-def reduce_any(spiked, value_grad, core, place, row):
+def reduce_any(spiked, value_grad):
     n_dp, n_seq = lax.axis_size("dp"), lax.axis_size("seq")
-    chip = place // 2
+    place, row = lax.axis_index("seq"), lax.axis_index("dp")
+    core, chip = place % 2, place // 2
     part = lax.dot_general(
         spiked, value_grad, (((0,), (0,)), ((), ())), preferred_element_type=f32
     )
@@ -562,78 +571,85 @@
     return ordered(core, owned, swapped(owned, "seq", 1), axis=1)
 
 
-def after(value, *others):
-    return lax.optimization_barrier((value, *others))[0]
-
-
 def body(hidden_in, spike_level, value_weight, queries, key_states, spike_mask, out_grad):
     tok = hidden_in.shape[1]
     n_dp, n_seq = lax.axis_size("dp"), lax.axis_size("seq")
-    place, row = lax.axis_index("seq"), lax.axis_index("dp")
-    core = place % 2
     assert 0 < WINDOW - 2 * tok <= tok and 2 * tok % BLOCK == 0
 
     def both(value):
         return value, swapped(value, "seq", 1)
 
     own_keys = key_states[0]
-    near_keys, far_keys = lax.optimization_barrier((shifted(own_keys, 2), shifted(own_keys, 4)))
-    query_own, query_out, grad_own, grad_out, marks = split(
-        tok, queries[0], out_grad[0], jnp.transpose(spike_mask, (2, 0, 1)), spike_level
-    )
-    near_keys, far_keys, _ = lax.optimization_barrier((near_keys, far_keys, query_out))
-    keys, keys_out = pack(tok, own_keys, near_keys, far_keys)
-    weight_half = lax.dynamic_slice_in_dim(value_weight, core * HD, HD, 1)
-    raw = [query_own, swapped(query_out, "seq", 1), grad_own, swapped(grad_out, "seq", 1)]
-    raw += [keys, swapped(keys_out, "seq", 1)]
-    marks = both(marks)
+    query_own, query_out, grad_own, grad_out, marks_own, weight_half, key_tail = split(
+        tok,
+        queries[0],
+        out_grad[0],
+        jnp.transpose(spike_mask, (2, 0, 1)),
+        spike_level,
+        value_weight,
+        own_keys,
+    )
+    near_keys, far_keys = lax.optimization_barrier(
+        (shifted(own_keys, 2), shifted(key_tail, 4, cores=(1,)))
+    )
+    query_oth, grad_oth, marks_oth = (
+        swapped(value, "seq", 1) for value in (query_out, grad_out, marks_own)
+    )
+    near_keys, far_keys, query_oth, grad_oth, marks_oth = lax.optimization_barrier(
+        (near_keys, far_keys, query_oth, grad_oth, marks_oth)
+    )
+    keys_own, keys_out = pack(tok, own_keys, near_keys, far_keys)
     if n_dp == 2:
         weight = (weight_half, swapped(weight_half, "dp", 1))
     else:
         weight = (lax.all_gather(weight_half, "dp", axis=0, tiled=True),)
+    keys_oth, hidden_own, *weight = lax.optimization_barrier(
+        (swapped(keys_out, "seq", 1), hidden_in[0], *weight)
+    )
+    raw = [query_own, query_oth, grad_own, grad_oth, keys_own, keys_oth]
+    marks = (marks_own, marks_oth)
 
     own, near, far, top, norm = value_terms(tok, raw, marks)
     near, far = shifted(near, -2), shifted(far, -4)
-    values, tail, spiked = project(tok, both(after(hidden_in[0], keys_out)), marks, weight)
+    values, tail, spiked = project(tok, both(hidden_own), marks, weight)
 
     fast = n_dp == 2 and n_seq == 16 and hidden_in.shape[2] % 256 == 0
     if fast:
         keep, send = weight_terms(tok, spiked, (own, near, far))
-        values, tail = lax.optimization_barrier((values, tail, send))[:2]
-        got = crossed(send, (n_seq, n_seq))
+        values, tail, send = lax.optimization_barrier((values, tail, send))
+        got = crossed(send, n_seq)
     window = (values, shifted(values, 2), shifted(tail, 4))
-    own_k, near_k, far_k, query_mine, query_send = key_terms(tok, raw, top, norm, window)
+    own_k, near_k, far_k, query_mine, query_out = key_terms(tok, raw, top, norm, window)
     if fast:
-        keep, send = halve(keep, after(got, own_k))
-        near_k, far_k = lax.optimization_barrier((near_k, far_k, send))[:2]
-        got = crossed(send, (2, 4))
+        got, own_k = lax.optimization_barrier((got, own_k))
+        keep, *sends = reduce_step(keep, [got], 4)
+        near_k, far_k, *sends = lax.optimization_barrier((near_k, far_k, *sends))
+        got = [crossed(send, flip) for send, flip in zip(sends, (4, 2, 6))]
     near_k, far_k = shifted(near_k, -2), shifted(far_k, -4)
     if fast:
-        keep, send = halve(keep, got)
-        query_send = after(query_send, send)
-        got = crossed(send, (4, 2))
-    query_got = swapped(query_send, "seq", 1)
+        keep, send = reduce_step(keep, got, 2)
+        query_out, send = lax.optimization_barrier((query_out, send))
+        got = crossed(send, 8)
+    query_got = swapped(query_out, "seq", 1)
     if fast:
-        keep, send = halve(keep, after(got, near_k, far_k, query_got))
-        near_k, far_k = lax.optimization_barrier((near_k, far_k, send))[:2]
-        got = crossed(send, (8, 8))
-    key_mine, key_send = sum_keys(tok, own_k, near_k, far_k)
-    key_got = swapped(key_send, "seq", 1)
+        got, near_k, far_k, query_got = lax.optimization_barrier((got, near_k, far_k, query_got))
+        (owned,) = reduce_step(keep, [got], 1)
+        near_k, owned = lax.optimization_barrier((near_k, owned))
+    key_mine, key_out = sum_keys(tok, own_k, near_k, far_k)
+    key_got = swapped(key_out, "seq", 1)
     if fast:
-        (owned,) = halve(keep, after(got, key_got), last=True)
-        key_got = after(key_got, owned)
-        got = crossed(owned, (8, 8))
+        got, key_got = lax.optimization_barrier((crossed(owned, 8), key_got))
+        owned = join(owned, got)
+        key_got, owned = lax.optimization_barrier((key_got, owned))
     query_grad, key_grad = place_tokens(query_mine, query_got, key_mine, key_got)
     if fast:
-        owned = join(owned, after(got, query_grad))
-        owned = join(owned, crossed(owned, (4, 2)))
-        other = crossed(owned, (2, 4))
-        weight_grad = place_weight(
-            owned, other, swapped(owned, "seq", 1), swapped(other, "seq", 1)
-        )
+        pieces = [crossed(owned, flip) for flip in (4, 2, 6)]
+        *pieces, key_grad = lax.optimization_barrier((*pieces, key_grad))
+        pieces = [owned, *pieces]
+        weight_grad = place_weight(*pieces, *[swapped(piece, "seq", 1) for piece in pieces])
     else:
         value_grad = value_sum(tok, own, near, far).astype(bf16)
-        weight_grad = reduce_any(spiked, value_grad, core, place, row)
+        weight_grad = reduce_any(spiked, value_grad)
     return (query_grad[None], key_grad[None], weight_grad)
 
 

time: 83.8 us -> 77.4 us (0.924)
  waiting for transfers between devices: 41.5 us -> 26.2 us
  starting transfers between devices: 21.5 us -> 32.8 us
  local copies, waits for them, and re-layouts: 1.43 us -> 0.01 us
  Pallas kernels: 18.2 us -> 17.2 us
    ppermute x15 -> x17, waiting for transfers between devices: 35.6 us -> 21.8 us  [the longest x9 11 us: crossed(): lax.ppermute(value, ('dp', 'seq'), [(i, i ^ flip) for i in range(count)])]
    ppermute x10 -> x12, starting transfers between devices: 2.67 us -> 10.6 us  [swapped(): lax.ppermute(value, axis, [(i, i ^ flip) for i in range(lax.axis_size(axi...]
    ppermute x15 -> x17, starting transfers between devices: 18.8 us -> 22.2 us  [the longest x8 11.7 us: shifted(): return lax.ppermute(value, 'seq', pairs)]
    ppermute x10 -> x12, waiting for transfers between devices: 5.84 us -> 4.39 us  [swapped(): lax.ppermute(value, axis, [(i, i ^ flip) for i in range(lax.axis_size(axi...]
    unnamed x8 -> x4, local copies, waits for them, and re-layouts: 1.39 us -> 0.01 us
    pallas_call x1, Pallas kernels: 3.29 us -> 1.95 us  [project(): pl.pallas_call(functools.partial(project_kernel, tok, split), out_shape=[...]
  transfers between devices with their start and end apart: 25 -> 29, of which waited for: 13 -> 18; matrix products, arithmetic and copies ran while one was open for 0% -> 0% of each run, Pallas kernels for 18% -> 17%
where the time goes in v4:
time: 77.4 us; the launch traced here: 77.2 us
  starting transfers between devices  32.8 us (42%)
  waiting for transfers between devices  26.2 us (34%)
  Pallas kernels  17.2 us (22%)
  between operations  0.94 us (1%)
    ppermute x8, starting transfers between devices, shifted(): return lax.ppermute(value, 'seq', pairs)  11.7 us
    ppermute x9, waiting for transfers between devices, crossed(): lax.ppermute(value, ('dp', 'seq'), [(i, i ^ flip) for i in range(count)])  11 us
    ppermute x8, waiting for transfers between devices, shifted(): return lax.ppermute(value, 'seq', pairs)  10.8 us
    ppermute x12, starting transfers between devices, swapped(): lax.ppermute(value, axis, [(i, i ^ flip) for i in range(lax.axis_size(axi...  10.6 us
    ppermute x9, starting transfers between devices, crossed(): lax.ppermute(value, ('dp', 'seq'), [(i, i ^ flip) for i in range(count)])  10.5 us
    pallas_call x1, Pallas kernels, key_terms(): pl.pallas_call(functools.partial(key_kernel, tok), out_shape=term_shapes(...  5.73 us
    ppermute x12, waiting for transfers between devices, swapped(): lax.ppermute(value, axis, [(i, i ^ flip) for i in range(lax.axis_size(axi...  4.39 us
    pallas_call x1, Pallas kernels, value_terms(): pl.pallas_call(functools.partial(value_kernel, tok), out_shape=term_shape...  3.81 us
  transfers between devices with their start and end apart: 29, of which 18 were waited for; matrix products, arithmetic and copies ran while one was open for 0% of the time, Pallas kernels for 17%

profile of v4, /device:TPU:0, one launch (start us, length us, event | category | flops | bytes accessed | tf_op | source)
XLA Modules:
  0.0 77.2 jit_solution(3992607920654291546)
XLA Ops:
  0.7 1.7 %split.1 = (bf16[192,896]{1,0:T(8,128)(2,1)S(1)}, bf16[192,896]{1,0:T(8,128)(2,1)S(1)}, bf16[192,896]{1,0:T(8,128)(2,1)S(1)}, bf16[192,896]{1,0:T(8,128)(2,1)S(1...) custom-call(bf16[192,1792]{1,0:T(8,128)(2,1)} %bitcast.9, ...), custom_call_target="tpu_custom_call" | custom-call | tf_op jit(solution)/shard_map/split/pallas_call | solution.py:92
  2.9 2.9 %collective-permute-start.6 = (bf16[1792,128]{1,0:T(8,128)(2,1)S(1)}, bf16[1792,128]{1,0:T(8,128)(2,1)S(1)}, u32[]{:S(2)}, u32[]{:S(2)}) collective-permute-start(bf16[1792,128]{1,0:T(8,128)(2,1)S(1)} %get-tuple-element.94.w_own), channel_id=1, source_target_pairs={{0,16},{16,0},{1,17},{17,1},{2,18},{18,2},{3,19},{19,3},{4,20},{20... | collective-permute-start | bytes 1376264 | tf_op jit(solution)/shard_map/ppermute | solution.py:41
  5.9 1.5 %collective-permute-start = (bf16[192,256]{1,0:T(8,128)(2,1)S(1)}, bf16[192,256]{1,0:T(8,128)(2,1)S(1)}, u32[]{:S(2)}, u32[]{:S(2)}) collective-permute-start(bf16[192,256]{1,0:T(8,128)(2,1)S(1)} %bitcast.13), channel_id=1, source_target_pairs={{0,2},{1,3},{2,4},{3,5},{4,6},{5,7},{6,8},{7,9},{8,10},{9,11},{10,... | collective-permute-start | bytes 294920 | tf_op jit(solution)/shard_map/ppermute | solution.py:37
  8.1 5.7 %collective-permute-start.4 = (s32[15,192]{1,0:T(8,128)S(1)}, s32[15,192]{1,0:T(8,128)S(1)}, u32[]{:S(2)}, u32[]{:S(2)}) collective-permute-start(s32[15,192]{1,0:T(8,128)S(1)} %get-tuple-element.80.refs_6_.l_own), channel_id=1, source_target_pairs={{0,1},{1,0},{2,3},{3,2},{4,5},{5,4},{6,7},{7,6},{8,9},{9,8},{10,11... | collective-permute-start | bytes 34568 | tf_op jit(solution)/shard_map/ppermute | solution.py:41
  13.8 0.8 %collective-permute-done.4.refs_7_.l_oth = s32[15,192]{1,0:T(8,128)S(1)} collective-permute-done((s32[15,192]{1,0:T(8,128)S(1)}, s32[15,192]{1,0:T(8,128)S(1)}, u32[]{:S(2)}, u32[]{:S(2)}) %collective-permute-start.4) | collective-permute-done | bytes 11552 | tf_op jit(solution)/shard_map/ppermute | solution.py:41
  14.6 0.8 %pack.1 = (bf16[512,128]{1,0:T(8,128)(2,1)S(1)}, bf16[512,128]{1,0:T(8,128)(2,1)S(1)}) custom-call(bf16[192,256]{1,0:T(8,128)(2,1)} %bitcast.12, bf16[192,256]{1,0:T(8,128)(2,1)S(1)} %collective-permute-done.near, bf16[128,256]{1,0:T(8,128)(2,1)S(1)} %collective-permute-done.1.far), custom_call_target="tpu_custom_call" | custom-call | tf_op jit(solution)/shard_map/pack/pallas_call | solution.py:131
  17.2 3.8 %value_terms.1 = (f32[384,128]{1,0:T(8,128)S(1)}, bf16[384,128]{1,0:T(8,128)(2,1)S(1)}, bf16[128,128]{1,0:T(8,128)(2,1)S(1)}, f32[21,128]{1,0:T(8,128)S(1)}, f32[21,128]{1,0:T(8,128)S(1)}) custom-call(bf16[192,896]{1,0:T(8,128)(2,1)S(1)} %get-tuple-element.74.refs_0_, bf16[192,896]{1,0:T(8,128)(2,1)S(1)} %collective-permute-done.2.refs_1_, ...), custom_call_target="tpu_custom_call" | custom-call | tf_op jit(solution)/shard_map/value_terms/pallas_call | solution.py:301
  21.0 4.3 %collective-permute-start.8 = (bf16[384,128]{1,0:T(8,128)(2,1)S(1)}, bf16[384,128]{1,0:T(8,128)(2,1)S(1)}, u32[]{:S(2)}, u32[]{:S(2)}) collective-permute-start(bf16[384,128]{1,0:T(8,128)(2,1)S(1)} %get-tuple-element.100), channel_id=1, source_target_pairs={{0,14},{1,15},{2,0},{3,1},{4,2},{5,3},{6,4},{7,5},{8,6},{9,7},{10,... | collective-permute-start | bytes 294920 | tf_op jit(solution)/shard_map/ppermute | solution.py:37
  25.8 2.0 %project.1 = (bf16[384,128]{1,0:T(8,128)(2,1)S(1)}, bf16[128,128]{1,0:T(8,128)(2,1)S(1)}, bf16[384,3584]{1,0:T(8,128)(2,1)S(1)}) custom-call(bf16[192,3584]{1,0:T(8,128)(2,1)S(1)} %bitcast.8, bf16[192,3584]{1,0:T(8,128)(2,1)S(1)} %collective-permute-done.7.h_oth, s32[15,192]{1,0:T(8,128)S(1)} %get-tuple-element.80.refs_6_.l_own, ...), custom_call_target="tpu_custom_call" | custom-call | tf_op jit(solution)/shard_map/project/pallas_call | solution.py:389
  27.7 1.5 %collective-permute-done.9.far = bf16[128,128]{1,0:T(8,128)(2,1)S(1)} collective-permute-done((bf16[128,128]{1,0:T(8,128)(2,1)S(1)}, bf16[128,128]{1,0:T(8,128)(2,1)S(1)}, u32[]{:S(2)}, u32[]{:S(2)}) %collective-permute-start.9) | collective-permute-done | bytes 32800 | tf_op jit(solution)/shard_map/ppermute | solution.py:37
  29.2 1.0 %weight_terms.1 = (f32[1792,128]{1,0:T(8,128)S(1)}, bf16[1792,128]{1,0:T(8,128)(2,1)S(1)}) custom-call(bf16[384,3584]{1,0:T(8,128)(2,1)S(1)} %get-tuple-element.98.spiked, f32[384,128]{1,0:T(8,128)S(1)} %get-tuple-element.99.own, bf16[384,128]{1,0:T(8,128)(2,1)S(1)} %collective-permute-done.8.near, bf16[128,128]{1,0:T(8,128)(2,1)S(1)} %collective-permute-done.9.far), custom_call_target="tpu_custom_call" | custom-call | tf_op jit(solution)/shard_map/weight_terms/pallas_call | solution.py:441
  30.3 1.6 %collective-permute-start.12 = (bf16[1792,128]{1,0:T(8,128)(2,1)S(1)}, bf16[1792,128]{1,0:T(8,128)(2,1)S(1)}, u32[]{:S(2)}, u32[]{:S(2)}) collective-permute-start(bf16[1792,128]{1,0:T(8,128)(2,1)S(1)} %get-tuple-element.108), channel_id=1, source_target_pairs={{0,16},{1,17},{2,18},{3,19},{4,20},{5,21},{6,22},{7,23},{8,24},{9,... | collective-permute-start | bytes 1376264 | tf_op jit(solution)/shard_map/ppermute | solution.py:46
  31.8 1.1 %collective-permute-start.11 = (bf16[128,128]{1,0:T(8,128)(2,1)S(1)}, bf16[128,128]{1,0:T(8,128)(2,1)S(1)}, u32[]{:S(2)}, u32[]{:S(2)}) collective-permute-start(bf16[128,128]{1,0:T(8,128)(2,1)S(1)} %get-tuple-element.104), channel_id=1, source_target_pairs={{0,4},{1,5},{2,6},{3,7},{4,8},{5,9},{6,10},{7,11},{8,12},{9,13},{1... | collective-permute-start | bytes 98312 | tf_op jit(solution)/shard_map/ppermute | solution.py:37
  32.9 5.7 %collective-permute-done.11.refs_10_ = bf16[128,128]{1,0:T(8,128)(2,1)S(1)} collective-permute-done((bf16[128,128]{1,0:T(8,128)(2,1)S(1)}, bf16[128,128]{1,0:T(8,128)(2,1)S(1)}, u32[]{:S(2)}, u32[]{:S(2)}) %collective-permute-start.11) | collective-permute-done | bytes 32800 | tf_op jit(solution)/shard_map/ppermute | solution.py:37
  39.1 5.7 %key_terms.1 = (f32[384,128]{1,0:T(8,128)S(1)}, bf16[384,128]{1,0:T(8,128)(2,1)S(1)}, bf16[128,128]{1,0:T(8,128)(2,1)S(1)}, bf16[192,896]{1,0:T(8,128)(2,1)S(1)}, bf16[192,896]{1,0:T(8,128)(2,1)S(1)}) custom-call(bf16[192,896]{1,0:T(8,128)(2,1)S(1)} %get-tuple-element.74.refs_0_, bf16[192,896]{1,0:T(8,128)(2,1)S(1)} %collective-permute-done.2.refs_1_, ...), custom_call_target="tpu_custom_call" | custom-call | tf_op jit(solution)/shard_map/key_terms/pallas_call | solution.py:318
  45.0 1.0 %collective-permute-start.14 = (bf16[448,128]{1,0:T(8,128)(2,1)S(1)}, bf16[448,128]{1,0:T(8,128)(2,1)S(1)}, u32[]{:S(2)}, u32[]{:S(2)}) collective-permute-start(bf16[448,128]{1,0:T(8,128)(2,1)S(1)} %get-tuple-element.118), channel_id=1, source_target_pairs={{0,2},{1,3},{2,0},{3,1},{4,6},{5,7},{6,4},{7,5},{8,10},{9,11},{10,... | collective-permute-start | bytes 344072 | tf_op jit(solution)/shard_map/ppermute | solution.py:46
  46.0 2.5 %collective-permute-start.15 = (bf16[448,128]{1,0:T(8,128)(2,1)S(1)}, bf16[448,128]{1,0:T(8,128)(2,1)S(1)}, u32[]{:S(2)}, u32[]{:S(2)}) collective-permute-start(bf16[448,128]{1,0:T(8,128)(2,1)S(1)} %get-tuple-element.119), channel_id=1, source_target_pairs={{0,6},{1,7},{2,4},{3,5},{4,2},{5,3},{6,0},{7,1},{8,14},{9,15},{10,... | collective-permute-start | bytes 344072 | tf_op jit(solution)/shard_map/ppermute | solution.py:46
  48.5 1.3 %collective-permute-done.13.refs_0_ = bf16[448,128]{1,0:T(8,128)(2,1)S(1)} collective-permute-done((bf16[448,128]{1,0:T(8,128)(2,1)S(1)}, bf16[448,128]{1,0:T(8,128)(2,1)S(1)}, u32[]{:S(2)}, u32[]{:S(2)}) %collective-permute-start.13) | collective-permute-done | bytes 114720 | tf_op jit(solution)/shard_map/ppermute | solution.py:46
  49.9 1.8 %collective-permute-done.15.refs_2_ = bf16[448,128]{1,0:T(8,128)(2,1)S(1)} collective-permute-done((bf16[448,128]{1,0:T(8,128)(2,1)S(1)}, bf16[448,128]{1,0:T(8,128)(2,1)S(1)}, u32[]{:S(2)}, u32[]{:S(2)}) %collective-permute-start.15) | collective-permute-done | bytes 114720 | tf_op jit(solution)/shard_map/ppermute | solution.py:46
  51.8 2.7 %collective-permute-start.17 = (bf16[384,128]{1,0:T(8,128)(2,1)S(1)}, bf16[384,128]{1,0:T(8,128)(2,1)S(1)}, u32[]{:S(2)}, u32[]{:S(2)}) collective-permute-start(bf16[384,128]{1,0:T(8,128)(2,1)S(1)} %get-tuple-element.122), channel_id=1, source_target_pairs={{0,14},{1,15},{2,0},{3,1},{4,2},{5,3},{6,4},{7,5},{8,6},{9,7},{10,... | collective-permute-start | bytes 294920 | tf_op jit(solution)/shard_map/ppermute | solution.py:37
  54.6 1.3 %collective-permute-start.16 = (bf16[224,128]{1,0:T(8,128)(2,1)S(1)}, bf16[224,128]{1,0:T(8,128)(2,1)S(1)}, u32[]{:S(2)}, u32[]{:S(2)}) collective-permute-start(bf16[224,128]{1,0:T(8,128)(2,1)S(1)} %get-tuple-element.121), channel_id=1, source_target_pairs={{0,8},{1,9},{2,10},{3,11},{4,12},{5,13},{6,14},{7,15},{8,0},{9,1},... | collective-permute-start | bytes 172040 | tf_op jit(solution)/shard_map/ppermute | solution.py:46
  55.8 1.0 %collective-permute-start.18 = (bf16[128,128]{1,0:T(8,128)(2,1)S(1)}, bf16[128,128]{1,0:T(8,128)(2,1)S(1)}, u32[]{:S(2)}, u32[]{:S(2)}) collective-permute-start(bf16[128,128]{1,0:T(8,128)(2,1)S(1)} %get-tuple-element.123), channel_id=1, source_target_pairs={{0,12},{1,13},{2,14},{3,15},{4,0},{5,1},{6,2},{7,3},{8,4},{9,5},{1... | collective-permute-start | bytes 98312 | tf_op jit(solution)/shard_map/ppermute | solution.py:37
  56.8 3.1 %collective-permute-done.18.far = bf16[128,128]{1,0:T(8,128)(2,1)S(1)} collective-permute-done((bf16[128,128]{1,0:T(8,128)(2,1)S(1)}, bf16[128,128]{1,0:T(8,128)(2,1)S(1)}, u32[]{:S(2)}, u32[]{:S(2)}) %collective-permute-start.18) | collective-permute-done | bytes 32800 | tf_op jit(solution)/shard_map/ppermute | solution.py:37
  59.9 1.8 %collective-permute-done.16.refs_0_ = bf16[224,128]{1,0:T(8,128)(2,1)S(1)} collective-permute-done((bf16[224,128]{1,0:T(8,128)(2,1)S(1)}, bf16[224,128]{1,0:T(8,128)(2,1)S(1)}, u32[]{:S(2)}, u32[]{:S(2)}) %collective-permute-start.16) | collective-permute-done | bytes 57376 | tf_op jit(solution)/shard_map/ppermute | solution.py:46
  62.5 1.2 %collective-permute-done.21.k_oth = bf16[192,128]{1,0:T(8,128)(2,1)S(1)} collective-permute-done((bf16[192,128]{1,0:T(8,128)(2,1)S(1)}, bf16[192,128]{1,0:T(8,128)(2,1)S(1)}, u32[]{:S(2)}, u32[]{:S(2)}) %collective-permute-start.21) | collective-permute-done | bytes 49184 | tf_op jit(solution)/shard_map/ppermute | solution.py:41
  63.7 3.8 %collective-permute-done.20.second = bf16[224,128]{1,0:T(8,128)(2,1)S(1)} collective-permute-done((bf16[224,128]{1,0:T(8,128)(2,1)S(1)}, bf16[224,128]{1,0:T(8,128)(2,1)S(1)}, u32[]{:S(2)}, u32[]{:S(2)}) %collective-permute-start.20) | collective-permute-done | bytes 57376 | tf_op jit(solution)/shard_map/ppermute | solution.py:46
  68.0 3.1 %collective-permute-start.24 = (bf16[448,128]{1,0:T(8,128)(2,1)S(1)}, bf16[448,128]{1,0:T(8,128)(2,1)S(1)}, u32[]{:S(2)}, u32[]{:S(2)}) collective-permute-start(bf16[448,128]{1,0:T(8,128)(2,1)S(1)} %join.1.refs_0_), channel_id=1, source_target_pairs={{0,6},{1,7},{2,4},{3,5},{4,2},{5,3},{6,0},{7,1},{8,14},{9,15},{10,... | collective-permute-start | bytes 344072 | tf_op jit(solution)/shard_map/ppermute | solution.py:46
  71.1 0.9 %place_tokens.1 = (bf16[192,1792]{1,0:T(8,128)(2,1)}, bf16[192,256]{1,0:T(8,128)(2,1)}) custom-call(bf16[192,896]{1,0:T(8,128)(2,1)S(1)} %get-tuple-element.105.q_own, bf16[192,896]{1,0:T(8,128)(2,1)S(1)} %collective-permute-done.19.q_oth, bf16[192,128]{1,0:T(8,128)(2,1)S(1)} %get-tuple-element.132.k_own, bf16[192,128]{1,0:T(8,128)(2,1)S(1)} %collective-permute-done.21.k_oth), custom_call_target="tpu_custom_call" | custom-call | tf_op jit(solution)/shard_map/place_tokens/pallas_call | solution.py:539
  72.0 0.8 %collective-permute-done.22.refs_1_ = bf16[448,128]{1,0:T(8,128)(2,1)S(1)} collective-permute-done((bf16[448,128]{1,0:T(8,128)(2,1)S(1)}, bf16[448,128]{1,0:T(8,128)(2,1)S(1)}, u32[]{:S(2)}, u32[]{:S(2)}) %collective-permute-start.22) | collective-permute-done | bytes 114720 | tf_op jit(solution)/shard_map/ppermute | solution.py:46
  72.8 1.3 %collective-permute-done.23.refs_2_ = bf16[448,128]{1,0:T(8,128)(2,1)S(1)} collective-permute-done((bf16[448,128]{1,0:T(8,128)(2,1)S(1)}, bf16[448,128]{1,0:T(8,128)(2,1)S(1)}, u32[]{:S(2)}, u32[]{:S(2)}) %collective-permute-start.23) | collective-permute-done | bytes 114720 | tf_op jit(solution)/shard_map/ppermute | solution.py:46
  74.6 0.8 %collective-permute-done.26.refs_5_ = bf16[448,128]{1,0:T(8,128)(2,1)S(1)} collective-permute-done((bf16[448,128]{1,0:T(8,128)(2,1)S(1)}, bf16[448,128]{1,0:T(8,128)(2,1)S(1)}, u32[]{:S(2)}, u32[]{:S(2)}) %collective-permute-start.26) | collective-permute-done | bytes 114720 | tf_op jit(solution)/shard_map/ppermute | solution.py:41
  76.0 1.0 %place_weight.1 = bf16[1792,256]{1,0:T(8,128)(2,1)} custom-call(bf16[448,128]{1,0:T(8,128)(2,1)S(1)} %join.1.refs_0_, bf16[448,128]{1,0:T(8,128)(2,1)S(1)} %collective-permute-done.22.refs_1_, bf16[448,128]{1,0:T(8,128)(2,1)S(1)} %collective-permute-done.23.refs_2_, bf16[448,128]{1,0:T(8,128)(2,1)S(1)} %collective-permute-done.24.refs_3_, ...), custom_call_target="tpu_custom_call" | custom-call | tf_op jit(solution)/shard_map/place_weight/pallas_call | solution.py:515
  (43 shorter events, 6.6 us)
Async XLA Ops:
  0.6 5.2 %copy-start.1 = (bf16[1,192,256]{2,1,0:T(8,128)(2,1)S(1)}, bf16[1,192,256]{2,1,0:T(8,128)(2,1)}, u32[]{:S(2)}) copy-start(bf16[1,192,256]{2,1,0:T(8,128)(2,1)} %param.11) | copy-start | bytes 294916
  0.6 16.2 %copy-start = (bf16[1,192,3584]{2,1,0:T(8,128)(2,1)S(1)}, bf16[1,192,3584]{2,1,0:T(8,128)(2,1)}, u32[]{:S(2)}) copy-start(bf16[1,192,3584]{2,1,0:T(8,128)(2,1)} %param.7) | copy-start | bytes 4128772
  2.3 12.3 %collective-permute-start.2 = (bf16[192,896]{1,0:T(8,128)(2,1)S(1)}, bf16[192,896]{1,0:T(8,128)(2,1)S(1)}, u32[]{:S(2)}, u32[]{:S(2)}) collective-permute-start(bf16[192,896]{1,0:T(8,128)(2,1)S(1)} %get-tuple-element.78), channel_id=1, source_target_pairs={{0,1},{1,0},{2,3},{3,2},{4,5},{5,4},{6,7},{7,6},{8,9},{9,8},{10,11... | collective-permute-start | bytes 1032200 | tf_op jit(solution)/shard_map/ppermute | solution.py:41
  2.9 11.8 %collective-permute-start.3 = (bf16[192,896]{1,0:T(8,128)(2,1)S(1)}, bf16[192,896]{1,0:T(8,128)(2,1)S(1)}, u32[]{:S(2)}, u32[]{:S(2)}) collective-permute-start(bf16[192,896]{1,0:T(8,128)(2,1)S(1)} %get-tuple-element.79), channel_id=1, source_target_pairs={{0,1},{1,0},{2,3},{3,2},{4,5},{5,4},{6,7},{7,6},{8,9},{9,8},{10,11... | collective-permute-start | bytes 1032200 | tf_op jit(solution)/shard_map/ppermute | solution.py:41
  2.9 13.7 %collective-permute-start.6 = (bf16[1792,128]{1,0:T(8,128)(2,1)S(1)}, bf16[1792,128]{1,0:T(8,128)(2,1)S(1)}, u32[]{:S(2)}, u32[]{:S(2)}) collective-permute-start(bf16[1792,128]{1,0:T(8,128)(2,1)S(1)} %get-tuple-element.94.w_own), channel_id=1, source_target_pairs={{0,16},{16,0},{1,17},{17,1},{2,18},{18,2},{3,19},{19,3},{4,20},{20... | collective-permute-start | bytes 1376264 | tf_op jit(solution)/shard_map/ppermute | solution.py:41
  5.9 7.9 %collective-permute-start = (bf16[192,256]{1,0:T(8,128)(2,1)S(1)}, bf16[192,256]{1,0:T(8,128)(2,1)S(1)}, u32[]{:S(2)}, u32[]{:S(2)}) collective-permute-start(bf16[192,256]{1,0:T(8,128)(2,1)S(1)} %bitcast.13), channel_id=1, source_target_pairs={{0,2},{1,3},{2,4},{3,5},{4,6},{5,7},{6,8},{7,9},{8,10},{9,11},{10,... | collective-permute-start | bytes 294920 | tf_op jit(solution)/shard_map/ppermute | solution.py:37
  7.4 0.7 collective-permute-start.1
  8.1 6.6 %collective-permute-start.4 = (s32[15,192]{1,0:T(8,128)S(1)}, s32[15,192]{1,0:T(8,128)S(1)}, u32[]{:S(2)}, u32[]{:S(2)}) collective-permute-start(s32[15,192]{1,0:T(8,128)S(1)} %get-tuple-element.80.refs_6_.l_own), channel_id=1, source_target_pairs={{0,1},{1,0},{2,3},{3,2},{4,5},{5,4},{6,7},{7,6},{8,9},{9,8},{10,11... | collective-permute-start | bytes 34568 | tf_op jit(solution)/shard_map/ppermute | solution.py:41
  15.5 1.4 %collective-permute-start.5 = (bf16[512,128]{1,0:T(8,128)(2,1)S(1)}, bf16[512,128]{1,0:T(8,128)(2,1)S(1)}, u32[]{:S(2)}, u32[]{:S(2)}) collective-permute-start(bf16[512,128]{1,0:T(8,128)(2,1)S(1)} %get-tuple-element.87), channel_id=1, source_target_pairs={{0,1},{1,0},{2,3},{3,2},{4,5},{5,4},{6,7},{7,6},{8,9},{9,8},{10,11... | collective-permute-start | bytes 393224 | tf_op jit(solution)/shard_map/ppermute | solution.py:41
  16.9 8.9 %collective-permute-start.7 = (bf16[192,3584]{1,0:T(8,128)(2,1)S(1)}, bf16[192,3584]{1,0:T(8,128)(2,1)S(1)}, u32[]{:S(2)}, u32[]{:S(2)}) collective-permute-start(bf16[192,3584]{1,0:T(8,128)(2,1)S(1)} %bitcast.7), channel_id=1, source_target_pairs={{0,1},{1,0},{2,3},{3,2},{4,5},{5,4},{6,7},{7,6},{8,9},{9,8},{10,11... | collective-permute-start | bytes 4128776 | tf_op jit(solution)/shard_map/ppermute | solution.py:41
  21.0 8.2 %collective-permute-start.8 = (bf16[384,128]{1,0:T(8,128)(2,1)S(1)}, bf16[384,128]{1,0:T(8,128)(2,1)S(1)}, u32[]{:S(2)}, u32[]{:S(2)}) collective-permute-start(bf16[384,128]{1,0:T(8,128)(2,1)S(1)} %get-tuple-element.100), channel_id=1, source_target_pairs={{0,14},{1,15},{2,0},{3,1},{4,2},{5,3},{6,4},{7,5},{8,6},{9,7},{10,... | collective-permute-start | bytes 294920 | tf_op jit(solution)/shard_map/ppermute | solution.py:37
  25.3 3.9 %collective-permute-start.9 = (bf16[128,128]{1,0:T(8,128)(2,1)S(1)}, bf16[128,128]{1,0:T(8,128)(2,1)S(1)}, u32[]{:S(2)}, u32[]{:S(2)}) collective-permute-start(bf16[128,128]{1,0:T(8,128)(2,1)S(1)} %get-tuple-element.101), channel_id=1, source_target_pairs={{0,12},{1,13},{2,14},{3,15},{4,0},{5,1},{6,2},{7,3},{8,4},{9,5},{1... | collective-permute-start | bytes 98312 | tf_op jit(solution)/shard_map/ppermute | solution.py:37
  30.3 14.6 %collective-permute-start.12 = (bf16[1792,128]{1,0:T(8,128)(2,1)S(1)}, bf16[1792,128]{1,0:T(8,128)(2,1)S(1)}, u32[]{:S(2)}, u32[]{:S(2)}) collective-permute-start(bf16[1792,128]{1,0:T(8,128)(2,1)S(1)} %get-tuple-element.108), channel_id=1, source_target_pairs={{0,16},{1,17},{2,18},{3,19},{4,20},{5,21},{6,22},{7,23},{8,24},{9,... | collective-permute-start | bytes 1376264 | tf_op jit(solution)/shard_map/ppermute | solution.py:46
  31.8 7.3 %collective-permute-start.10 = (bf16[384,128]{1,0:T(8,128)(2,1)S(1)}, bf16[384,128]{1,0:T(8,128)(2,1)S(1)}, u32[]{:S(2)}, u32[]{:S(2)}) collective-permute-start(bf16[384,128]{1,0:T(8,128)(2,1)S(1)} %get-tuple-element.103.refs_8_), channel_id=1, source_target_pairs={{0,2},{1,3},{2,4},{3,5},{4,6},{5,7},{6,8},{7,9},{8,10},{9,11},{10,... | collective-permute-start | bytes 294920 | tf_op jit(solution)/shard_map/ppermute | solution.py:37
  31.8 6.8 %collective-permute-start.11 = (bf16[128,128]{1,0:T(8,128)(2,1)S(1)}, bf16[128,128]{1,0:T(8,128)(2,1)S(1)}, u32[]{:S(2)}, u32[]{:S(2)}) collective-permute-start(bf16[128,128]{1,0:T(8,128)(2,1)S(1)} %get-tuple-element.104), channel_id=1, source_target_pairs={{0,4},{1,5},{2,6},{3,7},{4,8},{5,9},{6,10},{7,11},{8,12},{9,13},{1... | collective-permute-start | bytes 98312 | tf_op jit(solution)/shard_map/ppermute | solution.py:37
  44.9 4.9 %collective-permute-start.13 = (bf16[448,128]{1,0:T(8,128)(2,1)S(1)}, bf16[448,128]{1,0:T(8,128)(2,1)S(1)}, u32[]{:S(2)}, u32[]{:S(2)}) collective-permute-start(bf16[448,128]{1,0:T(8,128)(2,1)S(1)} %get-tuple-element.117), channel_id=1, source_target_pairs={{0,4},{1,5},{2,6},{3,7},{4,0},{5,1},{6,2},{7,3},{8,12},{9,13},{10,... | collective-permute-start | bytes 344072 | tf_op jit(solution)/shard_map/ppermute | solution.py:46
  45.0 4.9 %collective-permute-start.14 = (bf16[448,128]{1,0:T(8,128)(2,1)S(1)}, bf16[448,128]{1,0:T(8,128)(2,1)S(1)}, u32[]{:S(2)}, u32[]{:S(2)}) collective-permute-start(bf16[448,128]{1,0:T(8,128)(2,1)S(1)} %get-tuple-element.118), channel_id=1, source_target_pairs={{0,2},{1,3},{2,0},{3,1},{4,6},{5,7},{6,4},{7,5},{8,10},{9,11},{10,... | collective-permute-start | bytes 344072 | tf_op jit(solution)/shard_map/ppermute | solution.py:46
  46.0 5.7 %collective-permute-start.15 = (bf16[448,128]{1,0:T(8,128)(2,1)S(1)}, bf16[448,128]{1,0:T(8,128)(2,1)S(1)}, u32[]{:S(2)}, u32[]{:S(2)}) collective-permute-start(bf16[448,128]{1,0:T(8,128)(2,1)S(1)} %get-tuple-element.119), channel_id=1, source_target_pairs={{0,6},{1,7},{2,4},{3,5},{4,2},{5,3},{6,0},{7,1},{8,14},{9,15},{10,... | collective-permute-start | bytes 344072 | tf_op jit(solution)/shard_map/ppermute | solution.py:46
  51.8 10.0 %collective-permute-start.19 = (bf16[192,896]{1,0:T(8,128)(2,1)S(1)}, bf16[192,896]{1,0:T(8,128)(2,1)S(1)}, u32[]{:S(2)}, u32[]{:S(2)}) collective-permute-start(bf16[192,896]{1,0:T(8,128)(2,1)S(1)} %get-tuple-element.124), channel_id=1, source_target_pairs={{0,1},{1,0},{2,3},{3,2},{4,5},{5,4},{6,7},{7,6},{8,9},{9,8},{10,11... | collective-permute-start | bytes 1032200 | tf_op jit(solution)/shard_map/ppermute | solution.py:41
  51.8 8.1 %collective-permute-start.17 = (bf16[384,128]{1,0:T(8,128)(2,1)S(1)}, bf16[384,128]{1,0:T(8,128)(2,1)S(1)}, u32[]{:S(2)}, u32[]{:S(2)}) collective-permute-start(bf16[384,128]{1,0:T(8,128)(2,1)S(1)} %get-tuple-element.122), channel_id=1, source_target_pairs={{0,14},{1,15},{2,0},{3,1},{4,2},{5,3},{6,4},{7,5},{8,6},{9,7},{10,... | collective-permute-start | bytes 294920 | tf_op jit(solution)/shard_map/ppermute | solution.py:37
  54.6 7.2 %collective-permute-start.16 = (bf16[224,128]{1,0:T(8,128)(2,1)S(1)}, bf16[224,128]{1,0:T(8,128)(2,1)S(1)}, u32[]{:S(2)}, u32[]{:S(2)}) collective-permute-start(bf16[224,128]{1,0:T(8,128)(2,1)S(1)} %get-tuple-element.121), channel_id=1, source_target_pairs={{0,8},{1,9},{2,10},{3,11},{4,12},{5,13},{6,14},{7,15},{8,0},{9,1},... | collective-permute-start | bytes 172040 | tf_op jit(solution)/shard_map/ppermute | solution.py:46
  55.8 4.1 %collective-permute-start.18 = (bf16[128,128]{1,0:T(8,128)(2,1)S(1)}, bf16[128,128]{1,0:T(8,128)(2,1)S(1)}, u32[]{:S(2)}, u32[]{:S(2)}) collective-permute-start(bf16[128,128]{1,0:T(8,128)(2,1)S(1)} %get-tuple-element.123), channel_id=1, source_target_pairs={{0,12},{1,13},{2,14},{3,15},{4,0},{5,1},{6,2},{7,3},{8,4},{9,5},{1... | collective-permute-start | bytes 98312 | tf_op jit(solution)/shard_map/ppermute | solution.py:37
  61.8 5.8 %collective-permute-start.20 = (bf16[224,128]{1,0:T(8,128)(2,1)S(1)}, bf16[224,128]{1,0:T(8,128)(2,1)S(1)}, u32[]{:S(2)}, u32[]{:S(2)}) collective-permute-start(bf16[224,128]{1,0:T(8,128)(2,1)S(1)} %reduce_step.5.first), channel_id=1, source_target_pairs={{0,8},{1,9},{2,10},{3,11},{4,12},{5,13},{6,14},{7,15},{8,0},{9,1},... | collective-permute-start | bytes 172040 | tf_op jit(solution)/shard_map/ppermute | solution.py:46
  62.4 1.3 %collective-permute-start.21 = (bf16[192,128]{1,0:T(8,128)(2,1)S(1)}, bf16[192,128]{1,0:T(8,128)(2,1)S(1)}, u32[]{:S(2)}, u32[]{:S(2)}) collective-permute-start(bf16[192,128]{1,0:T(8,128)(2,1)S(1)} %get-tuple-element.134), channel_id=1, source_target_pairs={{0,1},{1,0},{2,3},{3,2},{4,5},{5,4},{6,7},{7,6},{8,9},{9,8},{10,11... | collective-permute-start | bytes 147464 | tf_op jit(solution)/shard_map/ppermute | solution.py:41
  67.6 5.3 %collective-permute-start.22 = (bf16[448,128]{1,0:T(8,128)(2,1)S(1)}, bf16[448,128]{1,0:T(8,128)(2,1)S(1)}, u32[]{:S(2)}, u32[]{:S(2)}) collective-permute-start(bf16[448,128]{1,0:T(8,128)(2,1)S(1)} %join.1.refs_0_), channel_id=1, source_target_pairs={{0,4},{1,5},{2,6},{3,7},{4,0},{5,1},{6,2},{7,3},{8,12},{9,13},{10,... | collective-permute-start | bytes 344072 | tf_op jit(solution)/shard_map/ppermute | solution.py:46
  68.0 6.1 %collective-permute-start.23 = (bf16[448,128]{1,0:T(8,128)(2,1)S(1)}, bf16[448,128]{1,0:T(8,128)(2,1)S(1)}, u32[]{:S(2)}, u32[]{:S(2)}) collective-permute-start(bf16[448,128]{1,0:T(8,128)(2,1)S(1)} %join.1.refs_0_), channel_id=1, source_target_pairs={{0,2},{1,3},{2,0},{3,1},{4,6},{5,7},{6,4},{7,5},{8,10},{9,11},{10,... | collective-permute-start | bytes 344072 | tf_op jit(solution)/shard_map/ppermute | solution.py:46
  68.0 6.1 %collective-permute-start.24 = (bf16[448,128]{1,0:T(8,128)(2,1)S(1)}, bf16[448,128]{1,0:T(8,128)(2,1)S(1)}, u32[]{:S(2)}, u32[]{:S(2)}) collective-permute-start(bf16[448,128]{1,0:T(8,128)(2,1)S(1)} %join.1.refs_0_), channel_id=1, source_target_pairs={{0,6},{1,7},{2,4},{3,5},{4,2},{5,3},{6,0},{7,1},{8,14},{9,15},{10,... | collective-permute-start | bytes 344072 | tf_op jit(solution)/shard_map/ppermute | solution.py:46
  71.1 3.5 %collective-permute-start.25 = (bf16[448,128]{1,0:T(8,128)(2,1)S(1)}, bf16[448,128]{1,0:T(8,128)(2,1)S(1)}, u32[]{:S(2)}, u32[]{:S(2)}) collective-permute-start(bf16[448,128]{1,0:T(8,128)(2,1)S(1)} %join.1.refs_0_), channel_id=1, source_target_pairs={{0,1},{1,0},{2,3},{3,2},{4,5},{5,4},{6,7},{7,6},{8,9},{9,8},{10,11... | collective-permute-start | bytes 344072 | tf_op jit(solution)/shard_map/ppermute | solution.py:41
  74.1 1.3 %collective-permute-start.26 = (bf16[448,128]{1,0:T(8,128)(2,1)S(1)}, bf16[448,128]{1,0:T(8,128)(2,1)S(1)}, u32[]{:S(2)}, u32[]{:S(2)}) collective-permute-start(bf16[448,128]{1,0:T(8,128)(2,1)S(1)} %collective-permute-done.22.refs_1_), channel_id=1, source_target_pairs={{0,1},{1,0},{2,3},{3,2},{4,5},{5,4},{6,7},{7,6},{8,9},{9,8},{10,11... | collective-permute-start | bytes 344072 | tf_op jit(solution)/shard_map/ppermute | solution.py:41
  74.1 1.5 %collective-permute-start.27 = (bf16[448,128]{1,0:T(8,128)(2,1)S(1)}, bf16[448,128]{1,0:T(8,128)(2,1)S(1)}, u32[]{:S(2)}, u32[]{:S(2)}) collective-permute-start(bf16[448,128]{1,0:T(8,128)(2,1)S(1)} %collective-permute-done.23.refs_2_), channel_id=1, source_target_pairs={{0,1},{1,0},{2,3},{3,2},{4,5},{5,4},{6,7},{7,6},{8,9},{9,8},{10,11... | collective-permute-start | bytes 344072 | tf_op jit(solution)/shard_map/ppermute | solution.py:41
  74.6 1.3 %collective-permute-start.28 = (bf16[448,128]{1,0:T(8,128)(2,1)S(1)}, bf16[448,128]{1,0:T(8,128)(2,1)S(1)}, u32[]{:S(2)}, u32[]{:S(2)}) collective-permute-start(bf16[448,128]{1,0:T(8,128)(2,1)S(1)} %collective-permute-done.24.refs_3_), channel_id=1, source_target_pairs={{0,1},{1,0},{2,3},{3,2},{4,5},{5,4},{6,7},{7,6},{8,9},{9,8},{10,11... | collective-permute-start | bytes 344072 | tf_op jit(solution)/shard_map/ppermute | solution.py:41

commit v5 on v4

--- a/solution.py
+++ b/solution.py
@@ -452,10 +452,14 @@
     )(spiked, *terms)
 
 
-def reduce_kernel(count, held, *refs):
-    total = held[...]
+def reduce_kernel(count, turned, held, *refs):
+    total = held[...].astype(f32)
     for got in refs[:count]:
-        total = total + got[...].astype(f32)
+        term = got[...].astype(f32)
+        if turned:
+            half = term.shape[0] // 2
+            term = jnp.concatenate([term[half:], term[:half]], axis=0)
+        total = total + term
     outs = refs[count:]
     rows = total.shape[0] // len(outs)
     outs[0][...] = total[:rows].astype(outs[0].dtype)
@@ -463,36 +467,19 @@
         outs[part][...] = total[part * rows : (part + 1) * rows].astype(bf16)
 
 
-def reduce_step(held, got, parts):
+def reduce_step(held, got, parts, turned=False):
     rows = held.shape[0] // parts
     shapes = [jax.ShapeDtypeStruct((rows, HD), bf16)] * parts
     if parts > 1:
         shapes[0] = jax.ShapeDtypeStruct((rows, HD), f32)
     return pl.pallas_call(
-        functools.partial(reduce_kernel, len(got)),
+        functools.partial(reduce_kernel, len(got), turned),
         out_shape=shapes,
         in_specs=[VMEM] * (1 + len(got)),
         out_specs=[VMEM] * parts,
         compiler_params=limit(6),
         name="reduce_step",
     )(held, *got)
-
-
-def join_kernel(first, second, out):
-    rows = first.shape[0]
-    out[:rows, :] = first[...]
-    out[rows:, :] = second[...]
-
-
-def join(first, second):
-    return pl.pallas_call(
-        join_kernel,
-        out_shape=jax.ShapeDtypeStruct((2 * first.shape[0], HD), bf16),
-        in_specs=[VMEM] * 2,
-        out_specs=VMEM,
-        compiler_params=limit(4),
-        name="join",
-    )(first, second)
 
 
 def place_weight_kernel(*refs):
@@ -627,20 +614,16 @@
         got = [crossed(send, flip) for send, flip in zip(sends, (4, 2, 6))]
     near_k, far_k = shifted(near_k, -2), shifted(far_k, -4)
     if fast:
-        keep, send = reduce_step(keep, got, 2)
-        query_out, send = lax.optimization_barrier((query_out, send))
-        got = crossed(send, 8)
+        (part,) = reduce_step(keep, got, 1)
+        query_out, part = lax.optimization_barrier((query_out, part))
+        got = crossed(part, 8)
     query_got = swapped(query_out, "seq", 1)
     if fast:
         got, near_k, far_k, query_got = lax.optimization_barrier((got, near_k, far_k, query_got))
-        (owned,) = reduce_step(keep, [got], 1)
+        (owned,) = reduce_step(part, [got], 1, turned=True)
         near_k, owned = lax.optimization_barrier((near_k, owned))
     key_mine, key_out = sum_keys(tok, own_k, near_k, far_k)
     key_got = swapped(key_out, "seq", 1)
-    if fast:
-        got, key_got = lax.optimization_barrier((crossed(owned, 8), key_got))
-        owned = join(owned, got)
-        key_got, owned = lax.optimization_barrier((key_got, owned))
     query_grad, key_grad = place_tokens(query_mine, query_got, key_mine, key_got)
     if fast:
         pieces = [crossed(owned, flip) for flip in (4, 2, 6)]

time: 77.4 us -> 74.5 us (0.963)
  waiting for transfers between devices: 26.2 us -> 22.7 us
    ppermute x9 -> x8, waiting for transfers between devices: 11 us -> 6.45 us  [crossed(): lax.ppermute(value, ('dp', 'seq'), [(i, i ^ flip) for i in range(count)])]
    ppermute x8, waiting for transfers between devices: 10.8 us -> 12.4 us  [shifted(): return lax.ppermute(value, 'seq', pairs)]
    ppermute x9 -> x8, starting transfers between devices: 10.5 us -> 11.9 us  [crossed(): lax.ppermute(value, ('dp', 'seq'), [(i, i ^ flip) for i in range(count)])]
    ppermute x8, starting transfers between devices: 11.7 us -> 10.4 us  [shifted(): return lax.ppermute(value, 'seq', pairs)]
  transfers between devices with their start and end apart: 29 -> 28, of which waited for: 18 -> 15; matrix products, arithmetic and copies ran while one was open for 0% -> 0% of each run, Pallas kernels for 17% -> 18%
where the time goes in v5:
time: 74.5 us; the launch traced here: 74.3 us
  starting transfers between devices  33.5 us (45%)
  waiting for transfers between devices  22.7 us (30%)
  Pallas kernels  17.2 us (23%)
  between operations  0.95 us (1%)
    ppermute x8, waiting for transfers between devices, shifted(): return lax.ppermute(value, 'seq', pairs)  12.4 us
    ppermute x8, starting transfers between devices, crossed(): lax.ppermute(value, ('dp', 'seq'), [(i, i ^ flip) for i in range(count)])  11.9 us
    ppermute x12, starting transfers between devices, swapped(): lax.ppermute(value, axis, [(i, i ^ flip) for i in range(lax.axis_size(axi...  11.1 us
    ppermute x8, starting transfers between devices, shifted(): return lax.ppermute(value, 'seq', pairs)  10.4 us
    ppermute x8, waiting for transfers between devices, crossed(): lax.ppermute(value, ('dp', 'seq'), [(i, i ^ flip) for i in range(count)])  6.45 us
    pallas_call x1, Pallas kernels, key_terms(): pl.pallas_call(functools.partial(key_kernel, tok), out_shape=term_shapes(...  5.73 us
    ppermute x12, waiting for transfers between devices, swapped(): lax.ppermute(value, axis, [(i, i ^ flip) for i in range(lax.axis_size(axi...  3.89 us
    pallas_call x1, Pallas kernels, value_terms(): pl.pallas_call(functools.partial(value_kernel, tok), out_shape=term_shape...  3.81 us
  transfers between devices with their start and end apart: 28, of which 15 were waited for; matrix products, arithmetic and copies ran while one was open for 0% of the time, Pallas kernels for 18%

profile of v5, /device:TPU:0, one launch (start us, length us, event | category | flops | bytes accessed | tf_op | source)
XLA Modules:
  0.0 74.3 jit_solution(14566659348874525675)
XLA Ops:
  0.7 1.7 %split.1 = (bf16[192,896]{1,0:T(8,128)(2,1)S(1)}, bf16[192,896]{1,0:T(8,128)(2,1)S(1)}, bf16[192,896]{1,0:T(8,128)(2,1)S(1)}, bf16[192,896]{1,0:T(8,128)(2,1)S(1...) custom-call(bf16[192,1792]{1,0:T(8,128)(2,1)} %bitcast.9, ...), custom_call_target="tpu_custom_call" | custom-call | tf_op jit(solution)/shard_map/split/pallas_call | solution.py:92
  2.3 0.5 collective-permute-start.2
  2.9 2.9 %collective-permute-start.6 = (bf16[1792,128]{1,0:T(8,128)(2,1)S(1)}, bf16[1792,128]{1,0:T(8,128)(2,1)S(1)}, u32[]{:S(2)}, u32[]{:S(2)}) collective-permute-start(bf16[1792,128]{1,0:T(8,128)(2,1)S(1)} %get-tuple-element.88.w_own), channel_id=1, source_target_pairs={{0,16},{16,0},{1,17},{17,1},{2,18},{18,2},{3,19},{19,3},{4,20},{20... | collective-permute-start | bytes 1376264 | tf_op jit(solution)/shard_map/ppermute | solution.py:41
  5.9 1.5 %collective-permute-start = (bf16[192,256]{1,0:T(8,128)(2,1)S(1)}, bf16[192,256]{1,0:T(8,128)(2,1)S(1)}, u32[]{:S(2)}, u32[]{:S(2)}) collective-permute-start(bf16[192,256]{1,0:T(8,128)(2,1)S(1)} %bitcast.13), channel_id=1, source_target_pairs={{0,2},{1,3},{2,4},{3,5},{4,6},{5,7},{6,8},{7,9},{8,10},{9,11},{10,... | collective-permute-start | bytes 294920 | tf_op jit(solution)/shard_map/ppermute | solution.py:37
  7.4 0.7 collective-permute-start.1
  8.1 5.7 %collective-permute-start.4 = (s32[15,192]{1,0:T(8,128)S(1)}, s32[15,192]{1,0:T(8,128)S(1)}, u32[]{:S(2)}, u32[]{:S(2)}) collective-permute-start(s32[15,192]{1,0:T(8,128)S(1)} %get-tuple-element.74.refs_6_.l_own), channel_id=1, source_target_pairs={{0,1},{1,0},{2,3},{3,2},{4,5},{5,4},{6,7},{7,6},{8,9},{9,8},{10,11... | collective-permute-start | bytes 34568 | tf_op jit(solution)/shard_map/ppermute | solution.py:41
  13.8 0.8 %collective-permute-done.4.refs_7_.l_oth = s32[15,192]{1,0:T(8,128)S(1)} collective-permute-done((s32[15,192]{1,0:T(8,128)S(1)}, s32[15,192]{1,0:T(8,128)S(1)}, u32[]{:S(2)}, u32[]{:S(2)}) %collective-permute-start.4) | collective-permute-done | bytes 11552 | tf_op jit(solution)/shard_map/ppermute | solution.py:41
  14.6 0.8 %pack.1 = (bf16[512,128]{1,0:T(8,128)(2,1)S(1)}, bf16[512,128]{1,0:T(8,128)(2,1)S(1)}) custom-call(bf16[192,256]{1,0:T(8,128)(2,1)} %bitcast.12, bf16[192,256]{1,0:T(8,128)(2,1)S(1)} %collective-permute-done.near, bf16[128,256]{1,0:T(8,128)(2,1)S(1)} %collective-permute-done.1.far), custom_call_target="tpu_custom_call" | custom-call | tf_op jit(solution)/shard_map/pack/pallas_call | solution.py:131
  15.9 0.7 %collective-permute-done.6.w_oth = bf16[1792,128]{1,0:T(8,128)(2,1)S(1)} collective-permute-done((bf16[1792,128]{1,0:T(8,128)(2,1)S(1)}, bf16[1792,128]{1,0:T(8,128)(2,1)S(1)}, u32[]{:S(2)}, u32[]{:S(2)}) %collective-permute-start.6) | collective-permute-done | bytes 458784 | tf_op jit(solution)/shard_map/ppermute | solution.py:41
  17.2 3.8 %value_terms.1 = (f32[384,128]{1,0:T(8,128)S(1)}, bf16[384,128]{1,0:T(8,128)(2,1)S(1)}, bf16[128,128]{1,0:T(8,128)(2,1)S(1)}, f32[21,128]{1,0:T(8,128)S(1)}, f32[21,128]{1,0:T(8,128)S(1)}) custom-call(bf16[192,896]{1,0:T(8,128)(2,1)S(1)} %get-tuple-element.68.refs_0_, bf16[192,896]{1,0:T(8,128)(2,1)S(1)} %collective-permute-done.2.refs_1_, ...), custom_call_target="tpu_custom_call" | custom-call | tf_op jit(solution)/shard_map/value_terms/pallas_call | solution.py:301
  21.0 4.3 %collective-permute-start.8 = (bf16[384,128]{1,0:T(8,128)(2,1)S(1)}, bf16[384,128]{1,0:T(8,128)(2,1)S(1)}, u32[]{:S(2)}, u32[]{:S(2)}) collective-permute-start(bf16[384,128]{1,0:T(8,128)(2,1)S(1)} %get-tuple-element.94), channel_id=1, source_target_pairs={{0,14},{1,15},{2,0},{3,1},{4,2},{5,3},{6,4},{7,5},{8,6},{9,7},{10,... | collective-permute-start | bytes 294920 | tf_op jit(solution)/shard_map/ppermute | solution.py:37
  25.8 2.0 %project.1 = (bf16[384,128]{1,0:T(8,128)(2,1)S(1)}, bf16[128,128]{1,0:T(8,128)(2,1)S(1)}, bf16[384,3584]{1,0:T(8,128)(2,1)S(1)}) custom-call(bf16[192,3584]{1,0:T(8,128)(2,1)S(1)} %bitcast.8, bf16[192,3584]{1,0:T(8,128)(2,1)S(1)} %collective-permute-done.7.h_oth, s32[15,192]{1,0:T(8,128)S(1)} %get-tuple-element.74.refs_6_.l_own, ...), custom_call_target="tpu_custom_call" | custom-call | tf_op jit(solution)/shard_map/project/pallas_call | solution.py:389
  27.7 1.5 %collective-permute-done.9.far = bf16[128,128]{1,0:T(8,128)(2,1)S(1)} collective-permute-done((bf16[128,128]{1,0:T(8,128)(2,1)S(1)}, bf16[128,128]{1,0:T(8,128)(2,1)S(1)}, u32[]{:S(2)}, u32[]{:S(2)}) %collective-permute-start.9) | collective-permute-done | bytes 32800 | tf_op jit(solution)/shard_map/ppermute | solution.py:37
  29.2 1.0 %weight_terms.1 = (f32[1792,128]{1,0:T(8,128)S(1)}, bf16[1792,128]{1,0:T(8,128)(2,1)S(1)}) custom-call(bf16[384,3584]{1,0:T(8,128)(2,1)S(1)} %get-tuple-element.92.spiked, f32[384,128]{1,0:T(8,128)S(1)} %get-tuple-element.93.own, bf16[384,128]{1,0:T(8,128)(2,1)S(1)} %collective-permute-done.8.near, bf16[128,128]{1,0:T(8,128)(2,1)S(1)} %collective-permute-done.9.far), custom_call_target="tpu_custom_call" | custom-call | tf_op jit(solution)/shard_map/weight_terms/pallas_call | solution.py:441
  30.3 1.6 %collective-permute-start.12 = (bf16[1792,128]{1,0:T(8,128)(2,1)S(1)}, bf16[1792,128]{1,0:T(8,128)(2,1)S(1)}, u32[]{:S(2)}, u32[]{:S(2)}) collective-permute-start(bf16[1792,128]{1,0:T(8,128)(2,1)S(1)} %get-tuple-element.102), channel_id=1, source_target_pairs={{0,16},{1,17},{2,18},{3,19},{4,20},{5,21},{6,22},{7,23},{8,24},{9,... | collective-permute-start | bytes 1376264 | tf_op jit(solution)/shard_map/ppermute | solution.py:46
  31.8 1.1 %collective-permute-start.11 = (bf16[128,128]{1,0:T(8,128)(2,1)S(1)}, bf16[128,128]{1,0:T(8,128)(2,1)S(1)}, u32[]{:S(2)}, u32[]{:S(2)}) collective-permute-start(bf16[128,128]{1,0:T(8,128)(2,1)S(1)} %get-tuple-element.98), channel_id=1, source_target_pairs={{0,4},{1,5},{2,6},{3,7},{4,8},{5,9},{6,10},{7,11},{8,12},{9,13},{1... | collective-permute-start | bytes 98312 | tf_op jit(solution)/shard_map/ppermute | solution.py:37
  32.9 5.7 %collective-permute-done.11.refs_10_ = bf16[128,128]{1,0:T(8,128)(2,1)S(1)} collective-permute-done((bf16[128,128]{1,0:T(8,128)(2,1)S(1)}, bf16[128,128]{1,0:T(8,128)(2,1)S(1)}, u32[]{:S(2)}, u32[]{:S(2)}) %collective-permute-start.11) | collective-permute-done | bytes 32800 | tf_op jit(solution)/shard_map/ppermute | solution.py:37
  39.1 5.7 %key_terms.1 = (f32[384,128]{1,0:T(8,128)S(1)}, bf16[384,128]{1,0:T(8,128)(2,1)S(1)}, bf16[128,128]{1,0:T(8,128)(2,1)S(1)}, bf16[192,896]{1,0:T(8,128)(2,1)S(1)}, bf16[192,896]{1,0:T(8,128)(2,1)S(1)}) custom-call(bf16[192,896]{1,0:T(8,128)(2,1)S(1)} %get-tuple-element.68.refs_0_, bf16[192,896]{1,0:T(8,128)(2,1)S(1)} %collective-permute-done.2.refs_1_, ...), custom_call_target="tpu_custom_call" | custom-call | tf_op jit(solution)/shard_map/key_terms/pallas_call | solution.py:318
  45.0 1.0 %collective-permute-start.14 = (bf16[448,128]{1,0:T(8,128)(2,1)S(1)}, bf16[448,128]{1,0:T(8,128)(2,1)S(1)}, u32[]{:S(2)}, u32[]{:S(2)}) collective-permute-start(bf16[448,128]{1,0:T(8,128)(2,1)S(1)} %get-tuple-element.112), channel_id=1, source_target_pairs={{0,2},{1,3},{2,0},{3,1},{4,6},{5,7},{6,4},{7,5},{8,10},{9,11},{10,... | collective-permute-start | bytes 344072 | tf_op jit(solution)/shard_map/ppermute | solution.py:46
  46.0 2.5 %collective-permute-start.15 = (bf16[448,128]{1,0:T(8,128)(2,1)S(1)}, bf16[448,128]{1,0:T(8,128)(2,1)S(1)}, u32[]{:S(2)}, u32[]{:S(2)}) collective-permute-start(bf16[448,128]{1,0:T(8,128)(2,1)S(1)} %get-tuple-element.113), channel_id=1, source_target_pairs={{0,6},{1,7},{2,4},{3,5},{4,2},{5,3},{6,0},{7,1},{8,14},{9,15},{10,... | collective-permute-start | bytes 344072 | tf_op jit(solution)/shard_map/ppermute | solution.py:46
  48.5 1.3 %collective-permute-done.13.refs_0_ = bf16[448,128]{1,0:T(8,128)(2,1)S(1)} collective-permute-done((bf16[448,128]{1,0:T(8,128)(2,1)S(1)}, bf16[448,128]{1,0:T(8,128)(2,1)S(1)}, u32[]{:S(2)}, u32[]{:S(2)}) %collective-permute-start.13) | collective-permute-done | bytes 114720 | tf_op jit(solution)/shard_map/ppermute | solution.py:46
  49.9 1.8 %collective-permute-done.15.refs_2_ = bf16[448,128]{1,0:T(8,128)(2,1)S(1)} collective-permute-done((bf16[448,128]{1,0:T(8,128)(2,1)S(1)}, bf16[448,128]{1,0:T(8,128)(2,1)S(1)}, u32[]{:S(2)}, u32[]{:S(2)}) %collective-permute-start.15) | collective-permute-done | bytes 114720 | tf_op jit(solution)/shard_map/ppermute | solution.py:46
  51.9 2.5 %collective-permute-start.16 = (bf16[448,128]{1,0:T(8,128)(2,1)S(1)}, bf16[448,128]{1,0:T(8,128)(2,1)S(1)}, u32[]{:S(2)}, u32[]{:S(2)}) collective-permute-start(bf16[448,128]{1,0:T(8,128)(2,1)S(1)} %reduce_step.4.held), channel_id=1, source_target_pairs={{0,8},{1,9},{2,10},{3,11},{4,12},{5,13},{6,14},{7,15},{8,0},{9,1},... | collective-permute-start | bytes 344072 | tf_op jit(solution)/shard_map/ppermute | solution.py:46
  54.4 2.4 %collective-permute-start.17 = (bf16[384,128]{1,0:T(8,128)(2,1)S(1)}, bf16[384,128]{1,0:T(8,128)(2,1)S(1)}, u32[]{:S(2)}, u32[]{:S(2)}) collective-permute-start(bf16[384,128]{1,0:T(8,128)(2,1)S(1)} %get-tuple-element.115), channel_id=1, source_target_pairs={{0,14},{1,15},{2,0},{3,1},{4,2},{5,3},{6,4},{7,5},{8,6},{9,7},{10,... | collective-permute-start | bytes 294920 | tf_op jit(solution)/shard_map/ppermute | solution.py:37
  56.8 4.6 %collective-permute-done.18.far = bf16[128,128]{1,0:T(8,128)(2,1)S(1)} collective-permute-done((bf16[128,128]{1,0:T(8,128)(2,1)S(1)}, bf16[128,128]{1,0:T(8,128)(2,1)S(1)}, u32[]{:S(2)}, u32[]{:S(2)}) %collective-permute-start.18) | collective-permute-done | bytes 32800 | tf_op jit(solution)/shard_map/ppermute | solution.py:37
  61.5 2.7 %collective-permute-start.21 = (bf16[448,128]{1,0:T(8,128)(2,1)S(1)}, bf16[448,128]{1,0:T(8,128)(2,1)S(1)}, u32[]{:S(2)}, u32[]{:S(2)}) collective-permute-start(bf16[448,128]{1,0:T(8,128)(2,1)S(1)} %reduce_step.5.refs_0_), channel_id=1, source_target_pairs={{0,4},{1,5},{2,6},{3,7},{4,0},{5,1},{6,2},{7,3},{8,12},{9,13},{10,... | collective-permute-start | bytes 344072 | tf_op jit(solution)/shard_map/ppermute | solution.py:46
  64.3 1.1 %collective-permute-start.22 = (bf16[448,128]{1,0:T(8,128)(2,1)S(1)}, bf16[448,128]{1,0:T(8,128)(2,1)S(1)}, u32[]{:S(2)}, u32[]{:S(2)}) collective-permute-start(bf16[448,128]{1,0:T(8,128)(2,1)S(1)} %reduce_step.5.refs_0_), channel_id=1, source_target_pairs={{0,2},{1,3},{2,0},{3,1},{4,6},{5,7},{6,4},{7,5},{8,10},{9,11},{10,... | collective-permute-start | bytes 344072 | tf_op jit(solution)/shard_map/ppermute | solution.py:46
  66.4 0.7 collective-permute-done.20.k_oth
  67.1 0.9 %place_tokens.1 = (bf16[192,1792]{1,0:T(8,128)(2,1)}, bf16[192,256]{1,0:T(8,128)(2,1)}) custom-call(bf16[192,896]{1,0:T(8,128)(2,1)S(1)} %get-tuple-element.99.q_own, bf16[192,896]{1,0:T(8,128)(2,1)S(1)} %collective-permute-done.19.q_oth, bf16[192,128]{1,0:T(8,128)(2,1)S(1)} %get-tuple-element.124.k_own, bf16[192,128]{1,0:T(8,128)(2,1)S(1)} %collective-permute-done.20.k_oth), custom_call_target="tpu_custom_call" | custom-call | tf_op jit(solution)/shard_map/place_tokens/pallas_call | solution.py:526
  68.1 3.2 %collective-permute-done.22.refs_2_ = bf16[448,128]{1,0:T(8,128)(2,1)S(1)} collective-permute-done((bf16[448,128]{1,0:T(8,128)(2,1)S(1)}, bf16[448,128]{1,0:T(8,128)(2,1)S(1)}, u32[]{:S(2)}, u32[]{:S(2)}) %collective-permute-start.22) | collective-permute-done | bytes 114720 | tf_op jit(solution)/shard_map/ppermute | solution.py:46
  71.8 0.8 %collective-permute-done.25.refs_5_ = bf16[448,128]{1,0:T(8,128)(2,1)S(1)} collective-permute-done((bf16[448,128]{1,0:T(8,128)(2,1)S(1)}, bf16[448,128]{1,0:T(8,128)(2,1)S(1)}, u32[]{:S(2)}, u32[]{:S(2)}) %collective-permute-start.25) | collective-permute-done | bytes 114720 | tf_op jit(solution)/shard_map/ppermute | solution.py:41
  73.1 1.0 %place_weight.1 = bf16[1792,256]{1,0:T(8,128)(2,1)} custom-call(bf16[448,128]{1,0:T(8,128)(2,1)S(1)} %reduce_step.5.refs_0_, bf16[448,128]{1,0:T(8,128)(2,1)S(1)} %collective-permute-done.21.refs_1_, bf16[448,128]{1,0:T(8,128)(2,1)S(1)} %collective-permute-done.22.refs_2_, bf16[448,128]{1,0:T(8,128)(2,1)S(1)} %collective-permute-done.23.refs_3_, ...), custom_call_target="tpu_custom_call" | custom-call | tf_op jit(solution)/shard_map/place_weight/pallas_call | solution.py:502
  (40 shorter events, 4.6 us)
Async XLA Ops:
  0.6 5.2 %copy-start.1 = (bf16[1,192,256]{2,1,0:T(8,128)(2,1)S(1)}, bf16[1,192,256]{2,1,0:T(8,128)(2,1)}, u32[]{:S(2)}) copy-start(bf16[1,192,256]{2,1,0:T(8,128)(2,1)} %param.11) | copy-start | bytes 294916
  0.6 16.2 %copy-start = (bf16[1,192,3584]{2,1,0:T(8,128)(2,1)S(1)}, bf16[1,192,3584]{2,1,0:T(8,128)(2,1)}, u32[]{:S(2)}) copy-start(bf16[1,192,3584]{2,1,0:T(8,128)(2,1)} %param.7) | copy-start | bytes 4128772
  2.3 12.3 %collective-permute-start.2 = (bf16[192,896]{1,0:T(8,128)(2,1)S(1)}, bf16[192,896]{1,0:T(8,128)(2,1)S(1)}, u32[]{:S(2)}, u32[]{:S(2)}) collective-permute-start(bf16[192,896]{1,0:T(8,128)(2,1)S(1)} %get-tuple-element.72), channel_id=1, source_target_pairs={{0,1},{1,0},{2,3},{3,2},{4,5},{5,4},{6,7},{7,6},{8,9},{9,8},{10,11... | collective-permute-start | bytes 1032200 | tf_op jit(solution)/shard_map/ppermute | solution.py:41
  2.9 11.8 %collective-permute-start.3 = (bf16[192,896]{1,0:T(8,128)(2,1)S(1)}, bf16[192,896]{1,0:T(8,128)(2,1)S(1)}, u32[]{:S(2)}, u32[]{:S(2)}) collective-permute-start(bf16[192,896]{1,0:T(8,128)(2,1)S(1)} %get-tuple-element.73), channel_id=1, source_target_pairs={{0,1},{1,0},{2,3},{3,2},{4,5},{5,4},{6,7},{7,6},{8,9},{9,8},{10,11... | collective-permute-start | bytes 1032200 | tf_op jit(solution)/shard_map/ppermute | solution.py:41
  2.9 13.7 %collective-permute-start.6 = (bf16[1792,128]{1,0:T(8,128)(2,1)S(1)}, bf16[1792,128]{1,0:T(8,128)(2,1)S(1)}, u32[]{:S(2)}, u32[]{:S(2)}) collective-permute-start(bf16[1792,128]{1,0:T(8,128)(2,1)S(1)} %get-tuple-element.88.w_own), channel_id=1, source_target_pairs={{0,16},{16,0},{1,17},{17,1},{2,18},{18,2},{3,19},{19,3},{4,20},{20... | collective-permute-start | bytes 1376264 | tf_op jit(solution)/shard_map/ppermute | solution.py:41
  5.9 7.9 %collective-permute-start = (bf16[192,256]{1,0:T(8,128)(2,1)S(1)}, bf16[192,256]{1,0:T(8,128)(2,1)S(1)}, u32[]{:S(2)}, u32[]{:S(2)}) collective-permute-start(bf16[192,256]{1,0:T(8,128)(2,1)S(1)} %bitcast.13), channel_id=1, source_target_pairs={{0,2},{1,3},{2,4},{3,5},{4,6},{5,7},{6,8},{7,9},{8,10},{9,11},{10,... | collective-permute-start | bytes 294920 | tf_op jit(solution)/shard_map/ppermute | solution.py:37
  7.4 0.7 collective-permute-start.1
  8.1 6.6 %collective-permute-start.4 = (s32[15,192]{1,0:T(8,128)S(1)}, s32[15,192]{1,0:T(8,128)S(1)}, u32[]{:S(2)}, u32[]{:S(2)}) collective-permute-start(s32[15,192]{1,0:T(8,128)S(1)} %get-tuple-element.74.refs_6_.l_own), channel_id=1, source_target_pairs={{0,1},{1,0},{2,3},{3,2},{4,5},{5,4},{6,7},{7,6},{8,9},{9,8},{10,11... | collective-permute-start | bytes 34568 | tf_op jit(solution)/shard_map/ppermute | solution.py:41
  15.5 1.4 %collective-permute-start.5 = (bf16[512,128]{1,0:T(8,128)(2,1)S(1)}, bf16[512,128]{1,0:T(8,128)(2,1)S(1)}, u32[]{:S(2)}, u32[]{:S(2)}) collective-permute-start(bf16[512,128]{1,0:T(8,128)(2,1)S(1)} %get-tuple-element.81), channel_id=1, source_target_pairs={{0,1},{1,0},{2,3},{3,2},{4,5},{5,4},{6,7},{7,6},{8,9},{9,8},{10,11... | collective-permute-start | bytes 393224 | tf_op jit(solution)/shard_map/ppermute | solution.py:41
  16.9 8.9 %collective-permute-start.7 = (bf16[192,3584]{1,0:T(8,128)(2,1)S(1)}, bf16[192,3584]{1,0:T(8,128)(2,1)S(1)}, u32[]{:S(2)}, u32[]{:S(2)}) collective-permute-start(bf16[192,3584]{1,0:T(8,128)(2,1)S(1)} %bitcast.7), channel_id=1, source_target_pairs={{0,1},{1,0},{2,3},{3,2},{4,5},{5,4},{6,7},{7,6},{8,9},{9,8},{10,11... | collective-permute-start | bytes 4128776 | tf_op jit(solution)/shard_map/ppermute | solution.py:41
  21.0 8.2 %collective-permute-start.8 = (bf16[384,128]{1,0:T(8,128)(2,1)S(1)}, bf16[384,128]{1,0:T(8,128)(2,1)S(1)}, u32[]{:S(2)}, u32[]{:S(2)}) collective-permute-start(bf16[384,128]{1,0:T(8,128)(2,1)S(1)} %get-tuple-element.94), channel_id=1, source_target_pairs={{0,14},{1,15},{2,0},{3,1},{4,2},{5,3},{6,4},{7,5},{8,6},{9,7},{10,... | collective-permute-start | bytes 294920 | tf_op jit(solution)/shard_map/ppermute | solution.py:37
  25.3 3.9 %collective-permute-start.9 = (bf16[128,128]{1,0:T(8,128)(2,1)S(1)}, bf16[128,128]{1,0:T(8,128)(2,1)S(1)}, u32[]{:S(2)}, u32[]{:S(2)}) collective-permute-start(bf16[128,128]{1,0:T(8,128)(2,1)S(1)} %get-tuple-element.95), channel_id=1, source_target_pairs={{0,12},{1,13},{2,14},{3,15},{4,0},{5,1},{6,2},{7,3},{8,4},{9,5},{1... | collective-permute-start | bytes 98312 | tf_op jit(solution)/shard_map/ppermute | solution.py:37
  30.3 14.6 %collective-permute-start.12 = (bf16[1792,128]{1,0:T(8,128)(2,1)S(1)}, bf16[1792,128]{1,0:T(8,128)(2,1)S(1)}, u32[]{:S(2)}, u32[]{:S(2)}) collective-permute-start(bf16[1792,128]{1,0:T(8,128)(2,1)S(1)} %get-tuple-element.102), channel_id=1, source_target_pairs={{0,16},{1,17},{2,18},{3,19},{4,20},{5,21},{6,22},{7,23},{8,24},{9,... | collective-permute-start | bytes 1376264 | tf_op jit(solution)/shard_map/ppermute | solution.py:46
  31.8 7.3 %collective-permute-start.10 = (bf16[384,128]{1,0:T(8,128)(2,1)S(1)}, bf16[384,128]{1,0:T(8,128)(2,1)S(1)}, u32[]{:S(2)}, u32[]{:S(2)}) collective-permute-start(bf16[384,128]{1,0:T(8,128)(2,1)S(1)} %get-tuple-element.97.refs_8_), channel_id=1, source_target_pairs={{0,2},{1,3},{2,4},{3,5},{4,6},{5,7},{6,8},{7,9},{8,10},{9,11},{10,... | collective-permute-start | bytes 294920 | tf_op jit(solution)/shard_map/ppermute | solution.py:37
  31.8 6.8 %collective-permute-start.11 = (bf16[128,128]{1,0:T(8,128)(2,1)S(1)}, bf16[128,128]{1,0:T(8,128)(2,1)S(1)}, u32[]{:S(2)}, u32[]{:S(2)}) collective-permute-start(bf16[128,128]{1,0:T(8,128)(2,1)S(1)} %get-tuple-element.98), channel_id=1, source_target_pairs={{0,4},{1,5},{2,6},{3,7},{4,8},{5,9},{6,10},{7,11},{8,12},{9,13},{1... | collective-permute-start | bytes 98312 | tf_op jit(solution)/shard_map/ppermute | solution.py:37
  44.9 4.9 %collective-permute-start.13 = (bf16[448,128]{1,0:T(8,128)(2,1)S(1)}, bf16[448,128]{1,0:T(8,128)(2,1)S(1)}, u32[]{:S(2)}, u32[]{:S(2)}) collective-permute-start(bf16[448,128]{1,0:T(8,128)(2,1)S(1)} %get-tuple-element.111), channel_id=1, source_target_pairs={{0,4},{1,5},{2,6},{3,7},{4,0},{5,1},{6,2},{7,3},{8,12},{9,13},{10,... | collective-permute-start | bytes 344072 | tf_op jit(solution)/shard_map/ppermute | solution.py:46
  45.0 4.9 %collective-permute-start.14 = (bf16[448,128]{1,0:T(8,128)(2,1)S(1)}, bf16[448,128]{1,0:T(8,128)(2,1)S(1)}, u32[]{:S(2)}, u32[]{:S(2)}) collective-permute-start(bf16[448,128]{1,0:T(8,128)(2,1)S(1)} %get-tuple-element.112), channel_id=1, source_target_pairs={{0,2},{1,3},{2,0},{3,1},{4,6},{5,7},{6,4},{7,5},{8,10},{9,11},{10,... | collective-permute-start | bytes 344072 | tf_op jit(solution)/shard_map/ppermute | solution.py:46
  46.0 5.7 %collective-permute-start.15 = (bf16[448,128]{1,0:T(8,128)(2,1)S(1)}, bf16[448,128]{1,0:T(8,128)(2,1)S(1)}, u32[]{:S(2)}, u32[]{:S(2)}) collective-permute-start(bf16[448,128]{1,0:T(8,128)(2,1)S(1)} %get-tuple-element.113), channel_id=1, source_target_pairs={{0,6},{1,7},{2,4},{3,5},{4,2},{5,3},{6,0},{7,1},{8,14},{9,15},{10,... | collective-permute-start | bytes 344072 | tf_op jit(solution)/shard_map/ppermute | solution.py:46
  51.8 9.7 %collective-permute-start.19 = (bf16[192,896]{1,0:T(8,128)(2,1)S(1)}, bf16[192,896]{1,0:T(8,128)(2,1)S(1)}, u32[]{:S(2)}, u32[]{:S(2)}) collective-permute-start(bf16[192,896]{1,0:T(8,128)(2,1)S(1)} %get-tuple-element.117), channel_id=1, source_target_pairs={{0,1},{1,0},{2,3},{3,2},{4,5},{5,4},{6,7},{7,6},{8,9},{9,8},{10,11... | collective-permute-start | bytes 1032200 | tf_op jit(solution)/shard_map/ppermute | solution.py:41
  51.9 9.6 %collective-permute-start.16 = (bf16[448,128]{1,0:T(8,128)(2,1)S(1)}, bf16[448,128]{1,0:T(8,128)(2,1)S(1)}, u32[]{:S(2)}, u32[]{:S(2)}) collective-permute-start(bf16[448,128]{1,0:T(8,128)(2,1)S(1)} %reduce_step.4.held), channel_id=1, source_target_pairs={{0,8},{1,9},{2,10},{3,11},{4,12},{5,13},{6,14},{7,15},{8,0},{9,1},... | collective-permute-start | bytes 344072 | tf_op jit(solution)/shard_map/ppermute | solution.py:46
  54.4 7.1 %collective-permute-start.17 = (bf16[384,128]{1,0:T(8,128)(2,1)S(1)}, bf16[384,128]{1,0:T(8,128)(2,1)S(1)}, u32[]{:S(2)}, u32[]{:S(2)}) collective-permute-start(bf16[384,128]{1,0:T(8,128)(2,1)S(1)} %get-tuple-element.115), channel_id=1, source_target_pairs={{0,14},{1,15},{2,0},{3,1},{4,2},{5,3},{6,4},{7,5},{8,6},{9,7},{10,... | collective-permute-start | bytes 294920 | tf_op jit(solution)/shard_map/ppermute | solution.py:37
  56.8 4.7 %collective-permute-start.18 = (bf16[128,128]{1,0:T(8,128)(2,1)S(1)}, bf16[128,128]{1,0:T(8,128)(2,1)S(1)}, u32[]{:S(2)}, u32[]{:S(2)}) collective-permute-start(bf16[128,128]{1,0:T(8,128)(2,1)S(1)} %get-tuple-element.116), channel_id=1, source_target_pairs={{0,12},{1,13},{2,14},{3,15},{4,0},{5,1},{6,2},{7,3},{8,4},{9,5},{1... | collective-permute-start | bytes 98312 | tf_op jit(solution)/shard_map/ppermute | solution.py:37
  61.5 6.5 %collective-permute-start.21 = (bf16[448,128]{1,0:T(8,128)(2,1)S(1)}, bf16[448,128]{1,0:T(8,128)(2,1)S(1)}, u32[]{:S(2)}, u32[]{:S(2)}) collective-permute-start(bf16[448,128]{1,0:T(8,128)(2,1)S(1)} %reduce_step.5.refs_0_), channel_id=1, source_target_pairs={{0,4},{1,5},{2,6},{3,7},{4,0},{5,1},{6,2},{7,3},{8,12},{9,13},{10,... | collective-permute-start | bytes 344072 | tf_op jit(solution)/shard_map/ppermute | solution.py:46
  64.3 7.0 %collective-permute-start.22 = (bf16[448,128]{1,0:T(8,128)(2,1)S(1)}, bf16[448,128]{1,0:T(8,128)(2,1)S(1)}, u32[]{:S(2)}, u32[]{:S(2)}) collective-permute-start(bf16[448,128]{1,0:T(8,128)(2,1)S(1)} %reduce_step.5.refs_0_), channel_id=1, source_target_pairs={{0,2},{1,3},{2,0},{3,1},{4,6},{5,7},{6,4},{7,5},{8,10},{9,11},{10,... | collective-permute-start | bytes 344072 | tf_op jit(solution)/shard_map/ppermute | solution.py:46
  65.4 5.9 %collective-permute-start.23 = (bf16[448,128]{1,0:T(8,128)(2,1)S(1)}, bf16[448,128]{1,0:T(8,128)(2,1)S(1)}, u32[]{:S(2)}, u32[]{:S(2)}) collective-permute-start(bf16[448,128]{1,0:T(8,128)(2,1)S(1)} %reduce_step.5.refs_0_), channel_id=1, source_target_pairs={{0,6},{1,7},{2,4},{3,5},{4,2},{5,3},{6,0},{7,1},{8,14},{9,15},{10,... | collective-permute-start | bytes 344072 | tf_op jit(solution)/shard_map/ppermute | solution.py:46
  65.8 1.3 %collective-permute-start.20 = (bf16[192,128]{1,0:T(8,128)(2,1)S(1)}, bf16[192,128]{1,0:T(8,128)(2,1)S(1)}, u32[]{:S(2)}, u32[]{:S(2)}) collective-permute-start(bf16[192,128]{1,0:T(8,128)(2,1)S(1)} %get-tuple-element.125), channel_id=1, source_target_pairs={{0,1},{1,0},{2,3},{3,2},{4,5},{5,4},{6,7},{7,6},{8,9},{9,8},{10,11... | collective-permute-start | bytes 147464 | tf_op jit(solution)/shard_map/ppermute | solution.py:41
  65.9 5.9 %collective-permute-start.24 = (bf16[448,128]{1,0:T(8,128)(2,1)S(1)}, bf16[448,128]{1,0:T(8,128)(2,1)S(1)}, u32[]{:S(2)}, u32[]{:S(2)}) collective-permute-start(bf16[448,128]{1,0:T(8,128)(2,1)S(1)} %reduce_step.5.refs_0_), channel_id=1, source_target_pairs={{0,1},{1,0},{2,3},{3,2},{4,5},{5,4},{6,7},{7,6},{8,9},{9,8},{10,11... | collective-permute-start | bytes 344072 | tf_op jit(solution)/shard_map/ppermute | solution.py:41
  71.3 1.3 %collective-permute-start.25 = (bf16[448,128]{1,0:T(8,128)(2,1)S(1)}, bf16[448,128]{1,0:T(8,128)(2,1)S(1)}, u32[]{:S(2)}, u32[]{:S(2)}) collective-permute-start(bf16[448,128]{1,0:T(8,128)(2,1)S(1)} %collective-permute-done.21.refs_1_), channel_id=1, source_target_pairs={{0,1},{1,0},{2,3},{3,2},{4,5},{5,4},{6,7},{7,6},{8,9},{9,8},{10,11... | collective-permute-start | bytes 344072 | tf_op jit(solution)/shard_map/ppermute | solution.py:41
  71.3 1.5 %collective-permute-start.26 = (bf16[448,128]{1,0:T(8,128)(2,1)S(1)}, bf16[448,128]{1,0:T(8,128)(2,1)S(1)}, u32[]{:S(2)}, u32[]{:S(2)}) collective-permute-start(bf16[448,128]{1,0:T(8,128)(2,1)S(1)} %collective-permute-done.22.refs_2_), channel_id=1, source_target_pairs={{0,1},{1,0},{2,3},{3,2},{4,5},{5,4},{6,7},{7,6},{8,9},{9,8},{10,11... | collective-permute-start | bytes 344072 | tf_op jit(solution)/shard_map/ppermute | solution.py:41
  71.8 1.3 %collective-permute-start.27 = (bf16[448,128]{1,0:T(8,128)(2,1)S(1)}, bf16[448,128]{1,0:T(8,128)(2,1)S(1)}, u32[]{:S(2)}, u32[]{:S(2)}) collective-permute-start(bf16[448,128]{1,0:T(8,128)(2,1)S(1)} %collective-permute-done.23.refs_3_), channel_id=1, source_target_pairs={{0,1},{1,0},{2,3},{3,2},{4,5},{5,4},{6,7},{7,6},{8,9},{9,8},{10,11... | collective-permute-start | bytes 344072 | tf_op jit(solution)/shard_map/ppermute | solution.py:41

commit v6 on v5

--- a/solution.py
+++ b/solution.py
@@ -239,14 +239,12 @@
 
 
 def key_kernel(tok, *refs):
-    raw = refs[:6]
-    top_in, norm_in, v_own, v_near, v_far = refs[6:11]
-    own_out, near_out, far_out, mine_out, send_out = refs[11:16]
-    q_buf, g_buf, k_buf, v_buf, d_buf, acc, r_buf = refs[16:]
+    q_buf, g_buf, k_buf, top_in, norm_in, v_own, v_near, v_far = refs[:8]
+    own_out, near_out, far_out, mine_out, send_out = refs[8:13]
+    v_buf, d_buf, acc, r_buf = refs[13:]
     place = lax.axis_index("seq")
     core, chip = lax.rem(place, 2), lax.div(place, 2)
     rest = WINDOW - 2 * tok
-    lay_out(core, tok, raw, q_buf, g_buf, k_buf)
     v_buf[:rest, :] = v_far[...]
     v_buf[rest:WINDOW, :] = v_near[...]
     v_buf[WINDOW:, :] = v_own[...]
@@ -280,11 +278,11 @@
     own_out[...] = acc[WINDOW:, :] * score_scale
 
 
-def head_scratch(tok):
+def head_shapes(tok):
     return [
-        pltpu.VMEM((2 * tok, GROUP * HD), bf16),
-        pltpu.VMEM((2 * tok, GROUP * HD), bf16),
-        pltpu.VMEM((WINDOW + 2 * tok, HD), bf16),
+        jax.ShapeDtypeStruct((2 * tok, GROUP * HD), bf16),
+        jax.ShapeDtypeStruct((2 * tok, GROUP * HD), bf16),
+        jax.ShapeDtypeStruct((WINDOW + 2 * tok, HD), bf16),
     ]
 
 
@@ -300,11 +298,10 @@
     stats = jax.ShapeDtypeStruct((2 * tok // BLOCK * GROUP, BLOCK), f32)
     return pl.pallas_call(
         functools.partial(value_kernel, tok),
-        out_shape=term_shapes(tok) + [stats, stats],
+        out_shape=term_shapes(tok) + [stats, stats] + head_shapes(tok),
         in_specs=[VMEM] * 8,
-        out_specs=[VMEM] * 5,
-        scratch_shapes=head_scratch(tok)
-        + [
+        out_specs=[VMEM] * 8,
+        scratch_shapes=[
             pltpu.VMEM((SPAN, GROUP * HD), bf16),
             pltpu.VMEM((WINDOW + 2 * tok, HD), f32),
         ],
@@ -313,15 +310,14 @@
     )(*raw, *spikes)
 
 
-def key_terms(tok, raw, top, norm, values):
+def key_terms(tok, heads, top, norm, values):
     half = jax.ShapeDtypeStruct((tok, GROUP * HD), bf16)
     return pl.pallas_call(
         functools.partial(key_kernel, tok),
         out_shape=term_shapes(tok) + [half, half],
-        in_specs=[VMEM] * 11,
+        in_specs=[VMEM] * 8,
         out_specs=[VMEM] * 5,
-        scratch_shapes=head_scratch(tok)
-        + [
+        scratch_shapes=[
             pltpu.VMEM((WINDOW + 2 * tok, HD), bf16),
             pltpu.VMEM((SPAN, GROUP * HD), bf16),
             pltpu.VMEM((WINDOW + 2 * tok, HD), f32),
@@ -329,7 +325,7 @@
         ],
         compiler_params=limit(14),
         name="key_terms",
-    )(*raw, top, norm, *values)
+    )(*heads, top, norm, *values)
 
 
 def sum_keys_kernel(tok, own, near, far, mine, send, buf):
@@ -596,7 +592,7 @@
     raw = [query_own, query_oth, grad_own, grad_oth, keys_own, keys_oth]
     marks = (marks_own, marks_oth)
 
-    own, near, far, top, norm = value_terms(tok, raw, marks)
+    own, near, far, top, norm, *heads = value_terms(tok, raw, marks)
     near, far = shifted(near, -2), shifted(far, -4)
     values, tail, spiked = project(tok, both(hidden_own), marks, weight)
 
@@ -606,7 +602,7 @@
         values, tail, send = lax.optimization_barrier((values, tail, send))
         got = crossed(send, n_seq)
     window = (values, shifted(values, 2), shifted(tail, 4))
-    own_k, near_k, far_k, query_mine, query_out = key_terms(tok, raw, top, norm, window)
+    own_k, near_k, far_k, query_mine, query_out = key_terms(tok, heads, top, norm, window)
     if fast:
         got, own_k = lax.optimization_barrier((got, own_k))
         keep, *sends = reduce_step(keep, [got], 4)

time: 74.5 us -> 74.5 us (level)
  no operation moved by 1% of the time
where the time goes in v6:
time: 74.5 us; the launch traced here: 74.3 us
  starting transfers between devices  33.5 us (45%)
  waiting for transfers between devices  22.7 us (30%)
  Pallas kernels  17.2 us (23%)
  between operations  0.95 us (1%)
    ppermute x8, waiting for transfers between devices, shifted(): return lax.ppermute(value, 'seq', pairs)  12.4 us
    ppermute x8, starting transfers between devices, crossed(): lax.ppermute(value, ('dp', 'seq'), [(i, i ^ flip) for i in range(count)])  11.9 us
    ppermute x12, starting transfers between devices, swapped(): lax.ppermute(value, axis, [(i, i ^ flip) for i in range(lax.axis_size(axi...  11.1 us
    ppermute x8, starting transfers between devices, shifted(): return lax.ppermute(value, 'seq', pairs)  10.4 us
    ppermute x8, waiting for transfers between devices, crossed(): lax.ppermute(value, ('dp', 'seq'), [(i, i ^ flip) for i in range(count)])  6.45 us
    pallas_call x1, Pallas kernels, key_terms(): pl.pallas_call(functools.partial(key_kernel, tok), out_shape=term_shapes(...  5.65 us
    ppermute x12, waiting for transfers between devices, swapped(): lax.ppermute(value, axis, [(i, i ^ flip) for i in range(lax.axis_size(axi...  3.89 us
    pallas_call x1, Pallas kernels, value_terms(): pl.pallas_call(functools.partial(value_kernel, tok), out_shape=term_shape...  3.85 us
  transfers between devices with their start and end apart: 28, of which 15 were waited for; matrix products, arithmetic and copies ran while one was open for 0% of the time, Pallas kernels for 18%

profile of v6, /device:TPU:0, one launch (start us, length us, event | category | flops | bytes accessed | tf_op | source)
XLA Modules:
  0.0 74.3 jit_solution(12035632654225484187)
XLA Ops:
  0.7 1.7 %split.1 = (bf16[192,896]{1,0:T(8,128)(2,1)S(1)}, bf16[192,896]{1,0:T(8,128)(2,1)S(1)}, bf16[192,896]{1,0:T(8,128)(2,1)S(1)}, bf16[192,896]{1,0:T(8,128)(2,1)S(1...) custom-call(bf16[192,1792]{1,0:T(8,128)(2,1)} %bitcast.9, ...), custom_call_target="tpu_custom_call" | custom-call | tf_op jit(solution)/shard_map/split/pallas_call | solution.py:92
  2.9 2.9 %collective-permute-start.6 = (bf16[1792,128]{1,0:T(8,128)(2,1)S(1)}, bf16[1792,128]{1,0:T(8,128)(2,1)S(1)}, u32[]{:S(2)}, u32[]{:S(2)}) collective-permute-start(bf16[1792,128]{1,0:T(8,128)(2,1)S(1)} %get-tuple-element.94.w_own), channel_id=1, source_target_pairs={{0,16},{16,0},{1,17},{17,1},{2,18},{18,2},{3,19},{19,3},{4,20},{20... | collective-permute-start | bytes 1376264 | tf_op jit(solution)/shard_map/ppermute | solution.py:41
  5.9 1.5 %collective-permute-start = (bf16[192,256]{1,0:T(8,128)(2,1)S(1)}, bf16[192,256]{1,0:T(8,128)(2,1)S(1)}, u32[]{:S(2)}, u32[]{:S(2)}) collective-permute-start(bf16[192,256]{1,0:T(8,128)(2,1)S(1)} %bitcast.13), channel_id=1, source_target_pairs={{0,2},{1,3},{2,4},{3,5},{4,6},{5,7},{6,8},{7,9},{8,10},{9,11},{10,... | collective-permute-start | bytes 294920 | tf_op jit(solution)/shard_map/ppermute | solution.py:37
  7.4 0.7 collective-permute-start.1
  8.1 5.7 %collective-permute-start.4 = (s32[15,192]{1,0:T(8,128)S(1)}, s32[15,192]{1,0:T(8,128)S(1)}, u32[]{:S(2)}, u32[]{:S(2)}) collective-permute-start(s32[15,192]{1,0:T(8,128)S(1)} %get-tuple-element.77.refs_6_.l_own), channel_id=1, source_target_pairs={{0,1},{1,0},{2,3},{3,2},{4,5},{5,4},{6,7},{7,6},{8,9},{9,8},{10,11... | collective-permute-start | bytes 34568 | tf_op jit(solution)/shard_map/ppermute | solution.py:41
  13.8 0.8 %collective-permute-done.4.refs_7_.l_oth = s32[15,192]{1,0:T(8,128)S(1)} collective-permute-done((s32[15,192]{1,0:T(8,128)S(1)}, s32[15,192]{1,0:T(8,128)S(1)}, u32[]{:S(2)}, u32[]{:S(2)}) %collective-permute-start.4) | collective-permute-done | bytes 11552 | tf_op jit(solution)/shard_map/ppermute | solution.py:41
  14.6 0.8 %pack.1 = (bf16[512,128]{1,0:T(8,128)(2,1)S(1)}, bf16[512,128]{1,0:T(8,128)(2,1)S(1)}) custom-call(bf16[192,256]{1,0:T(8,128)(2,1)} %bitcast.12, bf16[192,256]{1,0:T(8,128)(2,1)S(1)} %collective-permute-done.near, bf16[128,256]{1,0:T(8,128)(2,1)S(1)} %collective-permute-done.1.far), custom_call_target="tpu_custom_call" | custom-call | tf_op jit(solution)/shard_map/pack/pallas_call | solution.py:131
  15.9 0.7 %collective-permute-done.6.w_oth = bf16[1792,128]{1,0:T(8,128)(2,1)S(1)} collective-permute-done((bf16[1792,128]{1,0:T(8,128)(2,1)S(1)}, bf16[1792,128]{1,0:T(8,128)(2,1)S(1)}, u32[]{:S(2)}, u32[]{:S(2)}) %collective-permute-start.6) | collective-permute-done | bytes 458784 | tf_op jit(solution)/shard_map/ppermute | solution.py:41
  17.2 3.8 %value_terms.1 = (f32[384,128]{1,0:T(8,128)S(1)}, bf16[384,128]{1,0:T(8,128)(2,1)S(1)}, bf16[128,128]{1,0:T(8,128)(2,1)S(1)}, f32[21,128]{1,0:T(8,128)S(1)}, f32...) custom-call(bf16[192,896]{1,0:T(8,128)(2,1)S(1)} %get-tuple-element., ...), custom_call_target="tpu_custom_call" | custom-call | tf_op jit(solution)/shard_map/value_terms/pallas_call | solution.py:299
  21.1 4.3 %collective-permute-start.8 = (bf16[384,128]{1,0:T(8,128)(2,1)S(1)}, bf16[384,128]{1,0:T(8,128)(2,1)S(1)}, u32[]{:S(2)}, u32[]{:S(2)}) collective-permute-start(bf16[384,128]{1,0:T(8,128)(2,1)S(1)} %get-tuple-element.100), channel_id=1, source_target_pairs={{0,14},{1,15},{2,0},{3,1},{4,2},{5,3},{6,4},{7,5},{8,6},{9,7},{10,... | collective-permute-start | bytes 294920 | tf_op jit(solution)/shard_map/ppermute | solution.py:37
  25.8 2.0 %project.1 = (bf16[384,128]{1,0:T(8,128)(2,1)S(1)}, bf16[128,128]{1,0:T(8,128)(2,1)S(1)}, bf16[384,3584]{1,0:T(8,128)(2,1)S(1)}) custom-call(bf16[192,3584]{1,0:T(8,128)(2,1)S(1)} %bitcast.8, bf16[192,3584]{1,0:T(8,128)(2,1)S(1)} %collective-permute-done.7.h_oth, s32[15,192]{1,0:T(8,128)S(1)} %get-tuple-element.77.refs_6_.l_own, ...), custom_call_target="tpu_custom_call" | custom-call | tf_op jit(solution)/shard_map/project/pallas_call | solution.py:385
  27.8 1.5 %collective-permute-done.9.far = bf16[128,128]{1,0:T(8,128)(2,1)S(1)} collective-permute-done((bf16[128,128]{1,0:T(8,128)(2,1)S(1)}, bf16[128,128]{1,0:T(8,128)(2,1)S(1)}, u32[]{:S(2)}, u32[]{:S(2)}) %collective-permute-start.9) | collective-permute-done | bytes 32800 | tf_op jit(solution)/shard_map/ppermute | solution.py:37
  29.3 1.0 %weight_terms.1 = (f32[1792,128]{1,0:T(8,128)S(1)}, bf16[1792,128]{1,0:T(8,128)(2,1)S(1)}) custom-call(bf16[384,3584]{1,0:T(8,128)(2,1)S(1)} %get-tuple-element.98.spiked, f32[384,128]{1,0:T(8,128)S(1)} %get-tuple-element.99.own, bf16[384,128]{1,0:T(8,128)(2,1)S(1)} %collective-permute-done.8.near, bf16[128,128]{1,0:T(8,128)(2,1)S(1)} %collective-permute-done.9.far), custom_call_target="tpu_custom_call" | custom-call | tf_op jit(solution)/shard_map/weight_terms/pallas_call | solution.py:437
  30.3 1.6 %collective-permute-start.12 = (bf16[1792,128]{1,0:T(8,128)(2,1)S(1)}, bf16[1792,128]{1,0:T(8,128)(2,1)S(1)}, u32[]{:S(2)}, u32[]{:S(2)}) collective-permute-start(bf16[1792,128]{1,0:T(8,128)(2,1)S(1)} %get-tuple-element.108), channel_id=1, source_target_pairs={{0,16},{1,17},{2,18},{3,19},{4,20},{5,21},{6,22},{7,23},{8,24},{9,... | collective-permute-start | bytes 1376264 | tf_op jit(solution)/shard_map/ppermute | solution.py:46
  31.9 1.1 %collective-permute-start.11 = (bf16[128,128]{1,0:T(8,128)(2,1)S(1)}, bf16[128,128]{1,0:T(8,128)(2,1)S(1)}, u32[]{:S(2)}, u32[]{:S(2)}) collective-permute-start(bf16[128,128]{1,0:T(8,128)(2,1)S(1)} %get-tuple-element.104), channel_id=1, source_target_pairs={{0,4},{1,5},{2,6},{3,7},{4,8},{5,9},{6,10},{7,11},{8,12},{9,13},{1... | collective-permute-start | bytes 98312 | tf_op jit(solution)/shard_map/ppermute | solution.py:37
  32.9 5.7 %collective-permute-done.11.refs_7_ = bf16[128,128]{1,0:T(8,128)(2,1)S(1)} collective-permute-done((bf16[128,128]{1,0:T(8,128)(2,1)S(1)}, bf16[128,128]{1,0:T(8,128)(2,1)S(1)}, u32[]{:S(2)}, u32[]{:S(2)}) %collective-permute-start.11) | collective-permute-done | bytes 32800 | tf_op jit(solution)/shard_map/ppermute | solution.py:37
  38.6 0.5 collective-permute-done.10.refs_6_
  39.2 5.7 %key_terms.1 = (f32[384,128]{1,0:T(8,128)S(1)}, bf16[384,128]{1,0:T(8,128)(2,1)S(1)}, bf16[128,128]{1,0:T(8,128)(2,1)S(1)}, bf16[192,896]{1,0:T(8,128)(2,1)S(1)}, bf16[192,896]{1,0:T(8,128)(2,1)S(1)}) custom-call(bf16[384,896]{1,0:T(8,128)(2,1)S(1)} %get-tuple-element.88.refs_0_, bf16[384,896]{1,0:T(8,128)(2,1)S(1)} %get-tuple-element.89.refs_1_, ...), custom_call_target="tpu_custom_call" | custom-call | tf_op jit(solution)/shard_map/key_terms/pallas_call | solution.py:315
  45.0 1.0 %collective-permute-start.14 = (bf16[448,128]{1,0:T(8,128)(2,1)S(1)}, bf16[448,128]{1,0:T(8,128)(2,1)S(1)}, u32[]{:S(2)}, u32[]{:S(2)}) collective-permute-start(bf16[448,128]{1,0:T(8,128)(2,1)S(1)} %get-tuple-element.118), channel_id=1, source_target_pairs={{0,2},{1,3},{2,0},{3,1},{4,6},{5,7},{6,4},{7,5},{8,10},{9,11},{10,... | collective-permute-start | bytes 344072 | tf_op jit(solution)/shard_map/ppermute | solution.py:46
  46.0 2.5 %collective-permute-start.15 = (bf16[448,128]{1,0:T(8,128)(2,1)S(1)}, bf16[448,128]{1,0:T(8,128)(2,1)S(1)}, u32[]{:S(2)}, u32[]{:S(2)}) collective-permute-start(bf16[448,128]{1,0:T(8,128)(2,1)S(1)} %get-tuple-element.119), channel_id=1, source_target_pairs={{0,6},{1,7},{2,4},{3,5},{4,2},{5,3},{6,0},{7,1},{8,14},{9,15},{10,... | collective-permute-start | bytes 344072 | tf_op jit(solution)/shard_map/ppermute | solution.py:46
  48.5 1.3 %collective-permute-done.13.refs_0_ = bf16[448,128]{1,0:T(8,128)(2,1)S(1)} collective-permute-done((bf16[448,128]{1,0:T(8,128)(2,1)S(1)}, bf16[448,128]{1,0:T(8,128)(2,1)S(1)}, u32[]{:S(2)}, u32[]{:S(2)}) %collective-permute-start.13) | collective-permute-done | bytes 114720 | tf_op jit(solution)/shard_map/ppermute | solution.py:46
  49.9 1.8 %collective-permute-done.15.refs_2_ = bf16[448,128]{1,0:T(8,128)(2,1)S(1)} collective-permute-done((bf16[448,128]{1,0:T(8,128)(2,1)S(1)}, bf16[448,128]{1,0:T(8,128)(2,1)S(1)}, u32[]{:S(2)}, u32[]{:S(2)}) %collective-permute-start.15) | collective-permute-done | bytes 114720 | tf_op jit(solution)/shard_map/ppermute | solution.py:46
  51.8 2.5 %collective-permute-start.16 = (bf16[448,128]{1,0:T(8,128)(2,1)S(1)}, bf16[448,128]{1,0:T(8,128)(2,1)S(1)}, u32[]{:S(2)}, u32[]{:S(2)}) collective-permute-start(bf16[448,128]{1,0:T(8,128)(2,1)S(1)} %reduce_step.4.held), channel_id=1, source_target_pairs={{0,8},{1,9},{2,10},{3,11},{4,12},{5,13},{6,14},{7,15},{8,0},{9,1},... | collective-permute-start | bytes 344072 | tf_op jit(solution)/shard_map/ppermute | solution.py:46
  54.4 2.4 %collective-permute-start.17 = (bf16[384,128]{1,0:T(8,128)(2,1)S(1)}, bf16[384,128]{1,0:T(8,128)(2,1)S(1)}, u32[]{:S(2)}, u32[]{:S(2)}) collective-permute-start(bf16[384,128]{1,0:T(8,128)(2,1)S(1)} %get-tuple-element.121), channel_id=1, source_target_pairs={{0,14},{1,15},{2,0},{3,1},{4,2},{5,3},{6,4},{7,5},{8,6},{9,7},{10,... | collective-permute-start | bytes 294920 | tf_op jit(solution)/shard_map/ppermute | solution.py:37
  56.8 4.6 %collective-permute-done.18.far = bf16[128,128]{1,0:T(8,128)(2,1)S(1)} collective-permute-done((bf16[128,128]{1,0:T(8,128)(2,1)S(1)}, bf16[128,128]{1,0:T(8,128)(2,1)S(1)}, u32[]{:S(2)}, u32[]{:S(2)}) %collective-permute-start.18) | collective-permute-done | bytes 32800 | tf_op jit(solution)/shard_map/ppermute | solution.py:37
  61.5 2.7 %collective-permute-start.21 = (bf16[448,128]{1,0:T(8,128)(2,1)S(1)}, bf16[448,128]{1,0:T(8,128)(2,1)S(1)}, u32[]{:S(2)}, u32[]{:S(2)}) collective-permute-start(bf16[448,128]{1,0:T(8,128)(2,1)S(1)} %reduce_step.5.refs_0_), channel_id=1, source_target_pairs={{0,4},{1,5},{2,6},{3,7},{4,0},{5,1},{6,2},{7,3},{8,12},{9,13},{10,... | collective-permute-start | bytes 344072 | tf_op jit(solution)/shard_map/ppermute | solution.py:46
  64.2 1.1 %collective-permute-start.22 = (bf16[448,128]{1,0:T(8,128)(2,1)S(1)}, bf16[448,128]{1,0:T(8,128)(2,1)S(1)}, u32[]{:S(2)}, u32[]{:S(2)}) collective-permute-start(bf16[448,128]{1,0:T(8,128)(2,1)S(1)} %reduce_step.5.refs_0_), channel_id=1, source_target_pairs={{0,2},{1,3},{2,0},{3,1},{4,6},{5,7},{6,4},{7,5},{8,10},{9,11},{10,... | collective-permute-start | bytes 344072 | tf_op jit(solution)/shard_map/ppermute | solution.py:46
  66.4 0.7 collective-permute-done.20.k_oth
  67.1 0.9 %place_tokens.1 = (bf16[192,1792]{1,0:T(8,128)(2,1)}, bf16[192,256]{1,0:T(8,128)(2,1)}) custom-call(bf16[192,896]{1,0:T(8,128)(2,1)S(1)} %get-tuple-element.105.q_own, bf16[192,896]{1,0:T(8,128)(2,1)S(1)} %collective-permute-done.19.q_oth, bf16[192,128]{1,0:T(8,128)(2,1)S(1)} %get-tuple-element.130.k_own, bf16[192,128]{1,0:T(8,128)(2,1)S(1)} %collective-permute-done.20.k_oth), custom_call_target="tpu_custom_call" | custom-call | tf_op jit(solution)/shard_map/place_tokens/pallas_call | solution.py:522
  68.0 3.2 %collective-permute-done.22.refs_2_ = bf16[448,128]{1,0:T(8,128)(2,1)S(1)} collective-permute-done((bf16[448,128]{1,0:T(8,128)(2,1)S(1)}, bf16[448,128]{1,0:T(8,128)(2,1)S(1)}, u32[]{:S(2)}, u32[]{:S(2)}) %collective-permute-start.22) | collective-permute-done | bytes 114720 | tf_op jit(solution)/shard_map/ppermute | solution.py:46
  71.8 0.8 %collective-permute-done.25.refs_5_ = bf16[448,128]{1,0:T(8,128)(2,1)S(1)} collective-permute-done((bf16[448,128]{1,0:T(8,128)(2,1)S(1)}, bf16[448,128]{1,0:T(8,128)(2,1)S(1)}, u32[]{:S(2)}, u32[]{:S(2)}) %collective-permute-start.25) | collective-permute-done | bytes 114720 | tf_op jit(solution)/shard_map/ppermute | solution.py:41
  73.1 1.0 %place_weight.1 = bf16[1792,256]{1,0:T(8,128)(2,1)} custom-call(bf16[448,128]{1,0:T(8,128)(2,1)S(1)} %reduce_step.5.refs_0_, bf16[448,128]{1,0:T(8,128)(2,1)S(1)} %collective-permute-done.21.refs_1_, bf16[448,128]{1,0:T(8,128)(2,1)S(1)} %collective-permute-done.22.refs_2_, bf16[448,128]{1,0:T(8,128)(2,1)S(1)} %collective-permute-done.23.refs_3_, ...), custom_call_target="tpu_custom_call" | custom-call | tf_op jit(solution)/shard_map/place_weight/pallas_call | solution.py:498
  (40 shorter events, 4.7 us)
Async XLA Ops:
  0.6 5.2 %copy-start.1 = (bf16[1,192,256]{2,1,0:T(8,128)(2,1)S(1)}, bf16[1,192,256]{2,1,0:T(8,128)(2,1)}, u32[]{:S(2)}) copy-start(bf16[1,192,256]{2,1,0:T(8,128)(2,1)} %param.11) | copy-start | bytes 294916
  0.6 16.2 %copy-start = (bf16[1,192,3584]{2,1,0:T(8,128)(2,1)S(1)}, bf16[1,192,3584]{2,1,0:T(8,128)(2,1)}, u32[]{:S(2)}) copy-start(bf16[1,192,3584]{2,1,0:T(8,128)(2,1)} %param.7) | copy-start | bytes 4128772
  2.3 12.3 %collective-permute-start.2 = (bf16[192,896]{1,0:T(8,128)(2,1)S(1)}, bf16[192,896]{1,0:T(8,128)(2,1)S(1)}, u32[]{:S(2)}, u32[]{:S(2)}) collective-permute-start(bf16[192,896]{1,0:T(8,128)(2,1)S(1)} %get-tuple-element.75), channel_id=1, source_target_pairs={{0,1},{1,0},{2,3},{3,2},{4,5},{5,4},{6,7},{7,6},{8,9},{9,8},{10,11... | collective-permute-start | bytes 1032200 | tf_op jit(solution)/shard_map/ppermute | solution.py:41
  2.9 11.8 %collective-permute-start.3 = (bf16[192,896]{1,0:T(8,128)(2,1)S(1)}, bf16[192,896]{1,0:T(8,128)(2,1)S(1)}, u32[]{:S(2)}, u32[]{:S(2)}) collective-permute-start(bf16[192,896]{1,0:T(8,128)(2,1)S(1)} %get-tuple-element.76), channel_id=1, source_target_pairs={{0,1},{1,0},{2,3},{3,2},{4,5},{5,4},{6,7},{7,6},{8,9},{9,8},{10,11... | collective-permute-start | bytes 1032200 | tf_op jit(solution)/shard_map/ppermute | solution.py:41
  2.9 13.7 %collective-permute-start.6 = (bf16[1792,128]{1,0:T(8,128)(2,1)S(1)}, bf16[1792,128]{1,0:T(8,128)(2,1)S(1)}, u32[]{:S(2)}, u32[]{:S(2)}) collective-permute-start(bf16[1792,128]{1,0:T(8,128)(2,1)S(1)} %get-tuple-element.94.w_own), channel_id=1, source_target_pairs={{0,16},{16,0},{1,17},{17,1},{2,18},{18,2},{3,19},{19,3},{4,20},{20... | collective-permute-start | bytes 1376264 | tf_op jit(solution)/shard_map/ppermute | solution.py:41
  5.9 7.9 %collective-permute-start = (bf16[192,256]{1,0:T(8,128)(2,1)S(1)}, bf16[192,256]{1,0:T(8,128)(2,1)S(1)}, u32[]{:S(2)}, u32[]{:S(2)}) collective-permute-start(bf16[192,256]{1,0:T(8,128)(2,1)S(1)} %bitcast.13), channel_id=1, source_target_pairs={{0,2},{1,3},{2,4},{3,5},{4,6},{5,7},{6,8},{7,9},{8,10},{9,11},{10,... | collective-permute-start | bytes 294920 | tf_op jit(solution)/shard_map/ppermute | solution.py:37
  7.4 0.7 collective-permute-start.1
  8.1 6.6 %collective-permute-start.4 = (s32[15,192]{1,0:T(8,128)S(1)}, s32[15,192]{1,0:T(8,128)S(1)}, u32[]{:S(2)}, u32[]{:S(2)}) collective-permute-start(s32[15,192]{1,0:T(8,128)S(1)} %get-tuple-element.77.refs_6_.l_own), channel_id=1, source_target_pairs={{0,1},{1,0},{2,3},{3,2},{4,5},{5,4},{6,7},{7,6},{8,9},{9,8},{10,11... | collective-permute-start | bytes 34568 | tf_op jit(solution)/shard_map/ppermute | solution.py:41
  15.5 1.4 %collective-permute-start.5 = (bf16[512,128]{1,0:T(8,128)(2,1)S(1)}, bf16[512,128]{1,0:T(8,128)(2,1)S(1)}, u32[]{:S(2)}, u32[]{:S(2)}) collective-permute-start(bf16[512,128]{1,0:T(8,128)(2,1)S(1)} %get-tuple-element.84), channel_id=1, source_target_pairs={{0,1},{1,0},{2,3},{3,2},{4,5},{5,4},{6,7},{7,6},{8,9},{9,8},{10,11... | collective-permute-start | bytes 393224 | tf_op jit(solution)/shard_map/ppermute | solution.py:41
  16.9 8.9 %collective-permute-start.7 = (bf16[192,3584]{1,0:T(8,128)(2,1)S(1)}, bf16[192,3584]{1,0:T(8,128)(2,1)S(1)}, u32[]{:S(2)}, u32[]{:S(2)}) collective-permute-start(bf16[192,3584]{1,0:T(8,128)(2,1)S(1)} %bitcast.7), channel_id=1, source_target_pairs={{0,1},{1,0},{2,3},{3,2},{4,5},{5,4},{6,7},{7,6},{8,9},{9,8},{10,11... | collective-permute-start | bytes 4128776 | tf_op jit(solution)/shard_map/ppermute | solution.py:41
  21.1 8.2 %collective-permute-start.8 = (bf16[384,128]{1,0:T(8,128)(2,1)S(1)}, bf16[384,128]{1,0:T(8,128)(2,1)S(1)}, u32[]{:S(2)}, u32[]{:S(2)}) collective-permute-start(bf16[384,128]{1,0:T(8,128)(2,1)S(1)} %get-tuple-element.100), channel_id=1, source_target_pairs={{0,14},{1,15},{2,0},{3,1},{4,2},{5,3},{6,4},{7,5},{8,6},{9,7},{10,... | collective-permute-start | bytes 294920 | tf_op jit(solution)/shard_map/ppermute | solution.py:37
  25.4 3.9 %collective-permute-start.9 = (bf16[128,128]{1,0:T(8,128)(2,1)S(1)}, bf16[128,128]{1,0:T(8,128)(2,1)S(1)}, u32[]{:S(2)}, u32[]{:S(2)}) collective-permute-start(bf16[128,128]{1,0:T(8,128)(2,1)S(1)} %get-tuple-element.101), channel_id=1, source_target_pairs={{0,12},{1,13},{2,14},{3,15},{4,0},{5,1},{6,2},{7,3},{8,4},{9,5},{1... | collective-permute-start | bytes 98312 | tf_op jit(solution)/shard_map/ppermute | solution.py:37
  30.3 14.5 %collective-permute-start.12 = (bf16[1792,128]{1,0:T(8,128)(2,1)S(1)}, bf16[1792,128]{1,0:T(8,128)(2,1)S(1)}, u32[]{:S(2)}, u32[]{:S(2)}) collective-permute-start(bf16[1792,128]{1,0:T(8,128)(2,1)S(1)} %get-tuple-element.108), channel_id=1, source_target_pairs={{0,16},{1,17},{2,18},{3,19},{4,20},{5,21},{6,22},{7,23},{8,24},{9,... | collective-permute-start | bytes 1376264 | tf_op jit(solution)/shard_map/ppermute | solution.py:46
  31.9 7.3 %collective-permute-start.10 = (bf16[384,128]{1,0:T(8,128)(2,1)S(1)}, bf16[384,128]{1,0:T(8,128)(2,1)S(1)}, u32[]{:S(2)}, u32[]{:S(2)}) collective-permute-start(bf16[384,128]{1,0:T(8,128)(2,1)S(1)} %get-tuple-element.103.refs_5_), channel_id=1, source_target_pairs={{0,2},{1,3},{2,4},{3,5},{4,6},{5,7},{6,8},{7,9},{8,10},{9,11},{10,... | collective-permute-start | bytes 294920 | tf_op jit(solution)/shard_map/ppermute | solution.py:37
  31.9 6.8 %collective-permute-start.11 = (bf16[128,128]{1,0:T(8,128)(2,1)S(1)}, bf16[128,128]{1,0:T(8,128)(2,1)S(1)}, u32[]{:S(2)}, u32[]{:S(2)}) collective-permute-start(bf16[128,128]{1,0:T(8,128)(2,1)S(1)} %get-tuple-element.104), channel_id=1, source_target_pairs={{0,4},{1,5},{2,6},{3,7},{4,8},{5,9},{6,10},{7,11},{8,12},{9,13},{1... | collective-permute-start | bytes 98312 | tf_op jit(solution)/shard_map/ppermute | solution.py:37
  44.9 4.9 %collective-permute-start.13 = (bf16[448,128]{1,0:T(8,128)(2,1)S(1)}, bf16[448,128]{1,0:T(8,128)(2,1)S(1)}, u32[]{:S(2)}, u32[]{:S(2)}) collective-permute-start(bf16[448,128]{1,0:T(8,128)(2,1)S(1)} %get-tuple-element.117), channel_id=1, source_target_pairs={{0,4},{1,5},{2,6},{3,7},{4,0},{5,1},{6,2},{7,3},{8,12},{9,13},{10,... | collective-permute-start | bytes 344072 | tf_op jit(solution)/shard_map/ppermute | solution.py:46
  45.0 4.9 %collective-permute-start.14 = (bf16[448,128]{1,0:T(8,128)(2,1)S(1)}, bf16[448,128]{1,0:T(8,128)(2,1)S(1)}, u32[]{:S(2)}, u32[]{:S(2)}) collective-permute-start(bf16[448,128]{1,0:T(8,128)(2,1)S(1)} %get-tuple-element.118), channel_id=1, source_target_pairs={{0,2},{1,3},{2,0},{3,1},{4,6},{5,7},{6,4},{7,5},{8,10},{9,11},{10,... | collective-permute-start | bytes 344072 | tf_op jit(solution)/shard_map/ppermute | solution.py:46
  46.0 5.7 %collective-permute-start.15 = (bf16[448,128]{1,0:T(8,128)(2,1)S(1)}, bf16[448,128]{1,0:T(8,128)(2,1)S(1)}, u32[]{:S(2)}, u32[]{:S(2)}) collective-permute-start(bf16[448,128]{1,0:T(8,128)(2,1)S(1)} %get-tuple-element.119), channel_id=1, source_target_pairs={{0,6},{1,7},{2,4},{3,5},{4,2},{5,3},{6,0},{7,1},{8,14},{9,15},{10,... | collective-permute-start | bytes 344072 | tf_op jit(solution)/shard_map/ppermute | solution.py:46
  51.8 9.7 %collective-permute-start.19 = (bf16[192,896]{1,0:T(8,128)(2,1)S(1)}, bf16[192,896]{1,0:T(8,128)(2,1)S(1)}, u32[]{:S(2)}, u32[]{:S(2)}) collective-permute-start(bf16[192,896]{1,0:T(8,128)(2,1)S(1)} %get-tuple-element.123), channel_id=1, source_target_pairs={{0,1},{1,0},{2,3},{3,2},{4,5},{5,4},{6,7},{7,6},{8,9},{9,8},{10,11... | collective-permute-start | bytes 1032200 | tf_op jit(solution)/shard_map/ppermute | solution.py:41
  51.8 9.6 %collective-permute-start.16 = (bf16[448,128]{1,0:T(8,128)(2,1)S(1)}, bf16[448,128]{1,0:T(8,128)(2,1)S(1)}, u32[]{:S(2)}, u32[]{:S(2)}) collective-permute-start(bf16[448,128]{1,0:T(8,128)(2,1)S(1)} %reduce_step.4.held), channel_id=1, source_target_pairs={{0,8},{1,9},{2,10},{3,11},{4,12},{5,13},{6,14},{7,15},{8,0},{9,1},... | collective-permute-start | bytes 344072 | tf_op jit(solution)/shard_map/ppermute | solution.py:46
  54.4 7.1 %collective-permute-start.17 = (bf16[384,128]{1,0:T(8,128)(2,1)S(1)}, bf16[384,128]{1,0:T(8,128)(2,1)S(1)}, u32[]{:S(2)}, u32[]{:S(2)}) collective-permute-start(bf16[384,128]{1,0:T(8,128)(2,1)S(1)} %get-tuple-element.121), channel_id=1, source_target_pairs={{0,14},{1,15},{2,0},{3,1},{4,2},{5,3},{6,4},{7,5},{8,6},{9,7},{10,... | collective-permute-start | bytes 294920 | tf_op jit(solution)/shard_map/ppermute | solution.py:37
  56.8 4.7 %collective-permute-start.18 = (bf16[128,128]{1,0:T(8,128)(2,1)S(1)}, bf16[128,128]{1,0:T(8,128)(2,1)S(1)}, u32[]{:S(2)}, u32[]{:S(2)}) collective-permute-start(bf16[128,128]{1,0:T(8,128)(2,1)S(1)} %get-tuple-element.122), channel_id=1, source_target_pairs={{0,12},{1,13},{2,14},{3,15},{4,0},{5,1},{6,2},{7,3},{8,4},{9,5},{1... | collective-permute-start | bytes 98312 | tf_op jit(solution)/shard_map/ppermute | solution.py:37
  61.5 6.5 %collective-permute-start.21 = (bf16[448,128]{1,0:T(8,128)(2,1)S(1)}, bf16[448,128]{1,0:T(8,128)(2,1)S(1)}, u32[]{:S(2)}, u32[]{:S(2)}) collective-permute-start(bf16[448,128]{1,0:T(8,128)(2,1)S(1)} %reduce_step.5.refs_0_), channel_id=1, source_target_pairs={{0,4},{1,5},{2,6},{3,7},{4,0},{5,1},{6,2},{7,3},{8,12},{9,13},{10,... | collective-permute-start | bytes 344072 | tf_op jit(solution)/shard_map/ppermute | solution.py:46
  64.2 7.0 %collective-permute-start.22 = (bf16[448,128]{1,0:T(8,128)(2,1)S(1)}, bf16[448,128]{1,0:T(8,128)(2,1)S(1)}, u32[]{:S(2)}, u32[]{:S(2)}) collective-permute-start(bf16[448,128]{1,0:T(8,128)(2,1)S(1)} %reduce_step.5.refs_0_), channel_id=1, source_target_pairs={{0,2},{1,3},{2,0},{3,1},{4,6},{5,7},{6,4},{7,5},{8,10},{9,11},{10,... | collective-permute-start | bytes 344072 | tf_op jit(solution)/shard_map/ppermute | solution.py:46
  65.3 5.9 %collective-permute-start.23 = (bf16[448,128]{1,0:T(8,128)(2,1)S(1)}, bf16[448,128]{1,0:T(8,128)(2,1)S(1)}, u32[]{:S(2)}, u32[]{:S(2)}) collective-permute-start(bf16[448,128]{1,0:T(8,128)(2,1)S(1)} %reduce_step.5.refs_0_), channel_id=1, source_target_pairs={{0,6},{1,7},{2,4},{3,5},{4,2},{5,3},{6,0},{7,1},{8,14},{9,15},{10,... | collective-permute-start | bytes 344072 | tf_op jit(solution)/shard_map/ppermute | solution.py:46
  65.8 1.3 %collective-permute-start.20 = (bf16[192,128]{1,0:T(8,128)(2,1)S(1)}, bf16[192,128]{1,0:T(8,128)(2,1)S(1)}, u32[]{:S(2)}, u32[]{:S(2)}) collective-permute-start(bf16[192,128]{1,0:T(8,128)(2,1)S(1)} %get-tuple-element.131), channel_id=1, source_target_pairs={{0,1},{1,0},{2,3},{3,2},{4,5},{5,4},{6,7},{7,6},{8,9},{9,8},{10,11... | collective-permute-start | bytes 147464 | tf_op jit(solution)/shard_map/ppermute | solution.py:41
  65.9 5.9 %collective-permute-start.24 = (bf16[448,128]{1,0:T(8,128)(2,1)S(1)}, bf16[448,128]{1,0:T(8,128)(2,1)S(1)}, u32[]{:S(2)}, u32[]{:S(2)}) collective-permute-start(bf16[448,128]{1,0:T(8,128)(2,1)S(1)} %reduce_step.5.refs_0_), channel_id=1, source_target_pairs={{0,1},{1,0},{2,3},{3,2},{4,5},{5,4},{6,7},{7,6},{8,9},{9,8},{10,11... | collective-permute-start | bytes 344072 | tf_op jit(solution)/shard_map/ppermute | solution.py:41
  71.3 1.3 %collective-permute-start.25 = (bf16[448,128]{1,0:T(8,128)(2,1)S(1)}, bf16[448,128]{1,0:T(8,128)(2,1)S(1)}, u32[]{:S(2)}, u32[]{:S(2)}) collective-permute-start(bf16[448,128]{1,0:T(8,128)(2,1)S(1)} %collective-permute-done.21.refs_1_), channel_id=1, source_target_pairs={{0,1},{1,0},{2,3},{3,2},{4,5},{5,4},{6,7},{7,6},{8,9},{9,8},{10,11... | collective-permute-start | bytes 344072 | tf_op jit(solution)/shard_map/ppermute | solution.py:41
  71.3 1.5 %collective-permute-start.26 = (bf16[448,128]{1,0:T(8,128)(2,1)S(1)}, bf16[448,128]{1,0:T(8,128)(2,1)S(1)}, u32[]{:S(2)}, u32[]{:S(2)}) collective-permute-start(bf16[448,128]{1,0:T(8,128)(2,1)S(1)} %collective-permute-done.22.refs_2_), channel_id=1, source_target_pairs={{0,1},{1,0},{2,3},{3,2},{4,5},{5,4},{6,7},{7,6},{8,9},{9,8},{10,11... | collective-permute-start | bytes 344072 | tf_op jit(solution)/shard_map/ppermute | solution.py:41
  71.8 1.3 %collective-permute-start.27 = (bf16[448,128]{1,0:T(8,128)(2,1)S(1)}, bf16[448,128]{1,0:T(8,128)(2,1)S(1)}, u32[]{:S(2)}, u32[]{:S(2)}) collective-permute-start(bf16[448,128]{1,0:T(8,128)(2,1)S(1)} %collective-permute-done.23.refs_3_), channel_id=1, source_target_pairs={{0,1},{1,0},{2,3},{3,2},{4,5},{5,4},{6,7},{7,6},{8,9},{9,8},{10,11... | collective-permute-start | bytes 344072 | tf_op jit(solution)/shard_map/ppermute | solution.py:41

commit v7 on v6

--- a/solution.py
+++ b/solution.py
@@ -31,10 +31,14 @@
     return pltpu.CompilerParams(vmem_limit_bytes=mib * 1024 * 1024)
 
 
-def shifted(value, steps, cores=(0, 1)):
+def shifted(value, steps):
     count = lax.axis_size("seq")
-    pairs = [(i, (i + steps) % count) for i in range(count) if i % 2 in cores]
-    return lax.ppermute(value, "seq", pairs)
+    return lax.ppermute(value, "seq", [(i, (i + steps) % count) for i in range(count)])
+
+
+def shifted_odd(value, steps):
+    count = lax.axis_size("seq")
+    return lax.ppermute(value, "seq", [(i, i + steps) for i in range(1, count - steps, 2)])
 
 
 def swapped(value, axis, flip):
@@ -573,7 +577,7 @@
         own_keys,
     )
     near_keys, far_keys = lax.optimization_barrier(
-        (shifted(own_keys, 2), shifted(key_tail, 4, cores=(1,)))
+        (shifted(own_keys, 2), shifted_odd(key_tail, 4))
     )
     query_oth, grad_oth, marks_oth = (
         swapped(value, "seq", 1) for value in (query_out, grad_out, marks_own)

time: 74.5 us -> 74.5 us (level)
  starting transfers between devices: 33.5 us -> 31 us
  waiting for transfers between devices: 22.7 us -> 25.1 us
    ppermute x12, starting transfers between devices: 11.1 us -> 8.1 us  [swapped(): lax.ppermute(value, axis, [(i, i ^ flip) for i in range(lax.axis_size(axi...]
    ppermute x8, waiting for transfers between devices: 12.4 us -> 14.1 us  [the longest x7 14.1 us: shifted(): lax.ppermute(value, 'seq', [(i, (i + steps) % count) for i in range(count)])]
  transfers between devices with their start and end apart: 28 -> 28, of which waited for: 15 -> 14; matrix products, arithmetic and copies ran while one was open for 0% -> 0% of each run, Pallas kernels for 18% -> 18%
where the time goes in v7:
time: 74.5 us; the launch traced here: 74.3 us
  starting transfers between devices  31 us (42%)
  waiting for transfers between devices  25.1 us (34%)
  Pallas kernels  17.2 us (23%)
  between operations  0.97 us (1%)
    ppermute x7, waiting for transfers between devices, shifted(): lax.ppermute(value, 'seq', [(i, (i + steps) % count) for i in range(count)])  14.1 us
    ppermute x8, starting transfers between devices, crossed(): lax.ppermute(value, ('dp', 'seq'), [(i, i ^ flip) for i in range(count)])  11.9 us
    ppermute x7, starting transfers between devices, shifted(): lax.ppermute(value, 'seq', [(i, (i + steps) % count) for i in range(count)])  10.4 us
    ppermute x12, starting transfers between devices, swapped(): lax.ppermute(value, axis, [(i, i ^ flip) for i in range(lax.axis_size(axi...  8.1 us
    ppermute x8, waiting for transfers between devices, crossed(): lax.ppermute(value, ('dp', 'seq'), [(i, i ^ flip) for i in range(count)])  6.45 us
    pallas_call x1, Pallas kernels, key_terms(): pl.pallas_call(functools.partial(key_kernel, tok), out_shape=term_shapes(...  5.65 us
    ppermute x12, waiting for transfers between devices, swapped(): lax.ppermute(value, axis, [(i, i ^ flip) for i in range(lax.axis_size(axi...  4.55 us
    pallas_call x1, Pallas kernels, value_terms(): pl.pallas_call(functools.partial(value_kernel, tok), out_shape=term_shape...  3.85 us
  transfers between devices with their start and end apart: 28, of which 14 were waited for; matrix products, arithmetic and copies ran while one was open for 0% of the time, Pallas kernels for 18%

profile of v7, /device:TPU:0, one launch (start us, length us, event | category | flops | bytes accessed | tf_op | source)
XLA Modules:
  0.0 74.3 jit_solution(4456544788536103787)
XLA Ops:
  0.7 1.7 %split.1 = (bf16[192,896]{1,0:T(8,128)(2,1)S(1)}, bf16[192,896]{1,0:T(8,128)(2,1)S(1)}, bf16[192,896]{1,0:T(8,128)(2,1)S(1)}, bf16[192,896]{1,0:T(8,128)(2,1)S(1...) custom-call(bf16[192,1792]{1,0:T(8,128)(2,1)} %bitcast.9, ...), custom_call_target="tpu_custom_call" | custom-call | tf_op jit(solution)/shard_map/split/pallas_call | solution.py:96
  2.9 2.9 %collective-permute-start.6 = (bf16[1792,128]{1,0:T(8,128)(2,1)S(1)}, bf16[1792,128]{1,0:T(8,128)(2,1)S(1)}, u32[]{:S(2)}, u32[]{:S(2)}) collective-permute-start(bf16[1792,128]{1,0:T(8,128)(2,1)S(1)} %get-tuple-element.94.w_own), channel_id=1, source_target_pairs={{0,16},{16,0},{1,17},{17,1},{2,18},{18,2},{3,19},{19,3},{4,20},{20... | collective-permute-start | bytes 1376264 | tf_op jit(solution)/shard_map/ppermute | solution.py:45
  5.9 1.5 %collective-permute-start = (bf16[192,256]{1,0:T(8,128)(2,1)S(1)}, bf16[192,256]{1,0:T(8,128)(2,1)S(1)}, u32[]{:S(2)}, u32[]{:S(2)}) collective-permute-start(bf16[192,256]{1,0:T(8,128)(2,1)S(1)} %bitcast.13), channel_id=1, source_target_pairs={{0,2},{1,3},{2,4},{3,5},{4,6},{5,7},{6,8},{7,9},{8,10},{9,11},{10,... | collective-permute-start | bytes 294920 | tf_op jit(solution)/shard_map/ppermute | solution.py:36
  7.4 0.7 collective-permute-start.1
  8.1 3.4 %collective-permute-start.4 = (s32[15,192]{1,0:T(8,128)S(1)}, s32[15,192]{1,0:T(8,128)S(1)}, u32[]{:S(2)}, u32[]{:S(2)}) collective-permute-start(s32[15,192]{1,0:T(8,128)S(1)} %get-tuple-element.77.refs_6_.l_own), channel_id=1, source_target_pairs={{0,1},{1,0},{2,3},{3,2},{4,5},{5,4},{6,7},{7,6},{8,9},{9,8},{10,11... | collective-permute-start | bytes 34568 | tf_op jit(solution)/shard_map/ppermute | solution.py:45
  11.4 1.8 %collective-permute-done.near = bf16[192,256]{1,0:T(8,128)(2,1)S(1)} collective-permute-done((bf16[192,256]{1,0:T(8,128)(2,1)S(1)}, bf16[192,256]{1,0:T(8,128)(2,1)S(1)}, u32[]{:S(2)}, u32[]{:S(2)}) %collective-permute-start) | collective-permute-done | bytes 98336 | tf_op jit(solution)/shard_map/ppermute | solution.py:36
  13.2 0.9 %pack.1 = (bf16[512,128]{1,0:T(8,128)(2,1)S(1)}, bf16[512,128]{1,0:T(8,128)(2,1)S(1)}) custom-call(bf16[192,256]{1,0:T(8,128)(2,1)} %bitcast.12, bf16[192,256]{1,0:T(8,128)(2,1)S(1)} %collective-permute-done.near, bf16[128,256]{1,0:T(8,128)(2,1)S(1)} %collective-permute-done.1.far), custom_call_target="tpu_custom_call" | custom-call | tf_op jit(solution)/shard_map/pack/pallas_call | solution.py:135
  14.1 2.5 %collective-permute-done.6.w_oth = bf16[1792,128]{1,0:T(8,128)(2,1)S(1)} collective-permute-done((bf16[1792,128]{1,0:T(8,128)(2,1)S(1)}, bf16[1792,128]{1,0:T(8,128)(2,1)S(1)}, u32[]{:S(2)}, u32[]{:S(2)}) %collective-permute-start.6) | collective-permute-done | bytes 458784 | tf_op jit(solution)/shard_map/ppermute | solution.py:45
  16.6 3.9 %value_terms.1 = (f32[384,128]{1,0:T(8,128)S(1)}, bf16[384,128]{1,0:T(8,128)(2,1)S(1)}, bf16[128,128]{1,0:T(8,128)(2,1)S(1)}, f32[21,128]{1,0:T(8,128)S(1)}, f32...) custom-call(bf16[192,896]{1,0:T(8,128)(2,1)S(1)} %get-tuple-element., ...), custom_call_target="tpu_custom_call" | custom-call | tf_op jit(solution)/shard_map/value_terms/pallas_call | solution.py:303
  20.5 4.9 %collective-permute-start.8 = (bf16[384,128]{1,0:T(8,128)(2,1)S(1)}, bf16[384,128]{1,0:T(8,128)(2,1)S(1)}, u32[]{:S(2)}, u32[]{:S(2)}) collective-permute-start(bf16[384,128]{1,0:T(8,128)(2,1)S(1)} %get-tuple-element.100), channel_id=1, source_target_pairs={{0,14},{1,15},{2,0},{3,1},{4,2},{5,3},{6,4},{7,5},{8,6},{9,7},{10,... | collective-permute-start | bytes 294920 | tf_op jit(solution)/shard_map/ppermute | solution.py:36
  25.8 2.0 %project.1 = (bf16[384,128]{1,0:T(8,128)(2,1)S(1)}, bf16[128,128]{1,0:T(8,128)(2,1)S(1)}, bf16[384,3584]{1,0:T(8,128)(2,1)S(1)}) custom-call(bf16[192,3584]{1,0:T(8,128)(2,1)S(1)} %bitcast.8, bf16[192,3584]{1,0:T(8,128)(2,1)S(1)} %collective-permute-done.7.h_oth, s32[15,192]{1,0:T(8,128)S(1)} %get-tuple-element.77.refs_6_.l_own, ...), custom_call_target="tpu_custom_call" | custom-call | tf_op jit(solution)/shard_map/project/pallas_call | solution.py:389
  27.8 1.5 %collective-permute-done.9.far = bf16[128,128]{1,0:T(8,128)(2,1)S(1)} collective-permute-done((bf16[128,128]{1,0:T(8,128)(2,1)S(1)}, bf16[128,128]{1,0:T(8,128)(2,1)S(1)}, u32[]{:S(2)}, u32[]{:S(2)}) %collective-permute-start.9) | collective-permute-done | bytes 32800 | tf_op jit(solution)/shard_map/ppermute | solution.py:36
  29.3 1.0 %weight_terms.1 = (f32[1792,128]{1,0:T(8,128)S(1)}, bf16[1792,128]{1,0:T(8,128)(2,1)S(1)}) custom-call(bf16[384,3584]{1,0:T(8,128)(2,1)S(1)} %get-tuple-element.98.spiked, f32[384,128]{1,0:T(8,128)S(1)} %get-tuple-element.99.own, bf16[384,128]{1,0:T(8,128)(2,1)S(1)} %collective-permute-done.8.near, bf16[128,128]{1,0:T(8,128)(2,1)S(1)} %collective-permute-done.9.far), custom_call_target="tpu_custom_call" | custom-call | tf_op jit(solution)/shard_map/weight_terms/pallas_call | solution.py:441
  30.3 1.6 %collective-permute-start.12 = (bf16[1792,128]{1,0:T(8,128)(2,1)S(1)}, bf16[1792,128]{1,0:T(8,128)(2,1)S(1)}, u32[]{:S(2)}, u32[]{:S(2)}) collective-permute-start(bf16[1792,128]{1,0:T(8,128)(2,1)S(1)} %get-tuple-element.108), channel_id=1, source_target_pairs={{0,16},{1,17},{2,18},{3,19},{4,20},{5,21},{6,22},{7,23},{8,24},{9,... | collective-permute-start | bytes 1376264 | tf_op jit(solution)/shard_map/ppermute | solution.py:50
  31.9 1.1 %collective-permute-start.11 = (bf16[128,128]{1,0:T(8,128)(2,1)S(1)}, bf16[128,128]{1,0:T(8,128)(2,1)S(1)}, u32[]{:S(2)}, u32[]{:S(2)}) collective-permute-start(bf16[128,128]{1,0:T(8,128)(2,1)S(1)} %get-tuple-element.104), channel_id=1, source_target_pairs={{0,4},{1,5},{2,6},{3,7},{4,8},{5,9},{6,10},{7,11},{8,12},{9,13},{1... | collective-permute-start | bytes 98312 | tf_op jit(solution)/shard_map/ppermute | solution.py:36
  32.9 5.7 %collective-permute-done.11.refs_7_ = bf16[128,128]{1,0:T(8,128)(2,1)S(1)} collective-permute-done((bf16[128,128]{1,0:T(8,128)(2,1)S(1)}, bf16[128,128]{1,0:T(8,128)(2,1)S(1)}, u32[]{:S(2)}, u32[]{:S(2)}) %collective-permute-start.11) | collective-permute-done | bytes 32800 | tf_op jit(solution)/shard_map/ppermute | solution.py:36
  38.6 0.5 collective-permute-done.10.refs_6_
  39.2 5.7 %key_terms.1 = (f32[384,128]{1,0:T(8,128)S(1)}, bf16[384,128]{1,0:T(8,128)(2,1)S(1)}, bf16[128,128]{1,0:T(8,128)(2,1)S(1)}, bf16[192,896]{1,0:T(8,128)(2,1)S(1)}, bf16[192,896]{1,0:T(8,128)(2,1)S(1)}) custom-call(bf16[384,896]{1,0:T(8,128)(2,1)S(1)} %get-tuple-element.88.refs_0_, bf16[384,896]{1,0:T(8,128)(2,1)S(1)} %get-tuple-element.89.refs_1_, ...), custom_call_target="tpu_custom_call" | custom-call | tf_op jit(solution)/shard_map/key_terms/pallas_call | solution.py:319
  45.0 1.0 %collective-permute-start.14 = (bf16[448,128]{1,0:T(8,128)(2,1)S(1)}, bf16[448,128]{1,0:T(8,128)(2,1)S(1)}, u32[]{:S(2)}, u32[]{:S(2)}) collective-permute-start(bf16[448,128]{1,0:T(8,128)(2,1)S(1)} %get-tuple-element.118), channel_id=1, source_target_pairs={{0,2},{1,3},{2,0},{3,1},{4,6},{5,7},{6,4},{7,5},{8,10},{9,11},{10,... | collective-permute-start | bytes 344072 | tf_op jit(solution)/shard_map/ppermute | solution.py:50
  46.0 2.5 %collective-permute-start.15 = (bf16[448,128]{1,0:T(8,128)(2,1)S(1)}, bf16[448,128]{1,0:T(8,128)(2,1)S(1)}, u32[]{:S(2)}, u32[]{:S(2)}) collective-permute-start(bf16[448,128]{1,0:T(8,128)(2,1)S(1)} %get-tuple-element.119), channel_id=1, source_target_pairs={{0,6},{1,7},{2,4},{3,5},{4,2},{5,3},{6,0},{7,1},{8,14},{9,15},{10,... | collective-permute-start | bytes 344072 | tf_op jit(solution)/shard_map/ppermute | solution.py:50
  48.5 1.3 %collective-permute-done.13.refs_0_ = bf16[448,128]{1,0:T(8,128)(2,1)S(1)} collective-permute-done((bf16[448,128]{1,0:T(8,128)(2,1)S(1)}, bf16[448,128]{1,0:T(8,128)(2,1)S(1)}, u32[]{:S(2)}, u32[]{:S(2)}) %collective-permute-start.13) | collective-permute-done | bytes 114720 | tf_op jit(solution)/shard_map/ppermute | solution.py:50
  49.9 1.8 %collective-permute-done.15.refs_2_ = bf16[448,128]{1,0:T(8,128)(2,1)S(1)} collective-permute-done((bf16[448,128]{1,0:T(8,128)(2,1)S(1)}, bf16[448,128]{1,0:T(8,128)(2,1)S(1)}, u32[]{:S(2)}, u32[]{:S(2)}) %collective-permute-start.15) | collective-permute-done | bytes 114720 | tf_op jit(solution)/shard_map/ppermute | solution.py:50
  51.8 2.5 %collective-permute-start.16 = (bf16[448,128]{1,0:T(8,128)(2,1)S(1)}, bf16[448,128]{1,0:T(8,128)(2,1)S(1)}, u32[]{:S(2)}, u32[]{:S(2)}) collective-permute-start(bf16[448,128]{1,0:T(8,128)(2,1)S(1)} %reduce_step.4.held), channel_id=1, source_target_pairs={{0,8},{1,9},{2,10},{3,11},{4,12},{5,13},{6,14},{7,15},{8,0},{9,1},... | collective-permute-start | bytes 344072 | tf_op jit(solution)/shard_map/ppermute | solution.py:50
  54.4 2.4 %collective-permute-start.17 = (bf16[384,128]{1,0:T(8,128)(2,1)S(1)}, bf16[384,128]{1,0:T(8,128)(2,1)S(1)}, u32[]{:S(2)}, u32[]{:S(2)}) collective-permute-start(bf16[384,128]{1,0:T(8,128)(2,1)S(1)} %get-tuple-element.121), channel_id=1, source_target_pairs={{0,14},{1,15},{2,0},{3,1},{4,2},{5,3},{6,4},{7,5},{8,6},{9,7},{10,... | collective-permute-start | bytes 294920 | tf_op jit(solution)/shard_map/ppermute | solution.py:36
  56.8 4.6 %collective-permute-done.18.far = bf16[128,128]{1,0:T(8,128)(2,1)S(1)} collective-permute-done((bf16[128,128]{1,0:T(8,128)(2,1)S(1)}, bf16[128,128]{1,0:T(8,128)(2,1)S(1)}, u32[]{:S(2)}, u32[]{:S(2)}) %collective-permute-start.18) | collective-permute-done | bytes 32800 | tf_op jit(solution)/shard_map/ppermute | solution.py:36
  61.5 2.7 %collective-permute-start.21 = (bf16[448,128]{1,0:T(8,128)(2,1)S(1)}, bf16[448,128]{1,0:T(8,128)(2,1)S(1)}, u32[]{:S(2)}, u32[]{:S(2)}) collective-permute-start(bf16[448,128]{1,0:T(8,128)(2,1)S(1)} %reduce_step.5.refs_0_), channel_id=1, source_target_pairs={{0,4},{1,5},{2,6},{3,7},{4,0},{5,1},{6,2},{7,3},{8,12},{9,13},{10,... | collective-permute-start | bytes 344072 | tf_op jit(solution)/shard_map/ppermute | solution.py:50
  64.2 1.1 %collective-permute-start.22 = (bf16[448,128]{1,0:T(8,128)(2,1)S(1)}, bf16[448,128]{1,0:T(8,128)(2,1)S(1)}, u32[]{:S(2)}, u32[]{:S(2)}) collective-permute-start(bf16[448,128]{1,0:T(8,128)(2,1)S(1)} %reduce_step.5.refs_0_), channel_id=1, source_target_pairs={{0,2},{1,3},{2,0},{3,1},{4,6},{5,7},{6,4},{7,5},{8,10},{9,11},{10,... | collective-permute-start | bytes 344072 | tf_op jit(solution)/shard_map/ppermute | solution.py:50
  66.4 0.7 collective-permute-done.20.k_oth
  67.1 0.9 %place_tokens.1 = (bf16[192,1792]{1,0:T(8,128)(2,1)}, bf16[192,256]{1,0:T(8,128)(2,1)}) custom-call(bf16[192,896]{1,0:T(8,128)(2,1)S(1)} %get-tuple-element.105.q_own, bf16[192,896]{1,0:T(8,128)(2,1)S(1)} %collective-permute-done.19.q_oth, bf16[192,128]{1,0:T(8,128)(2,1)S(1)} %get-tuple-element.130.k_own, bf16[192,128]{1,0:T(8,128)(2,1)S(1)} %collective-permute-done.20.k_oth), custom_call_target="tpu_custom_call" | custom-call | tf_op jit(solution)/shard_map/place_tokens/pallas_call | solution.py:526
  68.0 3.2 %collective-permute-done.22.refs_2_ = bf16[448,128]{1,0:T(8,128)(2,1)S(1)} collective-permute-done((bf16[448,128]{1,0:T(8,128)(2,1)S(1)}, bf16[448,128]{1,0:T(8,128)(2,1)S(1)}, u32[]{:S(2)}, u32[]{:S(2)}) %collective-permute-start.22) | collective-permute-done | bytes 114720 | tf_op jit(solution)/shard_map/ppermute | solution.py:50
  71.8 0.8 %collective-permute-done.25.refs_5_ = bf16[448,128]{1,0:T(8,128)(2,1)S(1)} collective-permute-done((bf16[448,128]{1,0:T(8,128)(2,1)S(1)}, bf16[448,128]{1,0:T(8,128)(2,1)S(1)}, u32[]{:S(2)}, u32[]{:S(2)}) %collective-permute-start.25) | collective-permute-done | bytes 114720 | tf_op jit(solution)/shard_map/ppermute | solution.py:45
  73.1 1.0 %place_weight.1 = bf16[1792,256]{1,0:T(8,128)(2,1)} custom-call(bf16[448,128]{1,0:T(8,128)(2,1)S(1)} %reduce_step.5.refs_0_, bf16[448,128]{1,0:T(8,128)(2,1)S(1)} %collective-permute-done.21.refs_1_, bf16[448,128]{1,0:T(8,128)(2,1)S(1)} %collective-permute-done.22.refs_2_, bf16[448,128]{1,0:T(8,128)(2,1)S(1)} %collective-permute-done.23.refs_3_, ...), custom_call_target="tpu_custom_call" | custom-call | tf_op jit(solution)/shard_map/place_weight/pallas_call | solution.py:502
  (40 shorter events, 3.7 us)
Async XLA Ops:
  0.6 5.2 %copy-start.1 = (bf16[1,192,256]{2,1,0:T(8,128)(2,1)S(1)}, bf16[1,192,256]{2,1,0:T(8,128)(2,1)}, u32[]{:S(2)}) copy-start(bf16[1,192,256]{2,1,0:T(8,128)(2,1)} %param.11) | copy-start | bytes 294916
  0.6 16.0 %copy-start = (bf16[1,192,3584]{2,1,0:T(8,128)(2,1)S(1)}, bf16[1,192,3584]{2,1,0:T(8,128)(2,1)}, u32[]{:S(2)}) copy-start(bf16[1,192,3584]{2,1,0:T(8,128)(2,1)} %param.7) | copy-start | bytes 4128772
  2.3 10.8 %collective-permute-start.2 = (bf16[192,896]{1,0:T(8,128)(2,1)S(1)}, bf16[192,896]{1,0:T(8,128)(2,1)S(1)}, u32[]{:S(2)}, u32[]{:S(2)}) collective-permute-start(bf16[192,896]{1,0:T(8,128)(2,1)S(1)} %get-tuple-element.75), channel_id=1, source_target_pairs={{0,1},{1,0},{2,3},{3,2},{4,5},{5,4},{6,7},{7,6},{8,9},{9,8},{10,11... | collective-permute-start | bytes 1032200 | tf_op jit(solution)/shard_map/ppermute | solution.py:45
  2.9 10.3 %collective-permute-start.3 = (bf16[192,896]{1,0:T(8,128)(2,1)S(1)}, bf16[192,896]{1,0:T(8,128)(2,1)S(1)}, u32[]{:S(2)}, u32[]{:S(2)}) collective-permute-start(bf16[192,896]{1,0:T(8,128)(2,1)S(1)} %get-tuple-element.76), channel_id=1, source_target_pairs={{0,1},{1,0},{2,3},{3,2},{4,5},{5,4},{6,7},{7,6},{8,9},{9,8},{10,11... | collective-permute-start | bytes 1032200 | tf_op jit(solution)/shard_map/ppermute | solution.py:45
  2.9 13.7 %collective-permute-start.6 = (bf16[1792,128]{1,0:T(8,128)(2,1)S(1)}, bf16[1792,128]{1,0:T(8,128)(2,1)S(1)}, u32[]{:S(2)}, u32[]{:S(2)}) collective-permute-start(bf16[1792,128]{1,0:T(8,128)(2,1)S(1)} %get-tuple-element.94.w_own), channel_id=1, source_target_pairs={{0,16},{16,0},{1,17},{17,1},{2,18},{18,2},{3,19},{19,3},{4,20},{20... | collective-permute-start | bytes 1376264 | tf_op jit(solution)/shard_map/ppermute | solution.py:45
  5.9 7.3 %collective-permute-start = (bf16[192,256]{1,0:T(8,128)(2,1)S(1)}, bf16[192,256]{1,0:T(8,128)(2,1)S(1)}, u32[]{:S(2)}, u32[]{:S(2)}) collective-permute-start(bf16[192,256]{1,0:T(8,128)(2,1)S(1)} %bitcast.13), channel_id=1, source_target_pairs={{0,2},{1,3},{2,4},{3,5},{4,6},{5,7},{6,8},{7,9},{8,10},{9,11},{10,... | collective-permute-start | bytes 294920 | tf_op jit(solution)/shard_map/ppermute | solution.py:36
  7.4 0.7 collective-permute-start.1
  8.1 5.1 %collective-permute-start.4 = (s32[15,192]{1,0:T(8,128)S(1)}, s32[15,192]{1,0:T(8,128)S(1)}, u32[]{:S(2)}, u32[]{:S(2)}) collective-permute-start(s32[15,192]{1,0:T(8,128)S(1)} %get-tuple-element.77.refs_6_.l_own), channel_id=1, source_target_pairs={{0,1},{1,0},{2,3},{3,2},{4,5},{5,4},{6,7},{7,6},{8,9},{9,8},{10,11... | collective-permute-start | bytes 34568 | tf_op jit(solution)/shard_map/ppermute | solution.py:45
  14.0 2.6 %collective-permute-start.5 = (bf16[512,128]{1,0:T(8,128)(2,1)S(1)}, bf16[512,128]{1,0:T(8,128)(2,1)S(1)}, u32[]{:S(2)}, u32[]{:S(2)}) collective-permute-start(bf16[512,128]{1,0:T(8,128)(2,1)S(1)} %get-tuple-element.84), channel_id=1, source_target_pairs={{0,1},{1,0},{2,3},{3,2},{4,5},{5,4},{6,7},{7,6},{8,9},{9,8},{10,11... | collective-permute-start | bytes 393224 | tf_op jit(solution)/shard_map/ppermute | solution.py:45
  16.6 9.2 %collective-permute-start.7 = (bf16[192,3584]{1,0:T(8,128)(2,1)S(1)}, bf16[192,3584]{1,0:T(8,128)(2,1)S(1)}, u32[]{:S(2)}, u32[]{:S(2)}) collective-permute-start(bf16[192,3584]{1,0:T(8,128)(2,1)S(1)} %bitcast.7), channel_id=1, source_target_pairs={{0,1},{1,0},{2,3},{3,2},{4,5},{5,4},{6,7},{7,6},{8,9},{9,8},{10,11... | collective-permute-start | bytes 4128776 | tf_op jit(solution)/shard_map/ppermute | solution.py:45
  20.5 8.8 %collective-permute-start.8 = (bf16[384,128]{1,0:T(8,128)(2,1)S(1)}, bf16[384,128]{1,0:T(8,128)(2,1)S(1)}, u32[]{:S(2)}, u32[]{:S(2)}) collective-permute-start(bf16[384,128]{1,0:T(8,128)(2,1)S(1)} %get-tuple-element.100), channel_id=1, source_target_pairs={{0,14},{1,15},{2,0},{3,1},{4,2},{5,3},{6,4},{7,5},{8,6},{9,7},{10,... | collective-permute-start | bytes 294920 | tf_op jit(solution)/shard_map/ppermute | solution.py:36
  25.4 3.9 %collective-permute-start.9 = (bf16[128,128]{1,0:T(8,128)(2,1)S(1)}, bf16[128,128]{1,0:T(8,128)(2,1)S(1)}, u32[]{:S(2)}, u32[]{:S(2)}) collective-permute-start(bf16[128,128]{1,0:T(8,128)(2,1)S(1)} %get-tuple-element.101), channel_id=1, source_target_pairs={{0,12},{1,13},{2,14},{3,15},{4,0},{5,1},{6,2},{7,3},{8,4},{9,5},{1... | collective-permute-start | bytes 98312 | tf_op jit(solution)/shard_map/ppermute | solution.py:36
  30.3 14.5 %collective-permute-start.12 = (bf16[1792,128]{1,0:T(8,128)(2,1)S(1)}, bf16[1792,128]{1,0:T(8,128)(2,1)S(1)}, u32[]{:S(2)}, u32[]{:S(2)}) collective-permute-start(bf16[1792,128]{1,0:T(8,128)(2,1)S(1)} %get-tuple-element.108), channel_id=1, source_target_pairs={{0,16},{1,17},{2,18},{3,19},{4,20},{5,21},{6,22},{7,23},{8,24},{9,... | collective-permute-start | bytes 1376264 | tf_op jit(solution)/shard_map/ppermute | solution.py:50
  31.9 7.3 %collective-permute-start.10 = (bf16[384,128]{1,0:T(8,128)(2,1)S(1)}, bf16[384,128]{1,0:T(8,128)(2,1)S(1)}, u32[]{:S(2)}, u32[]{:S(2)}) collective-permute-start(bf16[384,128]{1,0:T(8,128)(2,1)S(1)} %get-tuple-element.103.refs_5_), channel_id=1, source_target_pairs={{0,2},{1,3},{2,4},{3,5},{4,6},{5,7},{6,8},{7,9},{8,10},{9,11},{10,... | collective-permute-start | bytes 294920 | tf_op jit(solution)/shard_map/ppermute | solution.py:36
  31.9 6.8 %collective-permute-start.11 = (bf16[128,128]{1,0:T(8,128)(2,1)S(1)}, bf16[128,128]{1,0:T(8,128)(2,1)S(1)}, u32[]{:S(2)}, u32[]{:S(2)}) collective-permute-start(bf16[128,128]{1,0:T(8,128)(2,1)S(1)} %get-tuple-element.104), channel_id=1, source_target_pairs={{0,4},{1,5},{2,6},{3,7},{4,8},{5,9},{6,10},{7,11},{8,12},{9,13},{1... | collective-permute-start | bytes 98312 | tf_op jit(solution)/shard_map/ppermute | solution.py:36
  44.9 4.9 %collective-permute-start.13 = (bf16[448,128]{1,0:T(8,128)(2,1)S(1)}, bf16[448,128]{1,0:T(8,128)(2,1)S(1)}, u32[]{:S(2)}, u32[]{:S(2)}) collective-permute-start(bf16[448,128]{1,0:T(8,128)(2,1)S(1)} %get-tuple-element.117), channel_id=1, source_target_pairs={{0,4},{1,5},{2,6},{3,7},{4,0},{5,1},{6,2},{7,3},{8,12},{9,13},{10,... | collective-permute-start | bytes 344072 | tf_op jit(solution)/shard_map/ppermute | solution.py:50
  45.0 4.9 %collective-permute-start.14 = (bf16[448,128]{1,0:T(8,128)(2,1)S(1)}, bf16[448,128]{1,0:T(8,128)(2,1)S(1)}, u32[]{:S(2)}, u32[]{:S(2)}) collective-permute-start(bf16[448,128]{1,0:T(8,128)(2,1)S(1)} %get-tuple-element.118), channel_id=1, source_target_pairs={{0,2},{1,3},{2,0},{3,1},{4,6},{5,7},{6,4},{7,5},{8,10},{9,11},{10,... | collective-permute-start | bytes 344072 | tf_op jit(solution)/shard_map/ppermute | solution.py:50
  46.0 5.7 %collective-permute-start.15 = (bf16[448,128]{1,0:T(8,128)(2,1)S(1)}, bf16[448,128]{1,0:T(8,128)(2,1)S(1)}, u32[]{:S(2)}, u32[]{:S(2)}) collective-permute-start(bf16[448,128]{1,0:T(8,128)(2,1)S(1)} %get-tuple-element.119), channel_id=1, source_target_pairs={{0,6},{1,7},{2,4},{3,5},{4,2},{5,3},{6,0},{7,1},{8,14},{9,15},{10,... | collective-permute-start | bytes 344072 | tf_op jit(solution)/shard_map/ppermute | solution.py:50
  51.8 9.7 %collective-permute-start.19 = (bf16[192,896]{1,0:T(8,128)(2,1)S(1)}, bf16[192,896]{1,0:T(8,128)(2,1)S(1)}, u32[]{:S(2)}, u32[]{:S(2)}) collective-permute-start(bf16[192,896]{1,0:T(8,128)(2,1)S(1)} %get-tuple-element.123), channel_id=1, source_target_pairs={{0,1},{1,0},{2,3},{3,2},{4,5},{5,4},{6,7},{7,6},{8,9},{9,8},{10,11... | collective-permute-start | bytes 1032200 | tf_op jit(solution)/shard_map/ppermute | solution.py:45
  51.8 9.6 %collective-permute-start.16 = (bf16[448,128]{1,0:T(8,128)(2,1)S(1)}, bf16[448,128]{1,0:T(8,128)(2,1)S(1)}, u32[]{:S(2)}, u32[]{:S(2)}) collective-permute-start(bf16[448,128]{1,0:T(8,128)(2,1)S(1)} %reduce_step.4.held), channel_id=1, source_target_pairs={{0,8},{1,9},{2,10},{3,11},{4,12},{5,13},{6,14},{7,15},{8,0},{9,1},... | collective-permute-start | bytes 344072 | tf_op jit(solution)/shard_map/ppermute | solution.py:50
  54.4 7.1 %collective-permute-start.17 = (bf16[384,128]{1,0:T(8,128)(2,1)S(1)}, bf16[384,128]{1,0:T(8,128)(2,1)S(1)}, u32[]{:S(2)}, u32[]{:S(2)}) collective-permute-start(bf16[384,128]{1,0:T(8,128)(2,1)S(1)} %get-tuple-element.121), channel_id=1, source_target_pairs={{0,14},{1,15},{2,0},{3,1},{4,2},{5,3},{6,4},{7,5},{8,6},{9,7},{10,... | collective-permute-start | bytes 294920 | tf_op jit(solution)/shard_map/ppermute | solution.py:36
  56.8 4.7 %collective-permute-start.18 = (bf16[128,128]{1,0:T(8,128)(2,1)S(1)}, bf16[128,128]{1,0:T(8,128)(2,1)S(1)}, u32[]{:S(2)}, u32[]{:S(2)}) collective-permute-start(bf16[128,128]{1,0:T(8,128)(2,1)S(1)} %get-tuple-element.122), channel_id=1, source_target_pairs={{0,12},{1,13},{2,14},{3,15},{4,0},{5,1},{6,2},{7,3},{8,4},{9,5},{1... | collective-permute-start | bytes 98312 | tf_op jit(solution)/shard_map/ppermute | solution.py:36
  61.5 6.5 %collective-permute-start.21 = (bf16[448,128]{1,0:T(8,128)(2,1)S(1)}, bf16[448,128]{1,0:T(8,128)(2,1)S(1)}, u32[]{:S(2)}, u32[]{:S(2)}) collective-permute-start(bf16[448,128]{1,0:T(8,128)(2,1)S(1)} %reduce_step.5.refs_0_), channel_id=1, source_target_pairs={{0,4},{1,5},{2,6},{3,7},{4,0},{5,1},{6,2},{7,3},{8,12},{9,13},{10,... | collective-permute-start | bytes 344072 | tf_op jit(solution)/shard_map/ppermute | solution.py:50
  64.2 7.0 %collective-permute-start.22 = (bf16[448,128]{1,0:T(8,128)(2,1)S(1)}, bf16[448,128]{1,0:T(8,128)(2,1)S(1)}, u32[]{:S(2)}, u32[]{:S(2)}) collective-permute-start(bf16[448,128]{1,0:T(8,128)(2,1)S(1)} %reduce_step.5.refs_0_), channel_id=1, source_target_pairs={{0,2},{1,3},{2,0},{3,1},{4,6},{5,7},{6,4},{7,5},{8,10},{9,11},{10,... | collective-permute-start | bytes 344072 | tf_op jit(solution)/shard_map/ppermute | solution.py:50
  65.3 5.9 %collective-permute-start.23 = (bf16[448,128]{1,0:T(8,128)(2,1)S(1)}, bf16[448,128]{1,0:T(8,128)(2,1)S(1)}, u32[]{:S(2)}, u32[]{:S(2)}) collective-permute-start(bf16[448,128]{1,0:T(8,128)(2,1)S(1)} %reduce_step.5.refs_0_), channel_id=1, source_target_pairs={{0,6},{1,7},{2,4},{3,5},{4,2},{5,3},{6,0},{7,1},{8,14},{9,15},{10,... | collective-permute-start | bytes 344072 | tf_op jit(solution)/shard_map/ppermute | solution.py:50
  65.8 1.3 %collective-permute-start.20 = (bf16[192,128]{1,0:T(8,128)(2,1)S(1)}, bf16[192,128]{1,0:T(8,128)(2,1)S(1)}, u32[]{:S(2)}, u32[]{:S(2)}) collective-permute-start(bf16[192,128]{1,0:T(8,128)(2,1)S(1)} %get-tuple-element.131), channel_id=1, source_target_pairs={{0,1},{1,0},{2,3},{3,2},{4,5},{5,4},{6,7},{7,6},{8,9},{9,8},{10,11... | collective-permute-start | bytes 147464 | tf_op jit(solution)/shard_map/ppermute | solution.py:45
  65.9 5.9 %collective-permute-start.24 = (bf16[448,128]{1,0:T(8,128)(2,1)S(1)}, bf16[448,128]{1,0:T(8,128)(2,1)S(1)}, u32[]{:S(2)}, u32[]{:S(2)}) collective-permute-start(bf16[448,128]{1,0:T(8,128)(2,1)S(1)} %reduce_step.5.refs_0_), channel_id=1, source_target_pairs={{0,1},{1,0},{2,3},{3,2},{4,5},{5,4},{6,7},{7,6},{8,9},{9,8},{10,11... | collective-permute-start | bytes 344072 | tf_op jit(solution)/shard_map/ppermute | solution.py:45
  71.3 1.3 %collective-permute-start.25 = (bf16[448,128]{1,0:T(8,128)(2,1)S(1)}, bf16[448,128]{1,0:T(8,128)(2,1)S(1)}, u32[]{:S(2)}, u32[]{:S(2)}) collective-permute-start(bf16[448,128]{1,0:T(8,128)(2,1)S(1)} %collective-permute-done.21.refs_1_), channel_id=1, source_target_pairs={{0,1},{1,0},{2,3},{3,2},{4,5},{5,4},{6,7},{7,6},{8,9},{9,8},{10,11... | collective-permute-start | bytes 344072 | tf_op jit(solution)/shard_map/ppermute | solution.py:45
  71.3 1.5 %collective-permute-start.26 = (bf16[448,128]{1,0:T(8,128)(2,1)S(1)}, bf16[448,128]{1,0:T(8,128)(2,1)S(1)}, u32[]{:S(2)}, u32[]{:S(2)}) collective-permute-start(bf16[448,128]{1,0:T(8,128)(2,1)S(1)} %collective-permute-done.22.refs_2_), channel_id=1, source_target_pairs={{0,1},{1,0},{2,3},{3,2},{4,5},{5,4},{6,7},{7,6},{8,9},{9,8},{10,11... | collective-permute-start | bytes 344072 | tf_op jit(solution)/shard_map/ppermute | solution.py:45
  71.8 1.3 %collective-permute-start.27 = (bf16[448,128]{1,0:T(8,128)(2,1)S(1)}, bf16[448,128]{1,0:T(8,128)(2,1)S(1)}, u32[]{:S(2)}, u32[]{:S(2)}) collective-permute-start(bf16[448,128]{1,0:T(8,128)(2,1)S(1)} %collective-permute-done.23.refs_3_), channel_id=1, source_target_pairs={{0,1},{1,0},{2,3},{3,2},{4,5},{5,4},{6,7},{7,6},{8,9},{9,8},{10,11... | collective-permute-start | bytes 344072 | tf_op jit(solution)/shard_map/ppermute | solution.py:45
